TPU v7x, 32 devices: a whole 2x2x4 slice. The times are simulated.
32 devices in a mesh: groups: 2 (over x), win: 4 (over z), lat: 4 (over y, core).
Axes of the slice: x: 2, y: 2, z: 4, core: 2. Of those that a mesh axis runs over, the one named last changes fastest.
Arguments:
- thickness: float32 [8, 2, 3, 8, 64, 256], P(('groups', 'win'), None, None, None, 'lat'), parts along dimension 0, may hold values from 0.5 to 1.5
- obs_cells: int32 [8, 2, 1024], P(('groups', 'win'), None, 'lat'), parts along dimension 0, may hold values from 0 to 4095
- obs_values: float32 [8, 2, 1024], P(('groups', 'win'), None, 'lat'), parts along dimension 0, may hold values from -6 to 6
- ocean_mask: int32 [128, 256], P(('groups', 'lat')), parts along dimension 0, may hold values 0 or 1
- coupling: float32 [8, 8], replicated, may hold values from -1.2 to 1.2
- damping: float32 [8], replicated, may hold values from 0.05 to 0.8
Outputs:
- window_adjoint: float32 [8, 3, 8, 64, 256], P(('groups', 'win'), None, None, 'lat'), parts along dimension 0
- bias_gradient: float32 [16, 64, 256], P('groups', 'lat'), parts along dimension 0
There are 2 independent parts, one for each index of `groups`. A program takes and returns all parts, laid end to end along the dimension named above; an argument that names none is the same for every part. Nothing has to cross between parts.
Inputs may be any that keep to these rules, and one draw needn't show every extreme that they name: `obs_cells`: entry k of a step's list names a cell of the latitude block that starts at row (k // 256) * 16, as row * 256 + column within that block; a cell may be named several times.
All inputs are finite; a program needn't handle non-finite values. No bound on the sum of `ocean_mask` on one device may be relied on, other than what follows from the above.
Results may differ from a plain program's by a relative error of at most 0.00011.
Values sent between devices are 32-bit elements; how exact they have to be, the bound alone decides.
No kernel may reach another device: no remote copies, remote signals or barrier semaphores. Data moves between devices by JAX's collectives and lax.ppermute only.
A program may use at most 64 MiB of HBM per device.

v0:
```python
import jax
import jax.numpy as jnp
from jax import lax
from jax.sharding import PartitionSpec as P

STEP_DT = 0.2
THIRD = 1.0 / 3.0
TWO_THIRDS = 2.0 / 3.0


def with_halo(value, sides, width):
    for axis, dim in sides:
        count, length = (lax.axis_size(axis), value.shape[dim])
        up = [(i, (i + 1) % count) for i in range(count - 1)]
        down = [(j, i) for i, j in up]
        last = lax.slice_in_dim(value, length - width, length, axis=dim)
        initial = lax.slice_in_dim(value, 0, width, axis=dim)
        before = lax.ppermute(last, axis, up)
        after = lax.ppermute(initial, axis, down)
        value = jnp.concatenate([before, value, after], axis=dim)
    return value


def passed_along(value, axis, steps):
    count = lax.axis_size(axis)
    initial, last = (max(0, -steps), min(count, count - steps))
    return lax.ppermute(value, axis, [(source, source + steps) for source in range(initial, last)])


def tendency(state, ocean, fcor, edges, mix, rate):
    p_part = state[1]
    q_part = state[2]
    a_part = state[0]
    w_mid = edges[0][:, 1:-1]
    dxp = 0.5 * (jnp.roll(p_part, -1, axis=2) - jnp.roll(p_part, 1, axis=2))
    dyq = 0.5 * (edges[1][:, 2:] - edges[1][:, :-2])
    mixed = jnp.einsum("kl,krc->lrc", mix, dxp + dyq, precision=lax.Precision.HIGHEST)
    t_a = ocean * (mixed - rate * a_part)
    t_p = ocean * (
        0.5 * (jnp.roll(w_mid, -1, axis=2) - jnp.roll(w_mid, 1, axis=2))
        + fcor * q_part
        - rate * p_part
    )
    t_q = ocean * (0.5 * (edges[0][:, 2:] - edges[0][:, :-2]) - fcor * p_part - rate * q_part)
    return jnp.stack([t_a, t_p, t_q])


def runge_kutta(state, section_tend):
    first = state + STEP_DT * section_tend(state, 0)
    second = 0.75 * state + 0.25 * (first + STEP_DT * section_tend(first, 1))
    return THIRD * state + TWO_THIRDS * (second + STEP_DT * section_tend(second, 2))


def add_obs(state, cells, values):
    layer_a = state[0]
    flat = layer_a.reshape(layer_a.shape[0], -1).at[:, cells].add(values[None, :])
    return state.at[0].set(flat.reshape(layer_a.shape))


def per_device(thickness, obs_cells, obs_values, ocean_mask, coupling, damping):
    rows = ocean_mask.shape[0]
    total_rows = rows * lax.axis_size("lat")
    first_row = lax.axis_index("lat") * rows
    mix = jnp.eye(coupling.shape[0], dtype=jnp.float32) + coupling
    rate = damping[:, None, None]
    steps = thickness.shape[1]
    ocean = ocean_mask.astype(jnp.float32)
    global_rows = first_row + jnp.arange(rows, dtype=jnp.int32)
    fcor = (0.3 + 0.4 * (global_rows.astype(jnp.float32) / total_rows - 0.5))[:, None]

    def adjoint_step(state, thick):

        def section_tend(current, section):
            pair = jnp.stack([thick[section] * current[0], current[2]])
            edges = with_halo(pair, (("lat", 2),), 1)
            return tendency(current, ocean, fcor, edges, mix, rate)

        return runge_kutta(state, section_tend)

    def integrate(state):
        bias = jnp.zeros(state.shape[1:], jnp.float32)
        for step in reversed(range(steps)):
            state = add_obs(state, obs_cells[0, step], obs_values[0, step])
            state = adjoint_step(state, thickness[0, step])
            bias = bias + STEP_DT * state[0]
        return (state, bias)

    zero_state = jnp.zeros((3,) + thickness.shape[3:], jnp.float32)
    rounds = lax.axis_size("win") - 1

    def relay_round(index, carry):
        start_state, unused = integrate(carry)
        return passed_along(start_state, "win", -1)

    incoming = lax.fori_loop(0, rounds, relay_round, zero_state)
    lam, bias = integrate(incoming)
    total_bias = lax.psum(bias, "win")
    return (lam[None], total_bias)


def solution(mesh):
    in_specs = (
        P(("groups", "win"), None, None, None, "lat", None),
        P(("groups", "win"), None, "lat"),
        P(("groups", "win"), None, "lat"),
        P(("groups", "lat"), None),
        P(),
        P(),
    )
    out_specs = (P(("groups", "win"), None, None, "lat", None), P("groups", "lat", None))
    return jax.shard_map(
        per_device, mesh=mesh, in_specs=in_specs, out_specs=out_specs, check_vma=False
    )
```

profile of v0, /device:TPU:1, one launch (start us, length us, event | category | flops | bytes accessed | tf_op | source)
XLA Modules:
  0.0 353.5 jit_solution(15236490072825664713)
XLA Ops:
  13.6 232.9 %while.17 = (s32[]{:T(128)}, f32[3,8,16,256]{3,1,2,0:T(8,128)S(1)}, s32[1,2,256]{2,1,0:T(2,128)}, f32[1,2,256]{2,1,0:T(2,128)}, f32[16,256]{1,0:T(8,128)S(1)}, /...) while((s32[]{:T(128)}, f32[3,8,16,256]{3,1,2,0:T(8,128)S(1)}, ...), condition=%wide.region_3.4_spmd.clone, body=%wide.region_0.3_spmd.clone.sunk | while | flops 31856224 | bytes 54825772 | solution.py:95
  22.9 4.5 %collective-permute-start.1 = (f32[2,8,1,256]{3,1,2,0:T(8,128)}, f32[2,8,1,256]{3,1,2,0:T(8,128)}, u32[]{:S(2)}, u32[]{:S(2)}) collective-permute-start(f32[2,8,1,256]{3,1,2,0:T(8,128)} %get-tuple-element.585), channel_id=1, source_target_pairs={{0,1},{1,2},{2,3},{4,5},{5,6},{6,7},{8,9},{9,10},{10,11},{12,13},{... | collective-permute-start | bytes 49160 | tf_op jit(solution)/shard_map/while/body/eval_jaxpr/ppermute | solution.py:18
  33.6 3.6 %collective-permute-start.3 = (f32[2,8,1,256]{3,1,2,0:T(8,128)S(1)}, f32[2,8,1,256]{3,1,2,0:T(8,128)S(1)}, u32[]{:S(2)}, u32[]{:S(2)}) collective-permute-start(f32[2,8,1,256]{3,1,2,0:T(8,128)S(1)} %get-tuple-element.601), channel_id=1, source_target_pairs={{0,1},{1,2},{2,3},{4,5},{5,6},{6,7},{8,9},{9,10},{10,11},{12,13},{... | collective-permute-start | bytes 49160 | tf_op jit(solution)/shard_map/while/body/eval_jaxpr/ppermute | solution.py:18
  41.7 4.2 %collective-permute-start.5 = (f32[2,8,1,256]{3,1,2,0:T(8,128)S(1)}, f32[2,8,1,256]{3,1,2,0:T(8,128)S(1)}, u32[]{:S(2)}, u32[]{:S(2)}) collective-permute-start(f32[2,8,1,256]{3,1,2,0:T(8,128)S(1)} %get-tuple-element.617), channel_id=1, source_target_pairs={{0,1},{1,2},{2,3},{4,5},{5,6},{6,7},{8,9},{9,10},{10,11},{12,13},{... | collective-permute-start | bytes 49160 | tf_op jit(solution)/shard_map/while/body/eval_jaxpr/ppermute | solution.py:18
  55.6 4.2 %collective-permute-start.7 = (f32[2,8,1,256]{3,1,2,0:T(8,128)S(1)}, f32[2,8,1,256]{3,1,2,0:T(8,128)S(1)}, u32[]{:S(2)}, u32[]{:S(2)}) collective-permute-start(f32[2,8,1,256]{3,1,2,0:T(8,128)S(1)} %get-tuple-element.635), channel_id=1, source_target_pairs={{0,1},{1,2},{2,3},{4,5},{5,6},{6,7},{8,9},{9,10},{10,11},{12,13},{... | collective-permute-start | bytes 49160 | tf_op jit(solution)/shard_map/while/body/eval_jaxpr/ppermute | solution.py:18
  64.5 4.2 %collective-permute-start.9 = (f32[2,8,1,256]{3,1,2,0:T(8,128)S(1)}, f32[2,8,1,256]{3,1,2,0:T(8,128)S(1)}, u32[]{:S(2)}, u32[]{:S(2)}) collective-permute-start(f32[2,8,1,256]{3,1,2,0:T(8,128)S(1)} %get-tuple-element.651), channel_id=1, source_target_pairs={{0,1},{1,2},{2,3},{4,5},{5,6},{6,7},{8,9},{9,10},{10,11},{12,13},{... | collective-permute-start | bytes 49160 | tf_op jit(solution)/shard_map/while/body/eval_jaxpr/ppermute | solution.py:18
  73.3 4.2 %collective-permute-start.11 = (f32[2,8,1,256]{3,1,2,0:T(8,128)S(1)}, f32[2,8,1,256]{3,1,2,0:T(8,128)S(1)}, u32[]{:S(2)}, u32[]{:S(2)}) collective-permute-start(f32[2,8,1,256]{3,1,2,0:T(8,128)S(1)} %get-tuple-element.667), channel_id=1, source_target_pairs={{0,1},{1,2},{2,3},{4,5},{5,6},{6,7},{8,9},{9,10},{10,11},{12,13},{... | collective-permute-start | bytes 49160 | tf_op jit(solution)/shard_map/while/body/eval_jaxpr/ppermute | solution.py:18
  81.4 10.1 %collective-permute-done.12 = f32[3,8,16,256]{3,1,2,0:T(8,128)S(1)} collective-permute-done((f32[3,8,16,256]{3,1,2,0:T(8,128)S(1)}, f32[3,8,16,256]{3,1,2,0:T(8,128)S(1)}, u32[]{:S(2)}, u32[]{:S(2)}) %collective-permute-start.12) | collective-permute-done | bytes 393248 | tf_op jit(solution)/shard_map/while/body/eval_jaxpr/ppermute | solution.py:27
  100.6 4.3 %collective-permute-start.1 = (f32[2,8,1,256]{3,1,2,0:T(8,128)}, f32[2,8,1,256]{3,1,2,0:T(8,128)}, u32[]{:S(2)}, u32[]{:S(2)}) collective-permute-start(f32[2,8,1,256]{3,1,2,0:T(8,128)} %get-tuple-element.585), channel_id=1, source_target_pairs={{0,1},{1,2},{2,3},{4,5},{5,6},{6,7},{8,9},{9,10},{10,11},{12,13},{... | collective-permute-start | bytes 49160 | tf_op jit(solution)/shard_map/while/body/eval_jaxpr/ppermute | solution.py:18
  111.1 3.6 %collective-permute-start.3 = (f32[2,8,1,256]{3,1,2,0:T(8,128)S(1)}, f32[2,8,1,256]{3,1,2,0:T(8,128)S(1)}, u32[]{:S(2)}, u32[]{:S(2)}) collective-permute-start(f32[2,8,1,256]{3,1,2,0:T(8,128)S(1)} %get-tuple-element.601), channel_id=1, source_target_pairs={{0,1},{1,2},{2,3},{4,5},{5,6},{6,7},{8,9},{9,10},{10,11},{12,13},{... | collective-permute-start | bytes 49160 | tf_op jit(solution)/shard_map/while/body/eval_jaxpr/ppermute | solution.py:18
  119.3 4.2 %collective-permute-start.5 = (f32[2,8,1,256]{3,1,2,0:T(8,128)S(1)}, f32[2,8,1,256]{3,1,2,0:T(8,128)S(1)}, u32[]{:S(2)}, u32[]{:S(2)}) collective-permute-start(f32[2,8,1,256]{3,1,2,0:T(8,128)S(1)} %get-tuple-element.617), channel_id=1, source_target_pairs={{0,1},{1,2},{2,3},{4,5},{5,6},{6,7},{8,9},{9,10},{10,11},{12,13},{... | collective-permute-start | bytes 49160 | tf_op jit(solution)/shard_map/while/body/eval_jaxpr/ppermute | solution.py:18
  133.1 4.2 %collective-permute-start.7 = (f32[2,8,1,256]{3,1,2,0:T(8,128)S(1)}, f32[2,8,1,256]{3,1,2,0:T(8,128)S(1)}, u32[]{:S(2)}, u32[]{:S(2)}) collective-permute-start(f32[2,8,1,256]{3,1,2,0:T(8,128)S(1)} %get-tuple-element.635), channel_id=1, source_target_pairs={{0,1},{1,2},{2,3},{4,5},{5,6},{6,7},{8,9},{9,10},{10,11},{12,13},{... | collective-permute-start | bytes 49160 | tf_op jit(solution)/shard_map/while/body/eval_jaxpr/ppermute | solution.py:18
  142.1 4.2 %collective-permute-start.9 = (f32[2,8,1,256]{3,1,2,0:T(8,128)S(1)}, f32[2,8,1,256]{3,1,2,0:T(8,128)S(1)}, u32[]{:S(2)}, u32[]{:S(2)}) collective-permute-start(f32[2,8,1,256]{3,1,2,0:T(8,128)S(1)} %get-tuple-element.651), channel_id=1, source_target_pairs={{0,1},{1,2},{2,3},{4,5},{5,6},{6,7},{8,9},{9,10},{10,11},{12,13},{... | collective-permute-start | bytes 49160 | tf_op jit(solution)/shard_map/while/body/eval_jaxpr/ppermute | solution.py:18
  150.8 4.2 %collective-permute-start.11 = (f32[2,8,1,256]{3,1,2,0:T(8,128)S(1)}, f32[2,8,1,256]{3,1,2,0:T(8,128)S(1)}, u32[]{:S(2)}, u32[]{:S(2)}) collective-permute-start(f32[2,8,1,256]{3,1,2,0:T(8,128)S(1)} %get-tuple-element.667), channel_id=1, source_target_pairs={{0,1},{1,2},{2,3},{4,5},{5,6},{6,7},{8,9},{9,10},{10,11},{12,13},{... | collective-permute-start | bytes 49160 | tf_op jit(solution)/shard_map/while/body/eval_jaxpr/ppermute | solution.py:18
  158.9 10.1 %collective-permute-done.12 = f32[3,8,16,256]{3,1,2,0:T(8,128)S(1)} collective-permute-done((f32[3,8,16,256]{3,1,2,0:T(8,128)S(1)}, f32[3,8,16,256]{3,1,2,0:T(8,128)S(1)}, u32[]{:S(2)}, u32[]{:S(2)}) %collective-permute-start.12) | collective-permute-done | bytes 393248 | tf_op jit(solution)/shard_map/while/body/eval_jaxpr/ppermute | solution.py:27
  178.2 4.3 %collective-permute-start.1 = (f32[2,8,1,256]{3,1,2,0:T(8,128)}, f32[2,8,1,256]{3,1,2,0:T(8,128)}, u32[]{:S(2)}, u32[]{:S(2)}) collective-permute-start(f32[2,8,1,256]{3,1,2,0:T(8,128)} %get-tuple-element.585), channel_id=1, source_target_pairs={{0,1},{1,2},{2,3},{4,5},{5,6},{6,7},{8,9},{9,10},{10,11},{12,13},{... | collective-permute-start | bytes 49160 | tf_op jit(solution)/shard_map/while/body/eval_jaxpr/ppermute | solution.py:18
  188.6 3.6 %collective-permute-start.3 = (f32[2,8,1,256]{3,1,2,0:T(8,128)S(1)}, f32[2,8,1,256]{3,1,2,0:T(8,128)S(1)}, u32[]{:S(2)}, u32[]{:S(2)}) collective-permute-start(f32[2,8,1,256]{3,1,2,0:T(8,128)S(1)} %get-tuple-element.601), channel_id=1, source_target_pairs={{0,1},{1,2},{2,3},{4,5},{5,6},{6,7},{8,9},{9,10},{10,11},{12,13},{... | collective-permute-start | bytes 49160 | tf_op jit(solution)/shard_map/while/body/eval_jaxpr/ppermute | solution.py:18
  196.8 4.2 %collective-permute-start.5 = (f32[2,8,1,256]{3,1,2,0:T(8,128)S(1)}, f32[2,8,1,256]{3,1,2,0:T(8,128)S(1)}, u32[]{:S(2)}, u32[]{:S(2)}) collective-permute-start(f32[2,8,1,256]{3,1,2,0:T(8,128)S(1)} %get-tuple-element.617), channel_id=1, source_target_pairs={{0,1},{1,2},{2,3},{4,5},{5,6},{6,7},{8,9},{9,10},{10,11},{12,13},{... | collective-permute-start | bytes 49160 | tf_op jit(solution)/shard_map/while/body/eval_jaxpr/ppermute | solution.py:18
  210.6 4.2 %collective-permute-start.7 = (f32[2,8,1,256]{3,1,2,0:T(8,128)S(1)}, f32[2,8,1,256]{3,1,2,0:T(8,128)S(1)}, u32[]{:S(2)}, u32[]{:S(2)}) collective-permute-start(f32[2,8,1,256]{3,1,2,0:T(8,128)S(1)} %get-tuple-element.635), channel_id=1, source_target_pairs={{0,1},{1,2},{2,3},{4,5},{5,6},{6,7},{8,9},{9,10},{10,11},{12,13},{... | collective-permute-start | bytes 49160 | tf_op jit(solution)/shard_map/while/body/eval_jaxpr/ppermute | solution.py:18
  219.6 4.2 %collective-permute-start.9 = (f32[2,8,1,256]{3,1,2,0:T(8,128)S(1)}, f32[2,8,1,256]{3,1,2,0:T(8,128)S(1)}, u32[]{:S(2)}, u32[]{:S(2)}) collective-permute-start(f32[2,8,1,256]{3,1,2,0:T(8,128)S(1)} %get-tuple-element.651), channel_id=1, source_target_pairs={{0,1},{1,2},{2,3},{4,5},{5,6},{6,7},{8,9},{9,10},{10,11},{12,13},{... | collective-permute-start | bytes 49160 | tf_op jit(solution)/shard_map/while/body/eval_jaxpr/ppermute | solution.py:18
  228.3 4.2 %collective-permute-start.11 = (f32[2,8,1,256]{3,1,2,0:T(8,128)S(1)}, f32[2,8,1,256]{3,1,2,0:T(8,128)S(1)}, u32[]{:S(2)}, u32[]{:S(2)}) collective-permute-start(f32[2,8,1,256]{3,1,2,0:T(8,128)S(1)} %get-tuple-element.667), channel_id=1, source_target_pairs={{0,1},{1,2},{2,3},{4,5},{5,6},{6,7},{8,9},{9,10},{10,11},{12,13},{... | collective-permute-start | bytes 49160 | tf_op jit(solution)/shard_map/while/body/eval_jaxpr/ppermute | solution.py:18
  236.4 10.1 %collective-permute-done.12 = f32[3,8,16,256]{3,1,2,0:T(8,128)S(1)} collective-permute-done((f32[3,8,16,256]{3,1,2,0:T(8,128)S(1)}, f32[3,8,16,256]{3,1,2,0:T(8,128)S(1)}, u32[]{:S(2)}, u32[]{:S(2)}) %collective-permute-start.12) | collective-permute-done | bytes 393248 | tf_op jit(solution)/shard_map/while/body/eval_jaxpr/ppermute | solution.py:27
  250.9 4.3 %collective-permute-start.13 = (f32[2,8,1,256]{3,1,2,0:T(8,128)S(1)}, f32[2,8,1,256]{3,1,2,0:T(8,128)S(1)}, u32[]{:S(2)}, u32[]{:S(2)}) collective-permute-start(f32[2,8,1,256]{3,1,2,0:T(8,128)S(1)} %get-tuple-element.367), channel_id=1, source_target_pairs={{0,1},{1,2},{2,3},{4,5},{5,6},{6,7},{8,9},{9,10},{10,11},{12,13},{... | collective-permute-start | bytes 49160 | tf_op jit(solution)/shard_map/ppermute | solution.py:18
  314.9 30.2 %all-reduce.2.cloned.1.call-done = f32[8,16,256]{2,0,1:T(8,128)} async-done(((f32[8,16,256]{2,0,1:T(8,128)}), f32[8,16,256]{2,0,1:T(8,128)}) %all-reduce.2.cloned.1.call-update) | async-done | bytes 131088 | tf_op jit(solution)/shard_map/psum | solution.py:97
  (617 shorter events, 197.2 us)
Async XLA Ops:
  7.2 337.9 %all-reduce.2.cloned.1.call-start = ((), (), s32[]{:S(2)}) async-start(), calls=%async_computation | async-start | bytes 262144 | tf_op jit(solution)/shard_map/psum | solution.py:97
  20.9 8.2 %collective-permute-start = (f32[2,8,1,256]{3,1,2,0:T(8,128)}, f32[2,8,1,256]{3,1,2,0:T(8,128)}, u32[]{:S(2)}, u32[]{:S(2)}) collective-permute-start(f32[2,8,1,256]{3,1,2,0:T(8,128)} %get-tuple-element.584), channel_id=1, source_target_pairs={{1,0},{2,1},{3,2},{5,4},{6,5},{7,6},{9,8},{10,9},{11,10},{13,12},{... | collective-permute-start | bytes 49160 | tf_op jit(solution)/shard_map/while/body/eval_jaxpr/ppermute | solution.py:19
  22.9 6.3 %collective-permute-start.1 = (f32[2,8,1,256]{3,1,2,0:T(8,128)}, f32[2,8,1,256]{3,1,2,0:T(8,128)}, u32[]{:S(2)}, u32[]{:S(2)}) collective-permute-start(f32[2,8,1,256]{3,1,2,0:T(8,128)} %get-tuple-element.585), channel_id=1, source_target_pairs={{0,1},{1,2},{2,3},{4,5},{5,6},{6,7},{8,9},{9,10},{10,11},{12,13},{... | collective-permute-start | bytes 49160 | tf_op jit(solution)/shard_map/while/body/eval_jaxpr/ppermute | solution.py:18
  39.8 6.1 %collective-permute-start.4 = (f32[2,8,1,256]{3,1,2,0:T(8,128)S(1)}, f32[2,8,1,256]{3,1,2,0:T(8,128)S(1)}, u32[]{:S(2)}, u32[]{:S(2)}) collective-permute-start(f32[2,8,1,256]{3,1,2,0:T(8,128)S(1)} %get-tuple-element.616), channel_id=1, source_target_pairs={{1,0},{2,1},{3,2},{5,4},{6,5},{7,6},{9,8},{10,9},{11,10},{13,12},{... | collective-permute-start | bytes 49160 | tf_op jit(solution)/shard_map/while/body/eval_jaxpr/ppermute | solution.py:19
  53.7 6.7 %collective-permute-start.6 = (f32[2,8,1,256]{3,1,2,0:T(8,128)S(1)}, f32[2,8,1,256]{3,1,2,0:T(8,128)S(1)}, u32[]{:S(2)}, u32[]{:S(2)}) collective-permute-start(f32[2,8,1,256]{3,1,2,0:T(8,128)S(1)} %get-tuple-element.634), channel_id=1, source_target_pairs={{1,0},{2,1},{3,2},{5,4},{6,5},{7,6},{9,8},{10,9},{11,10},{13,12},{... | collective-permute-start | bytes 49160 | tf_op jit(solution)/shard_map/while/body/eval_jaxpr/ppermute | solution.py:19
  62.6 6.1 %collective-permute-start.8 = (f32[2,8,1,256]{3,1,2,0:T(8,128)S(1)}, f32[2,8,1,256]{3,1,2,0:T(8,128)S(1)}, u32[]{:S(2)}, u32[]{:S(2)}) collective-permute-start(f32[2,8,1,256]{3,1,2,0:T(8,128)S(1)} %get-tuple-element.650), channel_id=1, source_target_pairs={{1,0},{2,1},{3,2},{5,4},{6,5},{7,6},{9,8},{10,9},{11,10},{13,12},{... | collective-permute-start | bytes 49160 | tf_op jit(solution)/shard_map/while/body/eval_jaxpr/ppermute | solution.py:19
  71.3 6.1 %collective-permute-start.10 = (f32[2,8,1,256]{3,1,2,0:T(8,128)S(1)}, f32[2,8,1,256]{3,1,2,0:T(8,128)S(1)}, u32[]{:S(2)}, u32[]{:S(2)}) collective-permute-start(f32[2,8,1,256]{3,1,2,0:T(8,128)S(1)} %get-tuple-element.666), channel_id=1, source_target_pairs={{1,0},{2,1},{3,2},{5,4},{6,5},{7,6},{9,8},{10,9},{11,10},{13,12},{... | collective-permute-start | bytes 49160 | tf_op jit(solution)/shard_map/while/body/eval_jaxpr/ppermute | solution.py:19
  80.1 11.4 %collective-permute-start.12 = (f32[3,8,16,256]{3,1,2,0:T(8,128)S(1)}, f32[3,8,16,256]{3,1,2,0:T(8,128)S(1)}, u32[]{:S(2)}, u32[]{:S(2)}) collective-permute-start(f32[3,8,16,256]{3,1,2,0:T(8,128)S(1)} %fusion.480), channel_id=1, source_target_pairs={{4,0},{8,4},{12,8},{5,1},{9,5},{13,9},{6,2},{10,6},{14,10},{7,3},{... | collective-permute-start | bytes 1179656 | tf_op jit(solution)/shard_map/while/body/eval_jaxpr/ppermute | solution.py:27
  98.7 7.9 %collective-permute-start = (f32[2,8,1,256]{3,1,2,0:T(8,128)}, f32[2,8,1,256]{3,1,2,0:T(8,128)}, u32[]{:S(2)}, u32[]{:S(2)}) collective-permute-start(f32[2,8,1,256]{3,1,2,0:T(8,128)} %get-tuple-element.584), channel_id=1, source_target_pairs={{1,0},{2,1},{3,2},{5,4},{6,5},{7,6},{9,8},{10,9},{11,10},{13,12},{... | collective-permute-start | bytes 49160 | tf_op jit(solution)/shard_map/while/body/eval_jaxpr/ppermute | solution.py:19
  100.6 6.0 %collective-permute-start.1 = (f32[2,8,1,256]{3,1,2,0:T(8,128)}, f32[2,8,1,256]{3,1,2,0:T(8,128)}, u32[]{:S(2)}, u32[]{:S(2)}) collective-permute-start(f32[2,8,1,256]{3,1,2,0:T(8,128)} %get-tuple-element.585), channel_id=1, source_target_pairs={{0,1},{1,2},{2,3},{4,5},{5,6},{6,7},{8,9},{9,10},{10,11},{12,13},{... | collective-permute-start | bytes 49160 | tf_op jit(solution)/shard_map/while/body/eval_jaxpr/ppermute | solution.py:18
  109.2 5.6 %collective-permute-start.2 = (f32[2,8,1,256]{3,1,2,0:T(8,128)S(1)}, f32[2,8,1,256]{3,1,2,0:T(8,128)S(1)}, u32[]{:S(2)}, u32[]{:S(2)}) collective-permute-start(f32[2,8,1,256]{3,1,2,0:T(8,128)S(1)} %get-tuple-element.600), channel_id=1, source_target_pairs={{1,0},{2,1},{3,2},{5,4},{6,5},{7,6},{9,8},{10,9},{11,10},{13,12},{... | collective-permute-start | bytes 49160 | tf_op jit(solution)/shard_map/while/body/eval_jaxpr/ppermute | solution.py:19
  117.3 6.1 %collective-permute-start.4 = (f32[2,8,1,256]{3,1,2,0:T(8,128)S(1)}, f32[2,8,1,256]{3,1,2,0:T(8,128)S(1)}, u32[]{:S(2)}, u32[]{:S(2)}) collective-permute-start(f32[2,8,1,256]{3,1,2,0:T(8,128)S(1)} %get-tuple-element.616), channel_id=1, source_target_pairs={{1,0},{2,1},{3,2},{5,4},{6,5},{7,6},{9,8},{10,9},{11,10},{13,12},{... | collective-permute-start | bytes 49160 | tf_op jit(solution)/shard_map/while/body/eval_jaxpr/ppermute | solution.py:19
  131.2 6.7 %collective-permute-start.6 = (f32[2,8,1,256]{3,1,2,0:T(8,128)S(1)}, f32[2,8,1,256]{3,1,2,0:T(8,128)S(1)}, u32[]{:S(2)}, u32[]{:S(2)}) collective-permute-start(f32[2,8,1,256]{3,1,2,0:T(8,128)S(1)} %get-tuple-element.634), channel_id=1, source_target_pairs={{1,0},{2,1},{3,2},{5,4},{6,5},{7,6},{9,8},{10,9},{11,10},{13,12},{... | collective-permute-start | bytes 49160 | tf_op jit(solution)/shard_map/while/body/eval_jaxpr/ppermute | solution.py:19
  140.1 6.1 %collective-permute-start.8 = (f32[2,8,1,256]{3,1,2,0:T(8,128)S(1)}, f32[2,8,1,256]{3,1,2,0:T(8,128)S(1)}, u32[]{:S(2)}, u32[]{:S(2)}) collective-permute-start(f32[2,8,1,256]{3,1,2,0:T(8,128)S(1)} %get-tuple-element.650), channel_id=1, source_target_pairs={{1,0},{2,1},{3,2},{5,4},{6,5},{7,6},{9,8},{10,9},{11,10},{13,12},{... | collective-permute-start | bytes 49160 | tf_op jit(solution)/shard_map/while/body/eval_jaxpr/ppermute | solution.py:19
  148.8 6.1 %collective-permute-start.10 = (f32[2,8,1,256]{3,1,2,0:T(8,128)S(1)}, f32[2,8,1,256]{3,1,2,0:T(8,128)S(1)}, u32[]{:S(2)}, u32[]{:S(2)}) collective-permute-start(f32[2,8,1,256]{3,1,2,0:T(8,128)S(1)} %get-tuple-element.666), channel_id=1, source_target_pairs={{1,0},{2,1},{3,2},{5,4},{6,5},{7,6},{9,8},{10,9},{11,10},{13,12},{... | collective-permute-start | bytes 49160 | tf_op jit(solution)/shard_map/while/body/eval_jaxpr/ppermute | solution.py:19
  157.6 11.4 %collective-permute-start.12 = (f32[3,8,16,256]{3,1,2,0:T(8,128)S(1)}, f32[3,8,16,256]{3,1,2,0:T(8,128)S(1)}, u32[]{:S(2)}, u32[]{:S(2)}) collective-permute-start(f32[3,8,16,256]{3,1,2,0:T(8,128)S(1)} %fusion.480), channel_id=1, source_target_pairs={{4,0},{8,4},{12,8},{5,1},{9,5},{13,9},{6,2},{10,6},{14,10},{7,3},{... | collective-permute-start | bytes 1179656 | tf_op jit(solution)/shard_map/while/body/eval_jaxpr/ppermute | solution.py:27
  176.2 7.9 %collective-permute-start = (f32[2,8,1,256]{3,1,2,0:T(8,128)}, f32[2,8,1,256]{3,1,2,0:T(8,128)}, u32[]{:S(2)}, u32[]{:S(2)}) collective-permute-start(f32[2,8,1,256]{3,1,2,0:T(8,128)} %get-tuple-element.584), channel_id=1, source_target_pairs={{1,0},{2,1},{3,2},{5,4},{6,5},{7,6},{9,8},{10,9},{11,10},{13,12},{... | collective-permute-start | bytes 49160 | tf_op jit(solution)/shard_map/while/body/eval_jaxpr/ppermute | solution.py:19
  178.2 6.0 %collective-permute-start.1 = (f32[2,8,1,256]{3,1,2,0:T(8,128)}, f32[2,8,1,256]{3,1,2,0:T(8,128)}, u32[]{:S(2)}, u32[]{:S(2)}) collective-permute-start(f32[2,8,1,256]{3,1,2,0:T(8,128)} %get-tuple-element.585), channel_id=1, source_target_pairs={{0,1},{1,2},{2,3},{4,5},{5,6},{6,7},{8,9},{9,10},{10,11},{12,13},{... | collective-permute-start | bytes 49160 | tf_op jit(solution)/shard_map/while/body/eval_jaxpr/ppermute | solution.py:18
  194.8 6.1 %collective-permute-start.4 = (f32[2,8,1,256]{3,1,2,0:T(8,128)S(1)}, f32[2,8,1,256]{3,1,2,0:T(8,128)S(1)}, u32[]{:S(2)}, u32[]{:S(2)}) collective-permute-start(f32[2,8,1,256]{3,1,2,0:T(8,128)S(1)} %get-tuple-element.616), channel_id=1, source_target_pairs={{1,0},{2,1},{3,2},{5,4},{6,5},{7,6},{9,8},{10,9},{11,10},{13,12},{... | collective-permute-start | bytes 49160 | tf_op jit(solution)/shard_map/while/body/eval_jaxpr/ppermute | solution.py:19
  208.7 6.7 %collective-permute-start.6 = (f32[2,8,1,256]{3,1,2,0:T(8,128)S(1)}, f32[2,8,1,256]{3,1,2,0:T(8,128)S(1)}, u32[]{:S(2)}, u32[]{:S(2)}) collective-permute-start(f32[2,8,1,256]{3,1,2,0:T(8,128)S(1)} %get-tuple-element.634), channel_id=1, source_target_pairs={{1,0},{2,1},{3,2},{5,4},{6,5},{7,6},{9,8},{10,9},{11,10},{13,12},{... | collective-permute-start | bytes 49160 | tf_op jit(solution)/shard_map/while/body/eval_jaxpr/ppermute | solution.py:19
  217.6 6.1 %collective-permute-start.8 = (f32[2,8,1,256]{3,1,2,0:T(8,128)S(1)}, f32[2,8,1,256]{3,1,2,0:T(8,128)S(1)}, u32[]{:S(2)}, u32[]{:S(2)}) collective-permute-start(f32[2,8,1,256]{3,1,2,0:T(8,128)S(1)} %get-tuple-element.650), channel_id=1, source_target_pairs={{1,0},{2,1},{3,2},{5,4},{6,5},{7,6},{9,8},{10,9},{11,10},{13,12},{... | collective-permute-start | bytes 49160 | tf_op jit(solution)/shard_map/while/body/eval_jaxpr/ppermute | solution.py:19
  226.4 6.1 %collective-permute-start.10 = (f32[2,8,1,256]{3,1,2,0:T(8,128)S(1)}, f32[2,8,1,256]{3,1,2,0:T(8,128)S(1)}, u32[]{:S(2)}, u32[]{:S(2)}) collective-permute-start(f32[2,8,1,256]{3,1,2,0:T(8,128)S(1)} %get-tuple-element.666), channel_id=1, source_target_pairs={{1,0},{2,1},{3,2},{5,4},{6,5},{7,6},{9,8},{10,9},{11,10},{13,12},{... | collective-permute-start | bytes 49160 | tf_op jit(solution)/shard_map/while/body/eval_jaxpr/ppermute | solution.py:19
  235.1 11.4 %collective-permute-start.12 = (f32[3,8,16,256]{3,1,2,0:T(8,128)S(1)}, f32[3,8,16,256]{3,1,2,0:T(8,128)S(1)}, u32[]{:S(2)}, u32[]{:S(2)}) collective-permute-start(f32[3,8,16,256]{3,1,2,0:T(8,128)S(1)} %fusion.480), channel_id=1, source_target_pairs={{4,0},{8,4},{12,8},{5,1},{9,5},{13,9},{6,2},{10,6},{14,10},{7,3},{... | collective-permute-start | bytes 1179656 | tf_op jit(solution)/shard_map/while/body/eval_jaxpr/ppermute | solution.py:27
  250.9 7.5 %collective-permute-start.13 = (f32[2,8,1,256]{3,1,2,0:T(8,128)S(1)}, f32[2,8,1,256]{3,1,2,0:T(8,128)S(1)}, u32[]{:S(2)}, u32[]{:S(2)}) collective-permute-start(f32[2,8,1,256]{3,1,2,0:T(8,128)S(1)} %get-tuple-element.367), channel_id=1, source_target_pairs={{0,1},{1,2},{2,3},{4,5},{5,6},{6,7},{8,9},{9,10},{10,11},{12,13},{... | collective-permute-start | bytes 49160 | tf_op jit(solution)/shard_map/ppermute | solution.py:18
  (69 other events, 295.0 us)
Sparse Core Ops, SparseCore 0:
  314.0 31.0 all-reduce.1
where the time goes:
time: 359 us; the launch traced here: 354 us
  starting transfers between devices  141 us (39%)
  waiting for transfers between devices  85.2 us (24%)
  local copies, waits for them, and re-layouts  51.5 us (14%)
  other arithmetic  50.6 us (14%)
  between operations  14.9 us (4%)
  matrix products  8.32 us (2%)
    ppermute x24, starting transfers between devices, with_halo(): before = lax.ppermute(last, axis, up)  88.3 us
    ppermute x24, starting transfers between devices, with_halo(): after = lax.ppermute(initial, axis, down)  48.5 us
    ppermute x3, waiting for transfers between devices, passed_along(): lax.ppermute(value, axis, [(source, source + steps) for source in range(i...  30.2 us
    psum x1, waiting for transfers between devices, per_device(): total_bias = lax.psum(bias, 'win')  30.2 us
    scatter-add x8, other arithmetic, add_obs(): layer_a.reshape(layer_a.shape[0], -1).at[:, cells].add(values[None, :])  23.2 us
    ppermute x24, waiting for transfers between devices, with_halo(): after = lax.ppermute(initial, axis, down)  13.9 us
    ppermute x24, waiting for transfers between devices, with_halo(): before = lax.ppermute(last, axis, up)  10.8 us
    dot_general x24, matrix products, tendency(): jnp.einsum('kl,krc->lrc', mix, dxp + dyq, precision=lax.Precision.HIGHEST)  8.32 us
  transfers between devices with their start and end apart: 52, of which 25 were waited for; matrix products, arithmetic and copies ran while one was open for 3% of the time, Pallas kernels for 0%

commit v1 on v0

v1 whole, which is shorter than its diff:
```python
import functools

import jax
import jax.numpy as jnp
from jax import lax
from jax.experimental import pallas as pl
from jax.experimental.pallas import tpu as pltpu
from jax.sharding import PartitionSpec as P

STEP_DT = 0.2
THIRD = 1.0 / 3.0
TWO_THIRDS = 2.0 / 3.0
STAGES = 3
UNROLL = 8
SUBLANES = 8

VMEM = pl.BlockSpec(memory_space=pltpu.VMEM)
SMEM = pl.BlockSpec(memory_space=pltpu.SMEM)


class Sizes:
    def __init__(self, steps, layers, rows, cols):
        self.steps, self.layers, self.rows, self.cols = steps, layers, rows, cols
        self.halo = STAGES * steps
        self.ext = rows + 2 * self.halo
        self.first = [sum(self.halo - m for m in range(j)) for j in range(self.halo)]
        self.halo_rows = sum(self.halo - m for m in range(self.halo))
        self.tail = -(-(steps + 1) * self.halo // SUBLANES)
        self.packed = self.halo_rows + self.tail

    def section(self, j):
        step, stage = self.steps - 1 - j // STAGES, j % STAGES
        return (step * STAGES + stage) * self.layers * self.rows


def rows_first(z, ref, base):
    lines = []
    for tile in range(z.rows // SUBLANES):
        block = jnp.stack(
            [ref[base + l * z.rows + tile * SUBLANES : base + l * z.rows + (tile + 1) * SUBLANES, :] for l in range(z.layers)]
        )
        block = jnp.swapaxes(block, 0, 1)
        lines.extend(block[m] for m in range(SUBLANES))
    return lines


def layers_first(z, ref, start, lines):
    for tile in range(z.rows // SUBLANES):
        block = jnp.swapaxes(jnp.stack(lines[tile * SUBLANES : (tile + 1) * SUBLANES]), 0, 1)
        for l in range(z.layers):
            low = start + l * z.rows + tile * SUBLANES
            ref[low : low + SUBLANES, :] = block[l]


def pack_kernel(z, th_ref, cells_ref, values_ref, mask_ref, up_ref, down_ref, own_ref):
    count = cells_ref.shape[1]
    row_ids = lax.broadcasted_iota(jnp.int32, (z.rows, count), 0)
    col_ids = lax.broadcasted_iota(jnp.int32, (z.cols, count), 0)
    for order in range(z.steps):
        step = z.steps - 1 - order
        cells = cells_ref[step : step + 1, :]
        values = values_ref[step : step + 1, :]
        by_row = jnp.where(row_ids == cells // z.cols, values, 0.0)
        by_col = jnp.where(col_ids == cells % z.cols, 1.0, 0.0).astype(jnp.bfloat16)
        field = jnp.zeros((z.rows, z.cols), jnp.float32)
        for _ in range(3):
            part = by_row.astype(jnp.bfloat16)
            by_row = by_row - part.astype(jnp.float32)
            field = field + lax.dot_general(
                part, by_col, (((1,), (1,)), ((), ())), preferred_element_type=jnp.float32
            )
        own_ref[order * z.rows : (order + 1) * z.rows, :] = field
    own_ref[z.steps * z.rows :, :] = mask_ref[...].astype(jnp.float32) * (0.5 * STEP_DT)
    for j in range(z.halo):
        lines, need = rows_first(z, th_ref, z.section(j)), z.halo - j
        for m in range(need):
            up_ref[z.first[j] + m] = lines[m]
            down_ref[z.first[j] + m] = lines[z.rows - need + m]
    for k in range(z.steps + 1):
        for m in range(z.halo):
            tile, line = divmod(k * z.halo + m, SUBLANES)
            start = k * z.rows
            up_ref[z.halo_rows + tile, line : line + 1, :] = own_ref[start + m : start + m + 1, :]
            last = start + z.rows - z.halo + m
            down_ref[z.halo_rows + tile, line : line + 1, :] = own_ref[last : last + 1, :]
    for q in range((z.steps + 1) * z.halo, z.tail * SUBLANES):
        tile, line = divmod(q, SUBLANES)
        for ref in (up_ref, down_ref):
            ref[z.halo_rows + tile, line : line + 1, :] = jnp.zeros((1, z.cols), jnp.float32)


def extend_kernel(z, coupling_ref, damping_ref, th_ref, above_ref, below_ref, own_ref, h_ref, obs_ref, oc_ref, keep_ref, mix_ref):
    layer_ids = lax.broadcasted_iota(jnp.int32, (z.layers, z.cols), 0)
    for j in range(z.layers):
        line = jnp.zeros((z.layers, z.cols), jnp.float32)
        for l in range(z.layers):
            k = (l - j) % z.layers
            weight = coupling_ref[k, l] + (1.0 if k == l else 0.0)
            line = jnp.where(layer_ids == l, weight, line)
        mix_ref[j * z.layers : (j + 1) * z.layers, :] = line
    rate = jnp.zeros((z.layers, z.cols), jnp.float32)
    for l in range(z.layers):
        rate = jnp.where(layer_ids == l, 2.0 * damping_ref[l], rate)

    shape = (z.layers, z.cols)

    def line_of(k, e):
        if e < z.halo:
            tile, line = divmod(k * z.halo + e, SUBLANES)
            return above_ref[z.halo_rows + tile, line : line + 1, :]
        if e >= z.halo + z.rows:
            tile, line = divmod(k * z.halo + e - z.halo - z.rows, SUBLANES)
            return below_ref[z.halo_rows + tile, line : line + 1, :]
        return own_ref[k * z.rows + e - z.halo : k * z.rows + e - z.halo + 1, :]

    for e in range(z.ext):
        for k in range(z.steps):
            obs_ref[k * z.ext + e] = jnp.broadcast_to(line_of(k, e), shape)
        oc = jnp.broadcast_to(line_of(z.steps, e), shape)
        oc_ref[e] = oc
        keep_ref[e] = 1.0 - oc * rate
    for j in range(z.halo):
        need = z.halo - j
        for m in range(need):
            h_ref[j * z.ext + j + m] = above_ref[z.first[j] + m]
            h_ref[j * z.ext + z.halo + z.rows + m] = below_ref[z.first[j] + m]
        for r, line in enumerate(rows_first(z, th_ref, z.section(j))):
            h_ref[j * z.ext + z.halo + r] = line


def over_rows(low, high, carry, body):
    turns = (high - low) // UNROLL

    def turn(t, carry):
        for u in range(UNROLL):
            carry = body(low + t * UNROLL + u, carry)
        return carry

    if turns > 1:
        carry = lax.fori_loop(0, turns, turn, carry)
        low = low + turns * UNROLL
    for row in range(low, high):
        carry = body(row, carry)
    return carry


def window_kernel(z, total_rows, first, *refs):
    if first:
        h_ref, obs_ref, oc_ref, keep_ref, mix_ref = refs[:5]
        refs = refs[5:]
    else:
        h_ref, obs_ref, oc_ref, keep_ref, mix_ref, main_in, above_in, below_in = refs[:8]
        refs = refs[8:]
    bias_ref, main_ref, top_ref, bottom_ref, x_ref, y_ref, w_ref, sum_ref = refs
    halo, ext, rows, layers = z.halo, z.ext, z.rows, z.layers
    first_row = lax.axis_index("lat") * rows - halo

    for e in range(ext):
        if first:
            zero = jnp.zeros((layers, z.cols), jnp.float32)
            a, p, q = zero, zero, zero
        elif e < halo:
            a, p, q = (above_in[c * halo + e] for c in range(3))
        elif e < halo + rows:
            a, p, q = (main_in[c * rows + e - halo] for c in range(3))
        else:
            a, p, q = (below_in[c * halo + e - halo - rows] for c in range(3))
        x_ref[e] = a + obs_ref[e]
        x_ref[ext + e] = p
        x_ref[2 * ext + e] = q

    mixers = [mix_ref[j * layers : (j + 1) * layers, :] for j in range(layers)]

    def run(j):
        order, stage = divmod(j, STAGES)
        source = (x_ref, y_ref, w_ref)[stage]
        target = (y_ref, w_ref, x_ref)[stage]
        low, high = j + 1, ext - j - 1

        def weighted(e, value):
            return h_ref[j * ext + e] * value

        def body(e, carry, place=None):
            b_before, b_here, a_here, q_before, q_here = carry
            a_after, q_after = source[e + 1], source[2 * ext + e + 1]
            b_after = weighted(e + 1, a_after)
            p_here = source[ext + e]
            oc, keep = oc_ref[e], keep_ref[e]
            coriolis = 2.0 * (0.3 + 0.4 * ((first_row + e).astype(jnp.float32) * (1.0 / total_rows) - 0.5))
            divergence = (
                pltpu.roll(p_here, z.cols - 1, axis=1) - pltpu.roll(p_here, 1, axis=1) + (q_after - q_before)
            )
            mixed = mixers[0] * divergence
            for k in range(1, layers):
                mixed = mixed + mixers[k] * pltpu.roll(divergence, k, axis=0)
            east = pltpu.roll(b_here, z.cols - 1, axis=1) - pltpu.roll(b_here, 1, axis=1)
            a = keep * a_here + oc * mixed
            p = keep * p_here + oc * (east + coriolis * q_here)
            q = keep * q_here + oc * (b_after - b_before - coriolis * p_here)
            if stage == 1:
                a = 0.75 * x_ref[e] + 0.25 * a
                p = 0.75 * x_ref[ext + e] + 0.25 * p
                q = 0.75 * x_ref[2 * ext + e] + 0.25 * q
            elif stage == 2:
                a = THIRD * x_ref[e] + TWO_THIRDS * a
                p = THIRD * x_ref[ext + e] + TWO_THIRDS * p
                q = THIRD * x_ref[2 * ext + e] + TWO_THIRDS * q
                if place is not None:
                    part = STEP_DT * a
                    if order > 0:
                        part = part + sum_ref[place]
                    if order < z.steps - 1:
                        sum_ref[place] = part
                    else:
                        bias_ref[place] = part
                        for c, value in enumerate((a, p, q)):
                            main_ref[c * rows + place] = value
                if order < z.steps - 1:
                    a = a + obs_ref[(order + 1) * ext + e]
            if not (stage == 2 and order == z.steps - 1):
                target[e] = a
                target[ext + e] = p
                target[2 * ext + e] = q
            return b_here, b_after, a_after, q_here, q_after

        a_first = source[low]
        carry = (
            weighted(low - 1, source[low - 1]),
            weighted(low, a_first),
            a_first,
            source[2 * ext + low - 1],
            source[2 * ext + low],
        )
        if stage < 2:
            over_rows(low, high, carry, body)
        else:
            carry = over_rows(low, halo, carry, body)
            carry = over_rows(0, rows, carry, lambda r, c: body(halo + r, c, place=r))
            over_rows(halo + rows, high, carry, body)

    for j in range(halo):
        run(j)
    for c in range(3):
        for m in range(halo):
            top_ref[c * halo + m] = main_ref[c * rows + m]
            bottom_ref[c * halo + m] = main_ref[c * rows + rows - halo + m]


def turn_kernel(z, count, lines_ref, out_ref):
    for c in range(count):
        layers_first(z, out_ref, c * z.layers * z.rows, [lines_ref[c * z.rows + r] for r in range(z.rows)])


def call(kernel, out_shapes, in_specs, scratch=(), cost=0):
    return pl.pallas_call(
        kernel,
        out_shape=[jax.ShapeDtypeStruct(s, jnp.float32) for s in out_shapes],
        in_specs=in_specs,
        out_specs=[VMEM] * len(out_shapes),
        scratch_shapes=list(scratch),
        compiler_params=pltpu.CompilerParams(vmem_limit_bytes=24 << 20),
        cost_estimate=pl.CostEstimate(flops=cost, bytes_accessed=4 << 20, transcendentals=0),
    )


def per_device(thickness, obs_cells, obs_values, ocean_mask, coupling, damping):
    _, steps, stages, layers, rows, cols = thickness.shape
    z = Sizes(steps, layers, rows, cols)
    n_win, n_lat = lax.axis_size("win"), lax.axis_size("lat")
    win = lax.axis_index("win")
    flat = thickness.reshape(steps * stages * layers * rows, cols)
    cube = (layers, cols)

    to_above, to_below, own = call(
        functools.partial(pack_kernel, z),
        [(z.packed,) + cube, (z.packed,) + cube, ((steps + 1) * rows, cols)],
        [VMEM] * 4,
    )(flat, obs_cells[0], obs_values[0], ocean_mask)
    southward = [(i, i + 1) for i in range(n_lat - 1)]
    northward = [(i + 1, i) for i in range(n_lat - 1)]
    above = lax.ppermute(to_below, "lat", southward)
    below = lax.ppermute(to_above, "lat", northward)
    fields = call(
        functools.partial(extend_kernel, z),
        [
            (z.halo * z.ext,) + cube,
            (steps * z.ext,) + cube,
            (z.ext,) + cube,
            (z.ext,) + cube,
            (layers * layers, cols),
        ],
        [SMEM, SMEM] + [VMEM] * 4,
    )(coupling, damping, flat, above, below, own)

    def relay(value, source_win, shift):
        pairs = [
            (source_win * n_lat + i, (source_win - 1) * n_lat + i + shift)
            for i in range(n_lat)
            if 0 <= i + shift < n_lat
        ]
        return lax.ppermute(value, ("win", "lat"), pairs)

    arrived = ()
    lam = bias = None
    total = None
    for source_win in reversed(range(n_win)):
        outs = call(
            functools.partial(window_kernel, z, n_lat * rows, not arrived),
            [
                (rows,) + cube,
                (3 * rows,) + cube,
                (3 * z.halo,) + cube,
                (3 * z.halo,) + cube,
            ],
            [VMEM] * (5 + len(arrived)),
            [pltpu.VMEM((3 * z.ext,) + cube, jnp.float32)] * 3 + [pltpu.VMEM((rows,) + cube, jnp.float32)],
            cost=40_000_000,
        )(*fields, *arrived)
        bias_here, main, top, bottom = outs
        lam = main if lam is None else jnp.where(win == source_win, main, lam)
        total = bias_here if total is None else total + bias_here
        if source_win:
            arrived = (
                relay(main, source_win, 0),
                relay(bottom, source_win, 1),
                relay(top, source_win, -1),
            )
            total = relay(total, source_win, 0)
    parts = [lax.ppermute(total, "win", [(0, w)]) for w in range(1, n_win)]
    result = jnp.where(win == 0, total, 0.0)
    for part in parts:
        result = result + part
    (lam,) = call(functools.partial(turn_kernel, z, 3), [(3 * layers * rows, cols)], [VMEM])(lam)
    (result,) = call(functools.partial(turn_kernel, z, 1), [(layers * rows, cols)], [VMEM])(result)
    return lam.reshape(1, 3, layers, rows, cols), result.reshape(layers, rows, cols)


def solution(mesh):
    in_specs = (
        P(("groups", "win"), None, None, None, "lat", None),
        P(("groups", "win"), None, "lat"),
        P(("groups", "win"), None, "lat"),
        P(("groups", "lat"), None),
        P(),
        P(),
    )
    out_specs = (P(("groups", "win"), None, None, "lat", None), P("groups", "lat", None))
    return jax.shard_map(
        per_device, mesh=mesh, in_specs=in_specs, out_specs=out_specs, check_vma=False
    )
```

time: 359 us -> 91.8 us (0.26); the launches traced: 354 us -> 90.8 us
  starting transfers between devices: 141 us -> 22.1 us
  other arithmetic: 50.6 us -> 1.76 us
  local copies, waits for them, and re-layouts: 51.5 us -> 4.55 us
  waiting for transfers between devices: 85.2 us -> 45 us
  Pallas kernels: 0 us -> 16.5 us
  between operations: 14.9 us -> 0.91 us
  matrix products: 8.32 us -> 0 us
    ppermute x51 -> x17, starting transfers between devices: 141 us -> 22.1 us  [the longest x12 10.5 us: relay(): return lax.ppermute(value, ('win', 'lat'), pairs)]
    psum x1 -> x0, waiting for transfers between devices: 30.2 us -> none  [per_device(): total_bias = lax.psum(bias, 'win')]
    slice x152 -> x0, local copies, waits for them, and re-layouts: 24.8 us -> none  [the longest x4 5.4 us: integrate(): state = add_obs(state, obs_cells[0, step], obs_values[0, step])]
    scatter-add x8 -> x0, other arithmetic: 23.2 us -> none  [add_obs(): layer_a.reshape(layer_a.shape[0], -1).at[:, cells].add(values[None, :])]
    pallas_call x0 -> x8, Pallas kernels: none -> 16.5 us  [the longest x4 13.8 us: per_device(): call(functools.partial(window_kernel, z, n_lat * rows, not arrived), [(ro...]
    squeeze x35 -> x0, local copies, waits for them, and re-layouts: 10.1 us -> none  [the longest x8 7.82 us: section_tend(): pair = jnp.stack([thick[section] * current[0], current[2]])]
    ppermute x51 -> x17, waiting for transfers between devices: 55 us -> 45 us  [the longest x12 34.6 us: relay(): return lax.ppermute(value, ('win', 'lat'), pairs)]
    concatenate x72 -> x0, local copies, waits for them, and re-layouts: 8.61 us -> none  [the longest x48 5.39 us: tendency(): jnp.roll(w_mid, 1, axis=2)]
  transfers between devices with their start and end apart: 52 -> 17, of which waited for: 25 -> 6; matrix products, arithmetic and copies ran while one was open for 3% -> 1% of each run, Pallas kernels for 0% -> 6%
where the time goes in v1:
time: 91.8 us; the launch traced here: 90.8 us
  waiting for transfers between devices  45 us (49%)
  starting transfers between devices  22.1 us (24%)
  Pallas kernels  16.5 us (18%)
  local copies, waits for them, and re-layouts  4.55 us (5%)
  other arithmetic  1.76 us (2%)
    ppermute x12, waiting for transfers between devices, relay(): return lax.ppermute(value, ('win', 'lat'), pairs)  34.6 us
    pallas_call x4, Pallas kernels, per_device(): call(functools.partial(window_kernel, z, n_lat * rows, not arrived), [(ro...  13.8 us
    ppermute x12, starting transfers between devices, relay(): return lax.ppermute(value, ('win', 'lat'), pairs)  10.5 us
    ppermute x3, waiting for transfers between devices, per_device(): parts = [lax.ppermute(total, 'win', [(0, w)]) for w in range(1, n_win)]  5.26 us
    ppermute x3, starting transfers between devices, per_device(): parts = [lax.ppermute(total, 'win', [(0, w)]) for w in range(1, n_win)]  5.14 us
    unnamed x12, local copies, waits for them, and re-layouts  4.55 us
    ppermute x1, starting transfers between devices, per_device(): above = lax.ppermute(to_below, 'lat', southward)  4.54 us
    ppermute x1, waiting for transfers between devices, per_device(): below = lax.ppermute(to_above, 'lat', northward)  4.4 us
  transfers between devices with their start and end apart: 17, of which 6 were waited for; matrix products, arithmetic and copies ran while one was open for 1% of the time, Pallas kernels for 6%

profile of v1, /device:TPU:1, one launch (start us, length us, event | category | flops | bytes accessed | tf_op | source)
XLA Modules:
  0.0 90.8 jit_solution(4480165656457518532)
XLA Ops:
  0.6 1.1 %copy-done = f32[1,2,3,8,16,256]{5,4,3,2,1,0:T(8,128)S(1)} copy-done((f32[1,2,3,8,16,256]{5,4,3,2,1,0:T(8,128)S(1)}, f32[1,2,3,8,16,256]{5,4,3,2,1,0:T(8,128)}, u32[]{:S(2)}) %copy-start) | copy-done | bytes 786456
  1.8 0.7 copy-done.1
  4.2 4.5 %collective-permute-start = (f32[24,8,256]{2,1,0:T(8,128)S(1)}, f32[24,8,256]{2,1,0:T(8,128)S(1)}, u32[]{:S(2)}, u32[]{:S(2)}) collective-permute-start(f32[24,8,256]{2,1,0:T(8,128)S(1)} %get-tuple-element.24), channel_id=1, source_target_pairs={{0,1},{1,2},{2,3},{4,5},{5,6},{6,7},{8,9},{9,10},{10,11},{12,13},{... | collective-permute-start | bytes 589832 | tf_op jit(solution)/shard_map/ppermute | solution.py:281
  8.7 1.9 %collective-permute-start.1 = (f32[24,8,256]{2,1,0:T(8,128)S(1)}, f32[24,8,256]{2,1,0:T(8,128)S(1)}, u32[]{:S(2)}, u32[]{:S(2)}) collective-permute-start(f32[24,8,256]{2,1,0:T(8,128)S(1)} %get-tuple-element.25), channel_id=1, source_target_pairs={{1,0},{2,1},{3,2},{5,4},{6,5},{7,6},{9,8},{10,9},{11,10},{13,12},{... | collective-permute-start | bytes 589832 | tf_op jit(solution)/shard_map/ppermute | solution.py:282
  11.3 4.4 %collective-permute-done.1.below_ref = f32[24,8,256]{2,1,0:T(8,128)S(1)} collective-permute-done((f32[24,8,256]{2,1,0:T(8,128)S(1)}, f32[24,8,256]{2,1,0:T(8,128)S(1)}, u32[]{:S(2)}, u32[]{:S(2)}) %collective-permute-start.1) | collective-permute-done | bytes 196640 | tf_op jit(solution)/shard_map/ppermute | solution.py:282
  17.1 0.8 shard_map.78
  17.9 2.8 %shard_map.79 = (f32[16,8,256]{2,1,0:T(8,128)S(1)}, f32[48,8,256]{2,1,0:T(8,128)S(1)}, f32[18,8,256]{2,1,0:T(8,128)S(1)}, f32[18,8,256]{2,1,0:T(8,128)S(1)}) custom-call(f32[168,8,256]{2,1,0:T(8,128)S(1)} %get-tuple-element.27.refs_0_, f32[56,8,256]{2,1,0:T(8,128)S(1)} %get-tuple-element.28.refs_1_, f32[28,8,256]{2,1,0:T(8,128)S(1)} %get-tuple-element.29.refs_2_, ...), custom_call_target="tpu_custom_call" | custom-call | flops 40000000 | bytes 4194304 | tf_op jit(solution)/shard_map/pallas_call | solution.py:307
  20.7 0.7 collective-permute-start.2
  22.8 2.8 %shard_map.80 = (f32[16,8,256]{2,1,0:T(8,128)S(1)}, f32[48,8,256]{2,1,0:T(8,128)S(1)}, f32[18,8,256]{2,1,0:T(8,128)S(1)}, f32[18,8,256]{2,1,0:T(8,128)S(1)}) custom-call(f32[168,8,256]{2,1,0:T(8,128)S(1)} %get-tuple-element.27.refs_0_, f32[56,8,256]{2,1,0:T(8,128)S(1)} %get-tuple-element.28.refs_1_, f32[28,8,256]{2,1,0:T(8,128)S(1)} %get-tuple-element.29.refs_2_, ...), custom_call_target="tpu_custom_call" | custom-call | flops 40000000 | bytes 4194304 | tf_op jit(solution)/shard_map/pallas_call | solution.py:307
  27.7 3.6 %shard_map.81 = (f32[16,8,256]{2,1,0:T(8,128)S(1)}, f32[48,8,256]{2,1,0:T(8,128)}, f32[18,8,256]{2,1,0:T(8,128)}, f32[18,8,256]{2,1,0:T(8,128)}) custom-call(f32[168,8,256]{2,1,0:T(8,128)S(1)} %get-tuple-element.27.refs_0_, f32[56,8,256]{2,1,0:T(8,128)S(1)} %get-tuple-element.28.refs_1_, f32[28,8,256]{2,1,0:T(8,128)S(1)} %get-tuple-element.29.refs_2_, ...), custom_call_target="tpu_custom_call" | custom-call | flops 40000000 | bytes 4194304 | tf_op jit(solution)/shard_map/pallas_call | solution.py:307
  31.4 1.3 %collective-permute-start.8 = (f32[48,8,256]{2,1,0:T(8,128)}, f32[48,8,256]{2,1,0:T(8,128)S(1)}, u32[]{:S(2)}, u32[]{:S(2)}) collective-permute-start(f32[48,8,256]{2,1,0:T(8,128)} %get-tuple-element.38), channel_id=1, source_target_pairs={{4,0},{5,1},{6,2},{7,3},{20,16},{21,17},{22,18},{23,19}} | collective-permute-start | bytes 1179656 | tf_op jit(solution)/shard_map/ppermute | solution.py:301
  34.0 1.3 %collective-permute-start.10 = (f32[18,8,256]{2,1,0:T(8,128)}, f32[18,8,256]{2,1,0:T(8,128)}, u32[]{:S(2)}, u32[]{:S(2)}) collective-permute-start(f32[18,8,256]{2,1,0:T(8,128)} %get-tuple-element.40), channel_id=1, source_target_pairs={{5,0},{6,1},{7,2},{21,16},{22,17},{23,18}} | collective-permute-start | bytes 442376 | tf_op jit(solution)/shard_map/ppermute | solution.py:301
  35.4 1.3 %collective-permute-start.9 = (f32[18,8,256]{2,1,0:T(8,128)}, f32[18,8,256]{2,1,0:T(8,128)}, u32[]{:S(2)}, u32[]{:S(2)}) collective-permute-start(f32[18,8,256]{2,1,0:T(8,128)} %get-tuple-element.39), channel_id=1, source_target_pairs={{4,1},{5,2},{6,3},{20,17},{21,18},{22,19}} | collective-permute-start | bytes 442376 | tf_op jit(solution)/shard_map/ppermute | solution.py:301
  37.3 1.3 %collective-permute-start.13 = (f32[16,8,256]{2,1,0:T(8,128)}, f32[16,8,256]{2,1,0:T(8,128)}, u32[]{:S(2)}, u32[]{:S(2)}) collective-permute-start(f32[16,8,256]{2,1,0:T(8,128)} %add.19), channel_id=1, source_target_pairs={{4,0},{5,1},{6,2},{7,3},{20,16},{21,17},{22,18},{23,19}} | collective-permute-start | bytes 393224 | tf_op jit(solution)/shard_map/ppermute | solution.py:301
  38.6 32.5 %collective-permute-done.10.refs_7_ = f32[18,8,256]{2,1,0:T(8,128)} collective-permute-done((f32[18,8,256]{2,1,0:T(8,128)}, f32[18,8,256]{2,1,0:T(8,128)}, u32[]{:S(2)}, u32[]{:S(2)}) %collective-permute-start.10) | collective-permute-done | bytes 147488 | tf_op jit(solution)/shard_map/ppermute | solution.py:301
  71.1 2.2 %collective-permute-done.9.refs_6_ = f32[18,8,256]{2,1,0:T(8,128)} collective-permute-done((f32[18,8,256]{2,1,0:T(8,128)}, f32[18,8,256]{2,1,0:T(8,128)}, u32[]{:S(2)}, u32[]{:S(2)}) %collective-permute-start.9) | collective-permute-done | bytes 147488 | tf_op jit(solution)/shard_map/ppermute | solution.py:301
  73.3 4.5 %shard_map.82 = (f32[16,8,256]{2,1,0:T(8,128)S(1)}, f32[48,8,256]{2,1,0:T(8,128)S(1)}, f32[18,8,256]{2,1,0:T(8,128)}, f32[18,8,256]{2,1,0:T(8,128)}) custom-call(f32[168,8,256]{2,1,0:T(8,128)S(1)} %get-tuple-element.27.refs_0_, f32[56,8,256]{2,1,0:T(8,128)S(1)} %get-tuple-element.28.refs_1_, f32[28,8,256]{2,1,0:T(8,128)S(1)} %get-tuple-element.29.refs_2_, ...), custom_call_target="tpu_custom_call" | custom-call | flops 40000000 | bytes 4194304 | tf_op jit(solution)/shard_map/pallas_call | solution.py:307
  77.8 0.9 %add.20 = f32[16,8,256]{2,1,0:T(8,128)S(1)} add(f32[16,8,256]{2,1,0:T(8,128)} %collective-permute-done.13, f32[16,8,256]{2,1,0:T(8,128)S(1)} %get-tuple-element.45) | non-fusion elementwise | flops 32768 | bytes 393216 | tf_op jit(solution)/shard_map/add | solution.py:321
  78.7 2.5 %collective-permute-start.14 = (f32[16,8,256]{2,1,0:T(8,128)S(1)}, f32[16,8,256]{2,1,0:T(8,128)S(1)}, u32[]{:S(2)}, u32[]{:S(2)}) collective-permute-start(f32[16,8,256]{2,1,0:T(8,128)S(1)} %add.20), channel_id=1, source_target_pairs={{0,4},{1,5},{2,6},{3,7},{16,20},{17,21},{18,22},{19,23}} | collective-permute-start | bytes 393224 | tf_op jit(solution)/shard_map/ppermute | solution.py:329
  81.3 1.3 %collective-permute-start.15 = (f32[16,8,256]{2,1,0:T(8,128)S(1)}, f32[16,8,256]{2,1,0:T(8,128)S(1)}, u32[]{:S(2)}, u32[]{:S(2)}) collective-permute-start(f32[16,8,256]{2,1,0:T(8,128)S(1)} %add.20), channel_id=1, source_target_pairs={{0,8},{1,9},{2,10},{3,11},{16,24},{17,25},{18,26},{19,27}} | collective-permute-start | bytes 393224 | tf_op jit(solution)/shard_map/ppermute | solution.py:329
  82.6 1.3 %collective-permute-start.16 = (f32[16,8,256]{2,1,0:T(8,128)S(1)}, f32[16,8,256]{2,1,0:T(8,128)S(1)}, u32[]{:S(2)}, u32[]{:S(2)}) collective-permute-start(f32[16,8,256]{2,1,0:T(8,128)S(1)} %add.20), channel_id=1, source_target_pairs={{0,12},{1,13},{2,14},{3,15},{16,28},{17,29},{18,30},{19,31}} | collective-permute-start | bytes 393224 | tf_op jit(solution)/shard_map/ppermute | solution.py:329
  84.0 0.8 shard_map.83
  84.8 2.4 %collective-permute-done.15 = f32[16,8,256]{2,1,0:T(8,128)S(1)} collective-permute-done((f32[16,8,256]{2,1,0:T(8,128)S(1)}, f32[16,8,256]{2,1,0:T(8,128)S(1)}, u32[]{:S(2)}, u32[]{:S(2)}) %collective-permute-start.15) | collective-permute-done | bytes 131104 | tf_op jit(solution)/shard_map/ppermute | solution.py:329
  87.3 2.8 %collective-permute-done.16 = f32[16,8,256]{2,1,0:T(8,128)S(1)} collective-permute-done((f32[16,8,256]{2,1,0:T(8,128)S(1)}, f32[16,8,256]{2,1,0:T(8,128)S(1)}, u32[]{:S(2)}, u32[]{:S(2)}) %collective-permute-start.16) | collective-permute-done | bytes 131104 | tf_op jit(solution)/shard_map/ppermute | solution.py:329
  (35 shorter events, 10.0 us)
Async XLA Ops:
  0.6 1.1 %copy-start = (f32[1,2,3,8,16,256]{5,4,3,2,1,0:T(8,128)S(1)}, f32[1,2,3,8,16,256]{5,4,3,2,1,0:T(8,128)}, u32[]{:S(2)}) copy-start(f32[1,2,3,8,16,256]{5,4,3,2,1,0:T(8,128)} %param.6) | copy-start | bytes 2359300
  1.8 0.7 copy-start.1
  2.5 0.7 copy-start.3
  3.2 0.7 copy-start.4
  4.2 7.1 %collective-permute-start = (f32[24,8,256]{2,1,0:T(8,128)S(1)}, f32[24,8,256]{2,1,0:T(8,128)S(1)}, u32[]{:S(2)}, u32[]{:S(2)}) collective-permute-start(f32[24,8,256]{2,1,0:T(8,128)S(1)} %get-tuple-element.24), channel_id=1, source_target_pairs={{0,1},{1,2},{2,3},{4,5},{5,6},{6,7},{8,9},{9,10},{10,11},{12,13},{... | collective-permute-start | bytes 589832 | tf_op jit(solution)/shard_map/ppermute | solution.py:281
  8.7 7.0 %collective-permute-start.1 = (f32[24,8,256]{2,1,0:T(8,128)S(1)}, f32[24,8,256]{2,1,0:T(8,128)S(1)}, u32[]{:S(2)}, u32[]{:S(2)}) collective-permute-start(f32[24,8,256]{2,1,0:T(8,128)S(1)} %get-tuple-element.25), channel_id=1, source_target_pairs={{1,0},{2,1},{3,2},{5,4},{6,5},{7,6},{9,8},{10,9},{11,10},{13,12},{... | collective-permute-start | bytes 589832 | tf_op jit(solution)/shard_map/ppermute | solution.py:282
  15.7 0.7 copy-start.2
  16.4 0.7 copy-start.5
  20.7 2.1 %collective-permute-start.2 = (f32[48,8,256]{2,1,0:T(8,128)S(1)}, f32[48,8,256]{2,1,0:T(8,128)S(1)}, u32[]{:S(2)}, u32[]{:S(2)}) collective-permute-start(f32[48,8,256]{2,1,0:T(8,128)S(1)} %get-tuple-element.32), channel_id=1, source_target_pairs={{12,8},{13,9},{14,10},{15,11},{28,24},{29,25},{30,26},{31,27}} | collective-permute-start | bytes 1179656 | tf_op jit(solution)/shard_map/ppermute | solution.py:301
  21.4 1.4 %collective-permute-start.3 = (f32[18,8,256]{2,1,0:T(8,128)S(1)}, f32[18,8,256]{2,1,0:T(8,128)S(1)}, u32[]{:S(2)}, u32[]{:S(2)}) collective-permute-start(f32[18,8,256]{2,1,0:T(8,128)S(1)} %get-tuple-element.33), channel_id=1, source_target_pairs={{12,9},{13,10},{14,11},{28,25},{29,26},{30,27}} | collective-permute-start | bytes 442376 | tf_op jit(solution)/shard_map/ppermute | solution.py:301
  22.1 0.7 collective-permute-start.4
  25.6 2.1 %collective-permute-start.5 = (f32[48,8,256]{2,1,0:T(8,128)S(1)}, f32[48,8,256]{2,1,0:T(8,128)S(1)}, u32[]{:S(2)}, u32[]{:S(2)}) collective-permute-start(f32[48,8,256]{2,1,0:T(8,128)S(1)} %get-tuple-element.35), channel_id=1, source_target_pairs={{8,4},{9,5},{10,6},{11,7},{24,20},{25,21},{26,22},{27,23}} | collective-permute-start | bytes 1179656 | tf_op jit(solution)/shard_map/ppermute | solution.py:301
  26.3 1.4 %collective-permute-start.6 = (f32[18,8,256]{2,1,0:T(8,128)S(1)}, f32[18,8,256]{2,1,0:T(8,128)S(1)}, u32[]{:S(2)}, u32[]{:S(2)}) collective-permute-start(f32[18,8,256]{2,1,0:T(8,128)S(1)} %get-tuple-element.36), channel_id=1, source_target_pairs={{8,5},{9,6},{10,7},{24,21},{25,22},{26,23}} | collective-permute-start | bytes 442376 | tf_op jit(solution)/shard_map/ppermute | solution.py:301
  27.0 0.7 collective-permute-start.7
  31.4 41.9 %collective-permute-start.8 = (f32[48,8,256]{2,1,0:T(8,128)}, f32[48,8,256]{2,1,0:T(8,128)S(1)}, u32[]{:S(2)}, u32[]{:S(2)}) collective-permute-start(f32[48,8,256]{2,1,0:T(8,128)} %get-tuple-element.38), channel_id=1, source_target_pairs={{4,0},{5,1},{6,2},{7,3},{20,16},{21,17},{22,18},{23,19}} | collective-permute-start | bytes 1179656 | tf_op jit(solution)/shard_map/ppermute | solution.py:301
  32.7 0.7 collective-permute-start.11
  33.4 3.3 %collective-permute-start.12 = (f32[16,8,256]{2,1,0:T(8,128)S(1)}, f32[16,8,256]{2,1,0:T(8,128)S(1)}, u32[]{:S(2)}, u32[]{:S(2)}) collective-permute-start(f32[16,8,256]{2,1,0:T(8,128)S(1)} %add.18), channel_id=1, source_target_pairs={{8,4},{9,5},{10,6},{11,7},{24,20},{25,21},{26,22},{27,23}} | collective-permute-start | bytes 393224 | tf_op jit(solution)/shard_map/ppermute | solution.py:301
  34.0 37.0 %collective-permute-start.10 = (f32[18,8,256]{2,1,0:T(8,128)}, f32[18,8,256]{2,1,0:T(8,128)}, u32[]{:S(2)}, u32[]{:S(2)}) collective-permute-start(f32[18,8,256]{2,1,0:T(8,128)} %get-tuple-element.40), channel_id=1, source_target_pairs={{5,0},{6,1},{7,2},{21,16},{22,17},{23,18}} | collective-permute-start | bytes 442376 | tf_op jit(solution)/shard_map/ppermute | solution.py:301
  35.4 37.9 %collective-permute-start.9 = (f32[18,8,256]{2,1,0:T(8,128)}, f32[18,8,256]{2,1,0:T(8,128)}, u32[]{:S(2)}, u32[]{:S(2)}) collective-permute-start(f32[18,8,256]{2,1,0:T(8,128)} %get-tuple-element.39), channel_id=1, source_target_pairs={{4,1},{5,2},{6,3},{20,17},{21,18},{22,19}} | collective-permute-start | bytes 442376 | tf_op jit(solution)/shard_map/ppermute | solution.py:301
  37.3 40.4 %collective-permute-start.13 = (f32[16,8,256]{2,1,0:T(8,128)}, f32[16,8,256]{2,1,0:T(8,128)}, u32[]{:S(2)}, u32[]{:S(2)}) collective-permute-start(f32[16,8,256]{2,1,0:T(8,128)} %add.19), channel_id=1, source_target_pairs={{4,0},{5,1},{6,2},{7,3},{20,16},{21,17},{22,18},{23,19}} | collective-permute-start | bytes 393224 | tf_op jit(solution)/shard_map/ppermute | solution.py:301
  78.7 6.1 %collective-permute-start.14 = (f32[16,8,256]{2,1,0:T(8,128)S(1)}, f32[16,8,256]{2,1,0:T(8,128)S(1)}, u32[]{:S(2)}, u32[]{:S(2)}) collective-permute-start(f32[16,8,256]{2,1,0:T(8,128)S(1)} %add.20), channel_id=1, source_target_pairs={{0,4},{1,5},{2,6},{3,7},{16,20},{17,21},{18,22},{19,23}} | collective-permute-start | bytes 393224 | tf_op jit(solution)/shard_map/ppermute | solution.py:329
  81.3 6.0 %collective-permute-start.15 = (f32[16,8,256]{2,1,0:T(8,128)S(1)}, f32[16,8,256]{2,1,0:T(8,128)S(1)}, u32[]{:S(2)}, u32[]{:S(2)}) collective-permute-start(f32[16,8,256]{2,1,0:T(8,128)S(1)} %add.20), channel_id=1, source_target_pairs={{0,8},{1,9},{2,10},{3,11},{16,24},{17,25},{18,26},{19,27}} | collective-permute-start | bytes 393224 | tf_op jit(solution)/shard_map/ppermute | solution.py:329
  82.6 7.5 %collective-permute-start.16 = (f32[16,8,256]{2,1,0:T(8,128)S(1)}, f32[16,8,256]{2,1,0:T(8,128)S(1)}, u32[]{:S(2)}, u32[]{:S(2)}) collective-permute-start(f32[16,8,256]{2,1,0:T(8,128)S(1)} %add.20), channel_id=1, source_target_pairs={{0,12},{1,13},{2,14},{3,15},{16,28},{17,29},{18,30},{19,31}} | collective-permute-start | bytes 393224 | tf_op jit(solution)/shard_map/ppermute | solution.py:329

commit v2 on v1

v2 whole, which is shorter than its diff:
```python
import functools

import jax
import jax.numpy as jnp
from jax import lax
from jax.experimental import pallas as pl
from jax.experimental.pallas import tpu as pltpu
from jax.sharding import PartitionSpec as P

STEP_DT = 0.2
THIRD = 1.0 / 3.0
TWO_THIRDS = 2.0 / 3.0
STAGES = 3
WEIGHTS = (1.0, 0.25, TWO_THIRDS)
SUBLANES = 8
LANES = 128

VMEM = pl.BlockSpec(memory_space=pltpu.VMEM)
HBM = pl.BlockSpec(memory_space=pltpu.HBM)
SMEM = pl.BlockSpec(memory_space=pltpu.SMEM)


class Sizes:
    def __init__(self, steps, layers, rows, cols):
        self.steps, self.layers, self.rows, self.cols = steps, layers, rows, cols
        self.halo = STAGES * steps
        self.ext = rows + 2 * self.halo
        self.first = [sum(self.halo - m for m in range(j)) for j in range(self.halo)]
        self.halo_rows = sum(self.halo - m for m in range(self.halo))
        self.tiles = rows // SUBLANES
        self.tail = -(-(steps + 1) * self.halo // SUBLANES)
        self.packed = self.halo_rows + self.tail
        self.fields = self.halo * rows + (steps + 1) * self.tiles

    def section(self, j):
        step, stage = self.steps - 1 - j // STAGES, j % STAGES
        return (step * STAGES + stage) * self.layers * self.rows


def rows_first(z, ref, base):
    lines = []
    for tile in range(z.rows // SUBLANES):
        block = jnp.stack(
            [ref[base + l * z.rows + tile * SUBLANES : base + l * z.rows + (tile + 1) * SUBLANES, :] for l in range(z.layers)]
        )
        block = jnp.swapaxes(block, 0, 1)
        lines.extend(block[m] for m in range(SUBLANES))
    return lines


def layers_first(z, ref, start, lines):
    for tile in range(z.rows // SUBLANES):
        block = jnp.swapaxes(jnp.stack(lines[tile * SUBLANES : (tile + 1) * SUBLANES]), 0, 1)
        for l in range(z.layers):
            low = start + l * z.rows + tile * SUBLANES
            ref[low : low + SUBLANES, :] = block[l]


def pack_kernel(z, th_in, cells_in, values_in, mask_in, up_ref, down_ref, own_ref, th_ref, cells_ref, values_ref, mask_ref, sem):
    copies = [
        pltpu.make_async_copy(source, target, sem.at[i])
        for i, (source, target) in enumerate(
            ((cells_in, cells_ref), (values_in, values_ref), (mask_in, mask_ref), (th_in, th_ref))
        )
    ]
    for copy in copies:
        copy.start()
    for copy in copies[:3]:
        copy.wait()
    count = cells_ref.shape[1]
    row_ids = lax.broadcasted_iota(jnp.int32, (z.rows, count), 0)
    col_ids = lax.broadcasted_iota(jnp.int32, (z.cols, count), 0)
    for order in range(z.steps):
        step = z.steps - 1 - order
        cells = cells_ref[step : step + 1, :]
        values = values_ref[step : step + 1, :]
        by_row = jnp.where(row_ids == cells // z.cols, values, 0.0)
        by_col = jnp.where(col_ids == cells % z.cols, 1.0, 0.0).astype(jnp.bfloat16)
        field = jnp.zeros((z.rows, z.cols), jnp.float32)
        for _ in range(3):
            part = by_row.astype(jnp.bfloat16)
            by_row = by_row - part.astype(jnp.float32)
            field = field + lax.dot_general(
                part, by_col, (((1,), (1,)), ((), ())), preferred_element_type=jnp.float32
            )
        own_ref[order * z.tiles : (order + 1) * z.tiles] = field.reshape(z.tiles, SUBLANES, z.cols)
    ocean = mask_ref[...].astype(jnp.float32) * (0.5 * STEP_DT)
    own_ref[z.steps * z.tiles :] = ocean.reshape(z.tiles, SUBLANES, z.cols)
    copies[3].wait()
    for j in range(z.halo):
        lines, need = rows_first(z, th_ref, z.section(j)), z.halo - j
        for m in range(need):
            up_ref[z.first[j] + m] = lines[m]
            down_ref[z.first[j] + m] = lines[z.rows - need + m]
    for k in range(z.steps + 1):
        for m in range(z.halo):
            tile, line = divmod(k * z.halo + m, SUBLANES)
            for ref, row in ((up_ref, m), (down_ref, z.rows - z.halo + m)):
                from_tile, from_line = divmod(k * z.rows + row, SUBLANES)
                ref[z.halo_rows + tile, line : line + 1, :] = own_ref[from_tile, from_line : from_line + 1, :]
    for q in range((z.steps + 1) * z.halo, z.tail * SUBLANES):
        tile, line = divmod(q, SUBLANES)
        for ref in (up_ref, down_ref):
            ref[z.halo_rows + tile, line : line + 1, :] = jnp.zeros((1, z.cols), jnp.float32)


def own_kernel(z, coupling_ref, damping_ref, th_ref, own_ref, h_ref, oc_ref, keep_ref, mix_ref):
    layer_ids = lax.broadcasted_iota(jnp.int32, (z.layers, LANES), 0)
    half = z.layers // 2
    for j in range(z.layers):
        line = jnp.zeros((z.layers, LANES), jnp.float32)
        for l in range(z.layers):
            target = l if j < half else (l + half) % z.layers
            k = (target - j) % z.layers
            weight = coupling_ref[k, target] + (1.0 if k == target else 0.0)
            line = jnp.where(layer_ids == l, weight, line)
        mix_ref[j * z.layers : (j + 1) * z.layers, :] = line
    rate = jnp.zeros((z.layers, LANES), jnp.float32)
    for l in range(z.layers):
        rate = jnp.where(layer_ids == l, 2.0 * damping_ref[l], rate)
    mix_ref[z.layers * z.layers :, :] = rate
    rate = jnp.concatenate([rate] * (z.cols // LANES), axis=1)
    for r in range(z.rows):
        tile, line = divmod(z.steps * z.rows + r, SUBLANES)
        oc = jnp.broadcast_to(own_ref[tile, line : line + 1, :], (z.layers, z.cols))
        keep = 1.0 - oc * rate
        for stage, weight in enumerate(WEIGHTS):
            oc_ref[stage * z.rows + r] = weight * oc
            keep_ref[stage * z.rows + r] = weight * keep
    for j in range(z.halo):
        for r, line in enumerate(rows_first(z, th_ref, z.section(j))):
            h_ref[j * z.rows + r] = line
    h_ref[z.halo * z.rows :] = own_ref[...]


def window_kernel(z, total_rows, first, last, target_win, *refs):
    h_ref, above_ref, below_ref = refs[:3]
    refs = refs[3:]
    own_ref = h_ref.at[pl.ds(z.halo * z.rows, (z.steps + 1) * z.tiles)]
    oc_ref, keep_ref, mix_ref = refs[:3]
    state, refs = refs[3 : 3 if first else 6], refs[3 if first else 6 :]
    if not first:
        lam_in, bias_in, refs = refs[0], refs[1], refs[2:]
        mine = lax.axis_index("win") == target_win
    if last:
        (bias_ref, lam_ref), refs = refs[:2], refs[2:]
    else:
        (bias_ref, lam_ref, main_ref, top_ref, bottom_ref), refs = refs[:5], refs[5:]
    x_ref, y_ref, w_ref, sum_ref, oc_out, keep_out = refs
    halo, ext, rows, layers = z.halo, z.ext, z.rows, z.layers
    first_row = lax.axis_index("lat") * rows - halo
    parts = z.cols // LANES
    lanes = [slice(i * LANES, (i + 1) * LANES) for i in range(parts)]
    shape = (layers, LANES)
    lane_ids = lax.broadcasted_iota(jnp.int32, shape, 1)
    at_start, at_end = lane_ids == 0, lane_ids == LANES - 1
    mixers = [mix_ref[j * layers : (j + 1) * layers, :] for j in range(layers)]

    def read(ref, row):
        return [ref[row, :, lane] for lane in lanes]

    def write(ref, row, values):
        for lane, value in zip(lanes, values):
            ref[row, :, lane] = value

    def each(function, *values):
        return [function(*v) for v in zip(*values)]

    def line(k, e):
        if e < halo:
            ref, (tile, at) = above_ref, divmod(k * halo + e, SUBLANES)
            tile += z.halo_rows
        elif e >= halo + rows:
            ref, (tile, at) = below_ref, divmod(k * halo + e - halo - rows, SUBLANES)
            tile += z.halo_rows
        else:
            ref, (tile, at) = own_ref, divmod(k * rows + e - halo, SUBLANES)
        return [jnp.broadcast_to(ref[tile, at : at + 1, lane], shape) for lane in lanes]

    def add(x, y):
        return each(lambda u, v: u + v, x, y)

    def incoming(c, e):
        main_in, above_in, below_in = state
        if e < halo:
            return read(above_in, c * halo + e)
        if e >= halo + rows:
            return read(below_in, c * halo + e - halo - rows)
        return read(main_in, c * rows + e - halo)

    def east(values):
        out = []
        for i, value in enumerate(values):
            after = jnp.where(at_start, values[(i + 1) % parts], value)
            before = jnp.where(at_end, values[i - 1], value)
            out.append(pltpu.roll(after, LANES - 1, axis=1) - pltpu.roll(before, 1, axis=1))
        return out

    def mixed(value):
        half = layers // 2
        low, high = mixers[0] * value, mixers[half] * value
        for k in range(1, half):
            turned = pltpu.roll(value, k, axis=0)
            low = low + mixers[k] * turned
            high = high + mixers[half + k] * turned
        return low + pltpu.roll(high, half, axis=0)

    zero = [jnp.zeros(shape, jnp.float32)] * parts
    for e in range(ext):
        a, p, q = (zero, zero, zero) if first else (incoming(c, e) for c in range(3))
        write(x_ref, e, add(a, line(0, e)))
        write(x_ref, ext + e, p)
        write(x_ref, 2 * ext + e, q)
    rate = mix_ref[layers * layers :, :]
    for i in range(2 * halo):
        oc = line(z.steps, i if i < halo else rows + i)
        keep = each(lambda v: 1.0 - v * rate, oc)
        for stage, weight in enumerate(WEIGHTS):
            write(oc_out, stage * 2 * halo + i, each(lambda v: weight * v, oc))
            write(keep_out, stage * 2 * halo + i, each(lambda v: weight * v, keep))

    def factors(stage, e):
        if halo <= e < halo + rows:
            return (read(ref, stage * rows + e - halo) for ref in (oc_ref, keep_ref))
        i = e if e < halo else e - rows
        return (read(ref, stage * 2 * halo + i) for ref in (oc_out, keep_out))

    def thickness(j, e):
        if e < halo:
            return read(above_ref, z.first[j] + e - j)
        if e >= halo + rows:
            return read(below_ref, z.first[j] + e - halo - rows)
        return read(h_ref, j * rows + e - halo)

    def run(j):
        order, stage = divmod(j, STAGES)
        source = (x_ref, y_ref, w_ref)[stage]
        target = (y_ref, w_ref, x_ref)[stage]
        low, high = j + 1, ext - j - 1

        def weighted(e, values):
            return each(lambda h, v: h * v, thickness(j, e), values)

        def body(e, carry):
            place = e - halo if halo <= e < halo + rows else None
            b_before, b_here, a_here, q_before, q_here = carry
            a_after, q_after = read(source, e + 1), read(source, 2 * ext + e + 1)
            b_after = weighted(e + 1, a_after)
            p_here = read(source, ext + e)
            oc, keep = factors(stage, e)
            row = jnp.asarray(first_row + e).astype(jnp.float32)
            coriolis = 2.0 * (0.3 + 0.4 * (row * (1.0 / total_rows) - 0.5))
            divergence = each(lambda x, n, s: x + (n - s), east(p_here), q_after, q_before)
            a = each(lambda k, v, o, m: k * v + o * mixed(m), keep, a_here, oc, divergence)
            p = each(lambda k, v, o, d, u: k * v + o * (d + coriolis * u), keep, p_here, oc, east(b_here), q_here)
            q = each(
                lambda k, v, o, n, s, u: k * v + o * ((n - s) - coriolis * u),
                keep, q_here, oc, b_after, b_before, p_here,
            )
            if stage:
                rest = 1.0 - WEIGHTS[stage]
                start = [read(x_ref, c * ext + e) for c in range(3)]
                a, p, q = (each(lambda s, v: rest * s + v, start[c], v) for c, v in enumerate((a, p, q)))
            if stage == STAGES - 1:
                if place is not None:
                    part = each(lambda v: STEP_DT * v, a)
                    if order > 0:
                        part = add(part, read(sum_ref, place))
                    if order < z.steps - 1:
                        write(sum_ref, place, part)
                    else:
                        if not first:
                            part = each(lambda v, o: jnp.where(mine, v, o), part, read(bias_in, place))
                        write(bias_ref, place, part)
                    if order == z.steps - 1:
                        for c, value in enumerate((a, p, q)):
                            if not last:
                                write(main_ref, c * rows + place, value)
                            if not first:
                                old = read(lam_in, c * rows + place)
                                value = each(lambda v, o: jnp.where(mine, v, o), value, old)
                            write(lam_ref, c * rows + place, value)
                if order < z.steps - 1:
                    a = add(a, line(order + 1, e))
            if j < halo - 1:
                for c, value in enumerate((a, p, q)):
                    write(target, c * ext + e, value)
            return b_here, b_after, a_after, q_here, q_after

        a_first = read(source, low)
        carry = (
            weighted(low - 1, read(source, low - 1)),
            weighted(low, a_first),
            a_first,
            read(source, 2 * ext + low - 1),
            read(source, 2 * ext + low),
        )
        for e in range(low, high):
            carry = body(e, carry)

    for j in range(halo):
        run(j)
    if not last:
        for c in range(3):
            for m in range(halo):
                top_ref[c * halo + m] = main_ref[c * rows + m]
                bottom_ref[c * halo + m] = main_ref[c * rows + rows - halo + m]


def turn_kernel(z, count, lines_ref, out_ref):
    for c in range(count):
        layers_first(z, out_ref, c * z.layers * z.rows, [lines_ref[c * z.rows + r] for r in range(z.rows)])


def call(kernel, out_shapes, in_specs, scratch=(), cost=0, limit=8 << 20, space=pltpu.VMEM):
    return pl.pallas_call(
        kernel,
        out_shape=[space(s, jnp.float32) for s in out_shapes],
        in_specs=in_specs,
        out_specs=[VMEM] * len(out_shapes),
        scratch_shapes=list(scratch),
        compiler_params=pltpu.CompilerParams(vmem_limit_bytes=limit),
        cost_estimate=pl.CostEstimate(flops=cost, bytes_accessed=4 << 20, transcendentals=0),
    )


def window_scratch(z):
    counts = [3 * z.ext] * 3 + [z.rows] + [STAGES * 2 * z.halo] * 2
    return [pltpu.VMEM((count, z.layers, z.cols), jnp.float32) for count in counts]


def per_device(thickness, obs_cells, obs_values, ocean_mask, coupling, damping):
    _, steps, stages, layers, rows, cols = thickness.shape
    z = Sizes(steps, layers, rows, cols)
    n_win, n_lat = lax.axis_size("win"), lax.axis_size("lat")
    win = lax.axis_index("win")
    flat = thickness.reshape(steps * stages * layers * rows, cols)
    cube = (layers, cols)
    count = obs_cells.shape[2]

    to_above, to_below, own = call(
        functools.partial(pack_kernel, z),
        [(z.packed,) + cube, (z.packed,) + cube, ((steps + 1) * z.tiles,) + cube],
        [HBM] * 4,
        [
            pltpu.VMEM(flat.shape, jnp.float32),
            pltpu.VMEM((steps, count), jnp.int32),
            pltpu.VMEM((steps, count), jnp.float32),
            pltpu.VMEM((rows, cols), jnp.int32),
            pltpu.SemaphoreType.DMA((4,)),
        ],
        limit=60 << 20,
    )(flat, obs_cells[0], obs_values[0], ocean_mask)
    southward = [(i, i + 1) for i in range(n_lat - 1)]
    northward = [(i + 1, i) for i in range(n_lat - 1)]
    above = lax.ppermute(to_below, "lat", southward)
    below = lax.ppermute(to_above, "lat", northward)
    h, *tables = call(
        functools.partial(own_kernel, z),
        [
            (z.fields,) + cube,
            (STAGES * rows,) + cube,
            (STAGES * rows,) + cube,
            ((layers + 1) * layers, LANES),
        ],
        [SMEM, SMEM, VMEM, VMEM],
    )(coupling, damping, flat, own)

    def relay(value, source_win, target_win, shift=0):
        pairs = [
            (source_win * n_lat + i, target_win * n_lat + i + shift)
            for i in range(n_lat)
            if 0 <= i + shift < n_lat
        ]
        return lax.ppermute(value, ("win", "lat"), pairs)

    fields = (h, above, below, *tables)
    one, state_rows, halo_rows = ((n,) + cube for n in (rows, 3 * rows, 3 * z.halo))

    def window(target_win, state, results):
        last = target_win == 0
        outs = [one, state_rows] if last else [one, state_rows, state_rows, halo_rows, halo_rows]
        operands = fields + state + results
        return call(
            functools.partial(window_kernel, z, n_lat * rows, not state, last, target_win),
            outs,
            [VMEM] * len(operands),
            window_scratch(z),
            cost=40_000_000,
        )(*operands)

    bias, lam, main, top, bottom = window(n_win - 1, (), ())
    for source_win in range(n_win - 1, 0, -1):
        state = (
            relay(main, source_win, source_win - 1),
            relay(bottom, source_win, source_win - 1, 1),
            relay(top, source_win, source_win - 1, -1),
        )
        if source_win > 1:
            bias, lam, main, top, bottom = window(source_win - 1, state, (lam, bias))
    others = n_win - 1
    for shift in range(1, others):
        pairs = [
            ((1 + w) * n_lat + i, (1 + (w + shift) % others) * n_lat + i) for w in range(others) for i in range(n_lat)
        ]
        part = lax.ppermute(bias, ("win", "lat"), pairs)
        total = part if shift == 1 else total + part
    total = bias if others == 1 else bias + total
    mine, lam = window(0, state, (lam, total))
    swap = [(a * n_lat + i, (1 - a) * n_lat + i) for a in range(2) for i in range(n_lat)]
    result = mine + sum(relay(mine, 0, target_win) for target_win in range(n_win - 1, 1, -1))
    result = result + lax.ppermute(mine, ("win", "lat"), swap)
    (lam,) = call(functools.partial(turn_kernel, z, 3), [(3 * layers * rows, cols)], [VMEM], space=jax.ShapeDtypeStruct)(lam)
    (result,) = call(functools.partial(turn_kernel, z, 1), [(layers * rows, cols)], [VMEM], space=jax.ShapeDtypeStruct)(result)
    return lam.reshape(1, 3, layers, rows, cols), result.reshape(layers, rows, cols)


def solution(mesh):
    in_specs = (
        P(("groups", "win"), None, None, None, "lat", None),
        P(("groups", "win"), None, "lat"),
        P(("groups", "win"), None, "lat"),
        P(("groups", "lat"), None),
        P(),
        P(),
    )
    out_specs = (P(("groups", "win"), None, None, "lat", None), P("groups", "lat", None))
    return jax.shard_map(
        per_device, mesh=mesh, in_specs=in_specs, out_specs=out_specs, check_vma=False
    )
```

time: 91.8 us -> 79.3 us (0.86)
  the two profiles are of different devices: /device:TPU:1 before, /device:TPU:0 now
where the time goes in v2:
time: 79.3 us; the launch traced here: 78.9 us
  waiting for transfers between devices  50.4 us (64%)
  starting transfers between devices  16.8 us (21%)
  Pallas kernels  10.7 us (13%)
  between operations  0.94 us (1%)
    ppermute x11, waiting for transfers between devices, relay(): return lax.ppermute(value, ('win', 'lat'), pairs)  45.5 us
    ppermute x11, starting transfers between devices, relay(): return lax.ppermute(value, ('win', 'lat'), pairs)  9.9 us
    pallas_call x4, Pallas kernels, window(): call(functools.partial(window_kernel, z, n_lat * rows, not state, last, t...  7 us
    ppermute x1, waiting for transfers between devices, per_device(): below = lax.ppermute(to_above, 'lat', northward)  3.31 us
    ppermute x1, starting transfers between devices, per_device(): above = lax.ppermute(to_below, 'lat', southward)  2.37 us
    ppermute x1, starting transfers between devices, per_device(): result = result + lax.ppermute(mine, ('win', 'lat'), swap)  1.92 us
  transfers between devices with their start and end apart: 16, of which 5 were waited for; matrix products, arithmetic and copies ran while one was open for 0% of the time, Pallas kernels for 2%

profile of v2, /device:TPU:0, one launch (start us, length us, event | category | flops | bytes accessed | tf_op | source)
XLA Modules:
  0.0 78.9 jit_solution(10300605560763513655)
XLA Ops:
  0.6 1.4 %shard_map.77 = (f32[24,8,256]{2,1,0:T(8,128)S(1)}, f32[24,8,256]{2,1,0:T(8,128)S(1)}, f32[6,8,256]{2,1,0:T(8,128)S(1)}) custom-call(f32[768,256]{1,0:T(8,128)} %bitcast.5, s32[2,256]{1,0:T(2,128)} %bitcast.9, f32[2,256]{1,0:T(2,128)} %bitcast.10, s32[16,256]{1,0:T(8,128)} %mask_in.1), custom_call_target="tpu_custom_call" | custom-call | bytes 4194304 | tf_op jit(solution)/shard_map/pallas_call | solution.py:341
  2.0 2.4 %collective-permute-start = (f32[24,8,256]{2,1,0:T(8,128)S(1)}, f32[24,8,256]{2,1,0:T(8,128)S(1)}, u32[]{:S(2)}, u32[]{:S(2)}) collective-permute-start(f32[24,8,256]{2,1,0:T(8,128)S(1)} %get-tuple-element.28), channel_id=1, source_target_pairs={{0,1},{1,2},{2,3},{4,5},{5,6},{6,7},{8,9},{9,10},{10,11},{12,13},{... | collective-permute-start | bytes 589832 | tf_op jit(solution)/shard_map/ppermute | solution.py:356
  4.4 1.3 %collective-permute-start.1 = (f32[24,8,256]{2,1,0:T(8,128)S(1)}, f32[24,8,256]{2,1,0:T(8,128)S(1)}, u32[]{:S(2)}, u32[]{:S(2)}) collective-permute-start(f32[24,8,256]{2,1,0:T(8,128)S(1)} %get-tuple-element.29), channel_id=1, source_target_pairs={{1,0},{2,1},{3,2},{5,4},{6,5},{7,6},{9,8},{10,9},{11,10},{13,12},{... | collective-permute-start | bytes 589832 | tf_op jit(solution)/shard_map/ppermute | solution.py:357
  5.8 0.8 %shard_map.78 = (f32[102,8,256]{2,1,0:T(8,128)S(1)}, f32[48,8,256]{2,1,0:T(8,128)S(1)}, f32[48,8,256]{2,1,0:T(8,128)S(1)}, f32[72,128]{1,0:T(8,128)S(1)}) custom-call(f32[8,8]{1,0:T(8,128)S(1)} %copy-done.1, f32[8]{0:T(128)S(1)} %copy-done.2, f32[768,256]{1,0:T(8,128)S(1)} %bitcast.6, f32[6,8,256]{2,1,0:T(8,128)S(1)} %get-tuple-element.26.own_ref), custom_call_target="tpu_custom_call" | custom-call | bytes 4194304 | tf_op jit(solution)/shard_map/pallas_call | solution.py:358
  6.6 3.3 %collective-permute-done.1.refs_2_ = f32[24,8,256]{2,1,0:T(8,128)S(1)} collective-permute-done((f32[24,8,256]{2,1,0:T(8,128)S(1)}, f32[24,8,256]{2,1,0:T(8,128)S(1)}, u32[]{:S(2)}, u32[]{:S(2)}) %collective-permute-start.1) | collective-permute-done | bytes 196640 | tf_op jit(solution)/shard_map/ppermute | solution.py:357
  9.9 1.6 %shard_map.79 = (f32[16,8,256]{2,1,0:T(8,128)S(1)}, f32[48,8,256]{2,1,0:T(8,128)S(1)}, f32[48,8,256]{2,1,0:T(8,128)S(1)}, f32[18,8,256]{2,1,0:T(8,128)S(1)}, f32[18,8,256]{2,1,0:T(8,128)S(1)}) custom-call(f32[102,8,256]{2,1,0:T(8,128)S(1)} %get-tuple-element.27.refs_0_, f32[24,8,256]{2,1,0:T(8,128)S(1)} %collective-permute-done.refs_1_, ...), custom_call_target="tpu_custom_call" | custom-call | flops 40000000 | bytes 4194304 | tf_op jit(solution)/shard_map/pallas_call | solution.py:384
  11.5 0.7 collective-permute-start.2
  12.2 0.7 collective-permute-start.3
  12.9 0.7 collective-permute-start.4
  13.6 1.8 %shard_map.80 = (f32[16,8,256]{2,1,0:T(8,128)S(1)}, f32[48,8,256]{2,1,0:T(8,128)S(1)}, f32[48,8,256]{2,1,0:T(8,128)S(1)}, f32[18,8,256]{2,1,0:T(8,128)S(1)}, f32[18,8,256]{2,1,0:T(8,128)S(1)}) custom-call(f32[102,8,256]{2,1,0:T(8,128)S(1)} %get-tuple-element.27.refs_0_, f32[24,8,256]{2,1,0:T(8,128)S(1)} %collective-permute-done.refs_1_, ...), custom_call_target="tpu_custom_call" | custom-call | flops 40000000 | bytes 4194304 | tf_op jit(solution)/shard_map/pallas_call | solution.py:384
  15.4 0.7 collective-permute-start.5
  17.5 1.8 %shard_map.81 = (f32[16,8,256]{2,1,0:T(8,128)S(1)}, f32[48,8,256]{2,1,0:T(8,128)S(1)}, f32[48,8,256]{2,1,0:T(8,128)S(1)}, f32[18,8,256]{2,1,0:T(8,128)S(1)}, f32[18,8,256]{2,1,0:T(8,128)S(1)}) custom-call(f32[102,8,256]{2,1,0:T(8,128)S(1)} %get-tuple-element.27.refs_0_, f32[24,8,256]{2,1,0:T(8,128)S(1)} %collective-permute-done.refs_1_, ...), custom_call_target="tpu_custom_call" | custom-call | flops 40000000 | bytes 4194304 | tf_op jit(solution)/shard_map/pallas_call | solution.py:384
  19.3 1.3 %collective-permute-start.8 = (f32[48,8,256]{2,1,0:T(8,128)S(1)}, f32[48,8,256]{2,1,0:T(8,128)S(1)}, u32[]{:S(2)}, u32[]{:S(2)}) collective-permute-start(f32[48,8,256]{2,1,0:T(8,128)S(1)} %get-tuple-element.43), channel_id=1, source_target_pairs={{4,0},{5,1},{6,2},{7,3},{20,16},{21,17},{22,18},{23,19}} | collective-permute-start | bytes 1179656 | tf_op jit(solution)/shard_map/ppermute | solution.py:375
  22.6 1.3 %collective-permute-start.10 = (f32[18,8,256]{2,1,0:T(8,128)S(1)}, f32[18,8,256]{2,1,0:T(8,128)S(1)}, u32[]{:S(2)}, u32[]{:S(2)}) collective-permute-start(f32[18,8,256]{2,1,0:T(8,128)S(1)} %get-tuple-element.45), channel_id=1, source_target_pairs={{5,0},{6,1},{7,2},{21,16},{22,17},{23,18}} | collective-permute-start | bytes 442376 | tf_op jit(solution)/shard_map/ppermute | solution.py:375
  24.0 42.3 %collective-permute-done.10.refs_8_ = f32[18,8,256]{2,1,0:T(8,128)S(1)} collective-permute-done((f32[18,8,256]{2,1,0:T(8,128)S(1)}, f32[18,8,256]{2,1,0:T(8,128)S(1)}, u32[]{:S(2)}, u32[]{:S(2)}) %collective-permute-start.10) | collective-permute-done | bytes 147488 | tf_op jit(solution)/shard_map/ppermute | solution.py:375
  66.3 1.8 %shard_map.82 = (f32[16,8,256]{2,1,0:T(8,128)S(1)}, f32[48,8,256]{2,1,0:T(8,128)S(1)}) custom-call(f32[102,8,256]{2,1,0:T(8,128)S(1)} %get-tuple-element.27.refs_0_, f32[24,8,256]{2,1,0:T(8,128)S(1)} %collective-permute-done.refs_1_, f32[24,8,256]{2,1,0:T(8,128)S(1)} %collective-permute-done.1.refs_2_, f32[48,8,256]{2,1,0:T(8,128)S(1)} %get-tuple-element.30.refs_3_, ...), custom_call_target="tpu_custom_call" | custom-call | flops 40000000 | bytes 4194304 | tf_op jit(solution)/shard_map/pallas_call | solution.py:384
  68.1 1.9 %collective-permute-start.15 = (f32[16,8,256]{2,1,0:T(8,128)S(1)}, f32[16,8,256]{2,1,0:T(8,128)S(1)}, u32[]{:S(2)}, u32[]{:S(2)}) collective-permute-start(f32[16,8,256]{2,1,0:T(8,128)S(1)} %get-tuple-element.49), channel_id=1, source_target_pairs={{0,4},{1,5},{2,6},{3,7},{4,0},{5,1},{6,2},{7,3},{16,20},{17,21},{1... | collective-permute-start | bytes 393224 | tf_op jit(solution)/shard_map/ppermute | solution.py:412
  70.0 1.3 %collective-permute-start.14 = (f32[16,8,256]{2,1,0:T(8,128)S(1)}, f32[16,8,256]{2,1,0:T(8,128)S(1)}, u32[]{:S(2)}, u32[]{:S(2)}) collective-permute-start(f32[16,8,256]{2,1,0:T(8,128)S(1)} %get-tuple-element.49), channel_id=1, source_target_pairs={{0,8},{1,9},{2,10},{3,11},{16,24},{17,25},{18,26},{19,27}} | collective-permute-start | bytes 393224 | tf_op jit(solution)/shard_map/ppermute | solution.py:375
  71.3 1.3 %collective-permute-start.13 = (f32[16,8,256]{2,1,0:T(8,128)S(1)}, f32[16,8,256]{2,1,0:T(8,128)S(1)}, u32[]{:S(2)}, u32[]{:S(2)}) collective-permute-start(f32[16,8,256]{2,1,0:T(8,128)S(1)} %get-tuple-element.49), channel_id=1, source_target_pairs={{0,12},{1,13},{2,14},{3,15},{16,28},{17,29},{18,30},{19,31}} | collective-permute-start | bytes 393224 | tf_op jit(solution)/shard_map/ppermute | solution.py:375
  72.6 0.8 %shard_map.83 = f32[384,256]{1,0:T(8,128)} custom-call(f32[48,8,256]{2,1,0:T(8,128)S(1)} %get-tuple-element.48.lines_ref), custom_call_target="tpu_custom_call" | custom-call | bytes 4194304 | tf_op jit(solution)/shard_map/pallas_call | solution.py:413
  73.4 1.5 %collective-permute-done.15 = f32[16,8,256]{2,1,0:T(8,128)S(1)} collective-permute-done((f32[16,8,256]{2,1,0:T(8,128)S(1)}, f32[16,8,256]{2,1,0:T(8,128)S(1)}, u32[]{:S(2)}, u32[]{:S(2)}) %collective-permute-start.15) | collective-permute-done | bytes 131104 | tf_op jit(solution)/shard_map/ppermute | solution.py:412
  74.9 1.8 %collective-permute-done.14 = f32[16,8,256]{2,1,0:T(8,128)S(1)} collective-permute-done((f32[16,8,256]{2,1,0:T(8,128)S(1)}, f32[16,8,256]{2,1,0:T(8,128)S(1)}, u32[]{:S(2)}, u32[]{:S(2)}) %collective-permute-start.14) | collective-permute-done | bytes 131104 | tf_op jit(solution)/shard_map/ppermute | solution.py:375
  76.7 1.4 %collective-permute-done.13 = f32[16,8,256]{2,1,0:T(8,128)S(1)} collective-permute-done((f32[16,8,256]{2,1,0:T(8,128)S(1)}, f32[16,8,256]{2,1,0:T(8,128)S(1)}, u32[]{:S(2)}, u32[]{:S(2)}) %collective-permute-start.13) | collective-permute-done | bytes 131104 | tf_op jit(solution)/shard_map/ppermute | solution.py:375
  78.2 0.7 shard_map.84
  (24 shorter events, 3.5 us)
Async XLA Ops:
  0.6 5.1 %copy-start = (f32[1,2,3,8,16,256]{5,4,3,2,1,0:T(8,128)S(1)}, f32[1,2,3,8,16,256]{5,4,3,2,1,0:T(8,128)}, u32[]{:S(2)}) copy-start(f32[1,2,3,8,16,256]{5,4,3,2,1,0:T(8,128)} %param.6) | copy-start | bytes 2359300
  2.0 3.7 %copy-start.1 = (f32[8,8]{1,0:T(8,128)S(1)}, f32[8,8]{1,0:T(8,128)}, u32[]{:S(2)}) copy-start(f32[8,8]{1,0:T(8,128)} %coupling_ref.1) | copy-start | bytes 772
  2.0 4.5 %collective-permute-start = (f32[24,8,256]{2,1,0:T(8,128)S(1)}, f32[24,8,256]{2,1,0:T(8,128)S(1)}, u32[]{:S(2)}, u32[]{:S(2)}) collective-permute-start(f32[24,8,256]{2,1,0:T(8,128)S(1)} %get-tuple-element.28), channel_id=1, source_target_pairs={{0,1},{1,2},{2,3},{4,5},{5,6},{6,7},{8,9},{9,10},{10,11},{12,13},{... | collective-permute-start | bytes 589832 | tf_op jit(solution)/shard_map/ppermute | solution.py:356
  4.4 1.3 %copy-start.2 = (f32[8]{0:T(128)S(1)}, f32[8]{0:T(128)}, u32[]{:S(2)}) copy-start(f32[8]{0:T(128)} %damping_ref.1) | copy-start | bytes 100
  4.4 5.5 %collective-permute-start.1 = (f32[24,8,256]{2,1,0:T(8,128)S(1)}, f32[24,8,256]{2,1,0:T(8,128)S(1)}, u32[]{:S(2)}, u32[]{:S(2)}) collective-permute-start(f32[24,8,256]{2,1,0:T(8,128)S(1)} %get-tuple-element.29), channel_id=1, source_target_pairs={{1,0},{2,1},{3,2},{5,4},{6,5},{7,6},{9,8},{10,9},{11,10},{13,12},{... | collective-permute-start | bytes 589832 | tf_op jit(solution)/shard_map/ppermute | solution.py:357
  11.5 2.1 %collective-permute-start.2 = (f32[48,8,256]{2,1,0:T(8,128)S(1)}, f32[48,8,256]{2,1,0:T(8,128)S(1)}, u32[]{:S(2)}, u32[]{:S(2)}) collective-permute-start(f32[48,8,256]{2,1,0:T(8,128)S(1)} %get-tuple-element.33), channel_id=1, source_target_pairs={{12,8},{13,9},{14,10},{15,11},{28,24},{29,25},{30,26},{31,27}} | collective-permute-start | bytes 1179656 | tf_op jit(solution)/shard_map/ppermute | solution.py:375
  12.2 1.4 %collective-permute-start.3 = (f32[18,8,256]{2,1,0:T(8,128)S(1)}, f32[18,8,256]{2,1,0:T(8,128)S(1)}, u32[]{:S(2)}, u32[]{:S(2)}) collective-permute-start(f32[18,8,256]{2,1,0:T(8,128)S(1)} %get-tuple-element.34), channel_id=1, source_target_pairs={{12,9},{13,10},{14,11},{28,25},{29,26},{30,27}} | collective-permute-start | bytes 442376 | tf_op jit(solution)/shard_map/ppermute | solution.py:375
  12.9 0.7 collective-permute-start.4
  15.4 2.1 %collective-permute-start.5 = (f32[48,8,256]{2,1,0:T(8,128)S(1)}, f32[48,8,256]{2,1,0:T(8,128)S(1)}, u32[]{:S(2)}, u32[]{:S(2)}) collective-permute-start(f32[48,8,256]{2,1,0:T(8,128)S(1)} %get-tuple-element.38), channel_id=1, source_target_pairs={{8,4},{9,5},{10,6},{11,7},{24,20},{25,21},{26,22},{27,23}} | collective-permute-start | bytes 1179656 | tf_op jit(solution)/shard_map/ppermute | solution.py:375
  16.1 1.4 %collective-permute-start.6 = (f32[18,8,256]{2,1,0:T(8,128)S(1)}, f32[18,8,256]{2,1,0:T(8,128)S(1)}, u32[]{:S(2)}, u32[]{:S(2)}) collective-permute-start(f32[18,8,256]{2,1,0:T(8,128)S(1)} %get-tuple-element.39), channel_id=1, source_target_pairs={{8,5},{9,6},{10,7},{24,21},{25,22},{26,23}} | collective-permute-start | bytes 442376 | tf_op jit(solution)/shard_map/ppermute | solution.py:375
  16.8 0.7 collective-permute-start.7
  19.3 47.0 %collective-permute-start.8 = (f32[48,8,256]{2,1,0:T(8,128)S(1)}, f32[48,8,256]{2,1,0:T(8,128)S(1)}, u32[]{:S(2)}, u32[]{:S(2)}) collective-permute-start(f32[48,8,256]{2,1,0:T(8,128)S(1)} %get-tuple-element.43), channel_id=1, source_target_pairs={{4,0},{5,1},{6,2},{7,3},{20,16},{21,17},{22,18},{23,19}} | collective-permute-start | bytes 1179656 | tf_op jit(solution)/shard_map/ppermute | solution.py:375
  20.6 3.3 %collective-permute-start.12 = (f32[16,8,256]{2,1,0:T(8,128)S(1)}, f32[16,8,256]{2,1,0:T(8,128)S(1)}, u32[]{:S(2)}, u32[]{:S(2)}) collective-permute-start(f32[16,8,256]{2,1,0:T(8,128)S(1)} %get-tuple-element.47), channel_id=1, source_target_pairs={{4,12},{5,13},{6,14},{7,15},{8,4},{9,5},{10,6},{11,7},{12,8},{13,9... | collective-permute-start | bytes 393224 | tf_op jit(solution)/shard_map/ppermute | solution.py:406
  21.3 2.7 %collective-permute-start.11 = (f32[16,8,256]{2,1,0:T(8,128)S(1)}, f32[16,8,256]{2,1,0:T(8,128)S(1)}, u32[]{:S(2)}, u32[]{:S(2)}) collective-permute-start(f32[16,8,256]{2,1,0:T(8,128)S(1)} %get-tuple-element.47), channel_id=1, source_target_pairs={{4,8},{5,9},{6,10},{7,11},{8,12},{9,13},{10,14},{11,15},{12,4},{13... | collective-permute-start | bytes 393224 | tf_op jit(solution)/shard_map/ppermute | solution.py:406
  22.0 2.0 %collective-permute-start.9 = (f32[18,8,256]{2,1,0:T(8,128)S(1)}, f32[18,8,256]{2,1,0:T(8,128)S(1)}, u32[]{:S(2)}, u32[]{:S(2)}) collective-permute-start(f32[18,8,256]{2,1,0:T(8,128)S(1)} %get-tuple-element.44), channel_id=1, source_target_pairs={{4,1},{5,2},{6,3},{20,17},{21,18},{22,19}} | collective-permute-start | bytes 442376 | tf_op jit(solution)/shard_map/ppermute | solution.py:375
  22.6 43.7 %collective-permute-start.10 = (f32[18,8,256]{2,1,0:T(8,128)S(1)}, f32[18,8,256]{2,1,0:T(8,128)S(1)}, u32[]{:S(2)}, u32[]{:S(2)}) collective-permute-start(f32[18,8,256]{2,1,0:T(8,128)S(1)} %get-tuple-element.45), channel_id=1, source_target_pairs={{5,0},{6,1},{7,2},{21,16},{22,17},{23,18}} | collective-permute-start | bytes 442376 | tf_op jit(solution)/shard_map/ppermute | solution.py:375
  68.1 6.9 %collective-permute-start.15 = (f32[16,8,256]{2,1,0:T(8,128)S(1)}, f32[16,8,256]{2,1,0:T(8,128)S(1)}, u32[]{:S(2)}, u32[]{:S(2)}) collective-permute-start(f32[16,8,256]{2,1,0:T(8,128)S(1)} %get-tuple-element.49), channel_id=1, source_target_pairs={{0,4},{1,5},{2,6},{3,7},{4,0},{5,1},{6,2},{7,3},{16,20},{17,21},{1... | collective-permute-start | bytes 393224 | tf_op jit(solution)/shard_map/ppermute | solution.py:412
  70.0 6.7 %collective-permute-start.14 = (f32[16,8,256]{2,1,0:T(8,128)S(1)}, f32[16,8,256]{2,1,0:T(8,128)S(1)}, u32[]{:S(2)}, u32[]{:S(2)}) collective-permute-start(f32[16,8,256]{2,1,0:T(8,128)S(1)} %get-tuple-element.49), channel_id=1, source_target_pairs={{0,8},{1,9},{2,10},{3,11},{16,24},{17,25},{18,26},{19,27}} | collective-permute-start | bytes 393224 | tf_op jit(solution)/shard_map/ppermute | solution.py:375
  71.3 6.9 %collective-permute-start.13 = (f32[16,8,256]{2,1,0:T(8,128)S(1)}, f32[16,8,256]{2,1,0:T(8,128)S(1)}, u32[]{:S(2)}, u32[]{:S(2)}) collective-permute-start(f32[16,8,256]{2,1,0:T(8,128)S(1)} %get-tuple-element.49), channel_id=1, source_target_pairs={{0,12},{1,13},{2,14},{3,15},{16,28},{17,29},{18,30},{19,31}} | collective-permute-start | bytes 393224 | tf_op jit(solution)/shard_map/ppermute | solution.py:375

commit v3 on v2

--- a/solution.py
+++ b/solution.py
@@ -56,7 +56,7 @@
             ref[low : low + SUBLANES, :] = block[l]
 
 
-def pack_kernel(z, th_in, cells_in, values_in, mask_in, up_ref, down_ref, own_ref, th_ref, cells_ref, values_ref, mask_ref, sem):
+def pack_kernel(z, th_in, cells_in, values_in, mask_in, partner_ref, other_ref, own_ref, th_ref, cells_ref, values_ref, mask_ref, sem):
     copies = [
         pltpu.make_async_copy(source, target, sem.at[i])
         for i, (source, target) in enumerate(
@@ -87,21 +87,22 @@
     ocean = mask_ref[...].astype(jnp.float32) * (0.5 * STEP_DT)
     own_ref[z.steps * z.tiles :] = ocean.reshape(z.tiles, SUBLANES, z.cols)
     copies[3].wait()
+    even = lax.axis_index("lat") % 2 == 0
     for j in range(z.halo):
         lines, need = rows_first(z, th_ref, z.section(j)), z.halo - j
         for m in range(need):
-            up_ref[z.first[j] + m] = lines[m]
-            down_ref[z.first[j] + m] = lines[z.rows - need + m]
-    for k in range(z.steps + 1):
-        for m in range(z.halo):
-            tile, line = divmod(k * z.halo + m, SUBLANES)
-            for ref, row in ((up_ref, m), (down_ref, z.rows - z.halo + m)):
-                from_tile, from_line = divmod(k * z.rows + row, SUBLANES)
-                ref[z.halo_rows + tile, line : line + 1, :] = own_ref[from_tile, from_line : from_line + 1, :]
-    for q in range((z.steps + 1) * z.halo, z.tail * SUBLANES):
+            head, foot = lines[m], lines[z.rows - need + m]
+            partner_ref[z.first[j] + m] = jnp.where(even, foot, head)
+            other_ref[z.first[j] + m] = jnp.where(even, head, foot)
+    for q in range(z.tail * SUBLANES):
         tile, line = divmod(q, SUBLANES)
-        for ref in (up_ref, down_ref):
-            ref[z.halo_rows + tile, line : line + 1, :] = jnp.zeros((1, z.cols), jnp.float32)
+        k, m = divmod(q, z.halo)
+        head = foot = jnp.zeros((1, z.cols), jnp.float32)
+        if k <= z.steps:
+            places = (divmod(k * z.rows + row, SUBLANES) for row in (m, z.rows - z.halo + m))
+            head, foot = (own_ref[t, at : at + 1, :] for t, at in places)
+        partner_ref[z.halo_rows + tile, line : line + 1, :] = jnp.where(even, foot, head)
+        other_ref[z.halo_rows + tile, line : line + 1, :] = jnp.where(even, head, foot)
 
 
 def own_kernel(z, coupling_ref, damping_ref, th_ref, own_ref, h_ref, oc_ref, keep_ref, mix_ref):
@@ -134,8 +135,16 @@
 
 
 def window_kernel(z, total_rows, first, last, target_win, *refs):
+    even = lax.axis_index("lat") % 2 == 0
     h_ref, above_ref, below_ref = refs[:3]
     refs = refs[3:]
+    if first:
+        partner_ref, other_ref = above_ref, below_ref
+        above_ref, below_ref = refs[3:5]
+        refs = refs[:3] + refs[5:]
+        for m in range(z.packed):
+            above_ref[m] = jnp.where(even, other_ref[m], partner_ref[m])
+            below_ref[m] = jnp.where(even, partner_ref[m], other_ref[m])
     own_ref = h_ref.at[pl.ds(z.halo * z.rows, (z.steps + 1) * z.tiles)]
     oc_ref, keep_ref, mix_ref = refs[:3]
     state, refs = refs[3 : 3 if first else 6], refs[3 if first else 6 :]
@@ -145,7 +154,7 @@
     if last:
         (bias_ref, lam_ref), refs = refs[:2], refs[2:]
     else:
-        (bias_ref, lam_ref, main_ref, top_ref, bottom_ref), refs = refs[:5], refs[5:]
+        (bias_ref, lam_ref, main_ref, partner_out, other_out), refs = refs[:5], refs[5:]
     x_ref, y_ref, w_ref, sum_ref, oc_out, keep_out = refs
     halo, ext, rows, layers = z.halo, z.ext, z.rows, z.layers
     first_row = lax.axis_index("lat") * rows - halo
@@ -181,11 +190,12 @@
         return each(lambda u, v: u + v, x, y)
 
     def incoming(c, e):
-        main_in, above_in, below_in = state
-        if e < halo:
-            return read(above_in, c * halo + e)
-        if e >= halo + rows:
-            return read(below_in, c * halo + e - halo - rows)
+        main_in, partner_in, other_in = state
+        if not halo <= e < halo + rows:
+            m = c * halo + (e if e < halo else e - halo - rows)
+            pair, rest = read(partner_in, m), read(other_in, m)
+            swap = even if e < halo else jnp.logical_not(even)
+            return each(lambda u, v: jnp.where(swap, v, u), pair, rest)
         return read(main_in, c * rows + e - halo)
 
     def east(values):
@@ -303,8 +313,9 @@
     if not last:
         for c in range(3):
             for m in range(halo):
-                top_ref[c * halo + m] = main_ref[c * rows + m]
-                bottom_ref[c * halo + m] = main_ref[c * rows + rows - halo + m]
+                head, foot = main_ref[c * rows + m], main_ref[c * rows + rows - halo + m]
+                partner_out[c * halo + m] = jnp.where(even, foot, head)
+                other_out[c * halo + m] = jnp.where(even, head, foot)
 
 
 def turn_kernel(z, count, lines_ref, out_ref):
@@ -338,7 +349,7 @@
     cube = (layers, cols)
     count = obs_cells.shape[2]
 
-    to_above, to_below, own = call(
+    to_partner, to_other, own = call(
         functools.partial(pack_kernel, z),
         [(z.packed,) + cube, (z.packed,) + cube, ((steps + 1) * z.tiles,) + cube],
         [HBM] * 4,
@@ -351,10 +362,8 @@
         ],
         limit=60 << 20,
     )(flat, obs_cells[0], obs_values[0], ocean_mask)
-    southward = [(i, i + 1) for i in range(n_lat - 1)]
-    northward = [(i + 1, i) for i in range(n_lat - 1)]
-    above = lax.ppermute(to_below, "lat", southward)
-    below = lax.ppermute(to_above, "lat", northward)
+    pairs, rests = ([(i + d, i + 1 - d) for i in range(k, n_lat - 1, 2) for d in range(2)] for k in range(2))
+    near = (lax.ppermute(to_partner, "lat", pairs), lax.ppermute(to_other, "lat", rests))
     h, *tables = call(
         functools.partial(own_kernel, z),
         [
@@ -366,47 +375,44 @@
         [SMEM, SMEM, VMEM, VMEM],
     )(coupling, damping, flat, own)
 
-    def relay(value, source_win, target_win, shift=0):
-        pairs = [
-            (source_win * n_lat + i, target_win * n_lat + i + shift)
-            for i in range(n_lat)
-            if 0 <= i + shift < n_lat
-        ]
-        return lax.ppermute(value, ("win", "lat"), pairs)
-
-    fields = (h, above, below, *tables)
+    straight = [(i, i) for i in range(n_lat)]
+
+    def relay(value, source_win, target_win, among=straight):
+        moves = [(source_win * n_lat + i, target_win * n_lat + j) for i, j in among]
+        return lax.ppermute(value, ("win", "lat"), moves)
+
     one, state_rows, halo_rows = ((n,) + cube for n in (rows, 3 * rows, 3 * z.halo))
 
-    def window(target_win, state, results):
-        last = target_win == 0
+    def window(target_win, fields, state, results):
+        first, last = target_win == n_win - 1, target_win == 0
         outs = [one, state_rows] if last else [one, state_rows, state_rows, halo_rows, halo_rows]
-        operands = fields + state + results
+        operands = fields + tuple(tables) + state + results
         return call(
-            functools.partial(window_kernel, z, n_lat * rows, not state, last, target_win),
-            outs,
+            functools.partial(window_kernel, z, n_lat * rows, first, last, target_win),
+            ([(z.packed,) + cube] * 2 if first else []) + outs,
             [VMEM] * len(operands),
             window_scratch(z),
             cost=40_000_000,
         )(*operands)
 
-    bias, lam, main, top, bottom = window(n_win - 1, (), ())
+    above, below, bias, lam, main, partner, other = window(n_win - 1, (h,) + near, (), ())
+    fields = (h, above, below)
     for source_win in range(n_win - 1, 0, -1):
         state = (
             relay(main, source_win, source_win - 1),
-            relay(bottom, source_win, source_win - 1, 1),
-            relay(top, source_win, source_win - 1, -1),
+            relay(partner, source_win, source_win - 1, pairs),
+            relay(other, source_win, source_win - 1, rests),
         )
         if source_win > 1:
-            bias, lam, main, top, bottom = window(source_win - 1, state, (lam, bias))
+            bias, lam, main, partner, other = window(source_win - 1, fields, state, (lam, bias))
     others = n_win - 1
+    total = bias
     for shift in range(1, others):
-        pairs = [
+        moves = [
             ((1 + w) * n_lat + i, (1 + (w + shift) % others) * n_lat + i) for w in range(others) for i in range(n_lat)
         ]
-        part = lax.ppermute(bias, ("win", "lat"), pairs)
-        total = part if shift == 1 else total + part
-    total = bias if others == 1 else bias + total
-    mine, lam = window(0, state, (lam, total))
+        total = total + lax.ppermute(bias, ("win", "lat"), moves)
+    mine, lam = window(0, fields, state, (lam, total))
     swap = [(a * n_lat + i, (1 - a) * n_lat + i) for a in range(2) for i in range(n_lat)]
     result = mine + sum(relay(mine, 0, target_win) for target_win in range(n_win - 1, 1, -1))
     result = result + lax.ppermute(mine, ("win", "lat"), swap)

time: 79.3 us -> 74.3 us (0.937)
  the two profiles are of different devices: /device:TPU:0 before, /device:TPU:1 now
where the time goes in v3:
time: 74.3 us; the launch traced here: 73.9 us
  waiting for transfers between devices  43.7 us (59%)
  starting transfers between devices  18.4 us (25%)
  Pallas kernels  10.7 us (14%)
  between operations  0.92 us (1%)
    ppermute x11, waiting for transfers between devices, relay(): return lax.ppermute(value, ('win', 'lat'), moves)  39.8 us
    ppermute x11, starting transfers between devices, relay(): return lax.ppermute(value, ('win', 'lat'), moves)  10.5 us
    pallas_call x4, Pallas kernels, window(): call(functools.partial(window_kernel, z, n_lat * rows, first, last, targe...  7.04 us
    ppermute x1, starting transfers between devices, per_device(): lax.ppermute(to_other, 'lat', rests)  4.5 us
    ppermute x1, waiting for transfers between devices, per_device(): lax.ppermute(to_other, 'lat', rests)  2.49 us
    ppermute x1, starting transfers between devices, per_device(): result = result + lax.ppermute(mine, ('win', 'lat'), swap)  1.92 us
  transfers between devices with their start and end apart: 16, of which 6 were waited for; matrix products, arithmetic and copies ran while one was open for 0% of the time, Pallas kernels for 2%

profile of v3, /device:TPU:1, one launch (start us, length us, event | category | flops | bytes accessed | tf_op | source)
XLA Modules:
  0.0 73.9 jit_solution(10214863113207119621)
XLA Ops:
  0.6 1.4 %shard_map.77 = (f32[24,8,256]{2,1,0:T(8,128)S(1)}, f32[24,8,256]{2,1,0:T(8,128)S(1)}, f32[6,8,256]{2,1,0:T(8,128)S(1)}) custom-call(f32[768,256]{1,0:T(8,128)} %bitcast.5, s32[2,256]{1,0:T(2,128)} %bitcast.9, f32[2,256]{1,0:T(2,128)} %bitcast.10, s32[16,256]{1,0:T(8,128)} %mask_in.1), custom_call_target="tpu_custom_call" | custom-call | bytes 4194304 | tf_op jit(solution)/shard_map/pallas_call | solution.py:352
  2.2 4.5 %collective-permute-start.1 = (f32[24,8,256]{2,1,0:T(8,128)S(1)}, f32[24,8,256]{2,1,0:T(8,128)S(1)}, u32[]{:S(2)}, u32[]{:S(2)}) collective-permute-start(f32[24,8,256]{2,1,0:T(8,128)S(1)} %get-tuple-element.31), channel_id=1, source_target_pairs={{1,2},{2,1},{5,6},{6,5},{9,10},{10,9},{13,14},{14,13},{17,18},{18,... | collective-permute-start | bytes 589832 | tf_op jit(solution)/shard_map/ppermute | solution.py:366
  6.7 0.8 %shard_map.78 = (f32[102,8,256]{2,1,0:T(8,128)S(1)}, f32[48,8,256]{2,1,0:T(8,128)S(1)}, f32[48,8,256]{2,1,0:T(8,128)S(1)}, f32[72,128]{1,0:T(8,128)S(1)}) custom-call(f32[8,8]{1,0:T(8,128)S(1)} %copy-done.1, f32[8]{0:T(128)S(1)} %copy-done.2, f32[768,256]{1,0:T(8,128)S(1)} %bitcast.6, f32[6,8,256]{2,1,0:T(8,128)S(1)} %get-tuple-element.28.own_ref), custom_call_target="tpu_custom_call" | custom-call | bytes 4194304 | tf_op jit(solution)/shard_map/pallas_call | solution.py:367
  7.5 2.5 %collective-permute-done.1.refs_2_ = f32[24,8,256]{2,1,0:T(8,128)S(1)} collective-permute-done((f32[24,8,256]{2,1,0:T(8,128)S(1)}, f32[24,8,256]{2,1,0:T(8,128)S(1)}, u32[]{:S(2)}, u32[]{:S(2)}) %collective-permute-start.1) | collective-permute-done | bytes 196640 | tf_op jit(solution)/shard_map/ppermute | solution.py:366
  10.0 1.7 %shard_map.79 = (f32[24,8,256]{2,1,0:T(8,128)S(1)}, f32[24,8,256]{2,1,0:T(8,128)S(1)}, f32[16,8,256]{2,1,0:T(8,128)S(1)}, f32[48,8,256]{2,1,0:T(8,128)S(1)}, f32...) custom-call(f32[102,8,256]{2,1,0:T(8,128)S(1)} %get-tuple-element.29.refs_0_, ...), custom_call_target="tpu_custom_call" | custom-call | flops 40000000 | bytes 4194304 | tf_op jit(solution)/shard_map/pallas_call | solution.py:390
  11.7 0.7 collective-permute-start.2
  12.4 0.7 collective-permute-start.3
  13.8 1.8 %shard_map.80 = (f32[16,8,256]{2,1,0:T(8,128)S(1)}, f32[48,8,256]{2,1,0:T(8,128)S(1)}, f32[48,8,256]{2,1,0:T(8,128)S(1)}, f32[18,8,256]{2,1,0:T(8,128)S(1)}, f32[18,8,256]{2,1,0:T(8,128)S(1)}) custom-call(f32[102,8,256]{2,1,0:T(8,128)S(1)} %get-tuple-element.29.refs_0_, f32[24,8,256]{2,1,0:T(8,128)S(1)} %get-tuple-element.35.refs_1_, ...), custom_call_target="tpu_custom_call" | custom-call | flops 40000000 | bytes 4194304 | tf_op jit(solution)/shard_map/pallas_call | solution.py:390
  15.6 0.7 collective-permute-start.5
  17.7 1.8 %shard_map.81 = (f32[16,8,256]{2,1,0:T(8,128)S(1)}, f32[48,8,256]{2,1,0:T(8,128)S(1)}, f32[48,8,256]{2,1,0:T(8,128)S(1)}, f32[18,8,256]{2,1,0:T(8,128)S(1)}, f32[18,8,256]{2,1,0:T(8,128)S(1)}) custom-call(f32[102,8,256]{2,1,0:T(8,128)S(1)} %get-tuple-element.29.refs_0_, f32[24,8,256]{2,1,0:T(8,128)S(1)} %get-tuple-element.35.refs_1_, ...), custom_call_target="tpu_custom_call" | custom-call | flops 40000000 | bytes 4194304 | tf_op jit(solution)/shard_map/pallas_call | solution.py:390
  19.5 1.3 %collective-permute-start.8 = (f32[48,8,256]{2,1,0:T(8,128)S(1)}, f32[48,8,256]{2,1,0:T(8,128)S(1)}, u32[]{:S(2)}, u32[]{:S(2)}) collective-permute-start(f32[48,8,256]{2,1,0:T(8,128)S(1)} %get-tuple-element.47), channel_id=1, source_target_pairs={{4,0},{5,1},{6,2},{7,3},{20,16},{21,17},{22,18},{23,19}} | collective-permute-start | bytes 1179656 | tf_op jit(solution)/shard_map/ppermute | solution.py:382
  22.1 1.3 %collective-permute-start.9 = (f32[18,8,256]{2,1,0:T(8,128)S(1)}, f32[18,8,256]{2,1,0:T(8,128)S(1)}, u32[]{:S(2)}, u32[]{:S(2)}) collective-permute-start(f32[18,8,256]{2,1,0:T(8,128)S(1)} %get-tuple-element.48), channel_id=1, source_target_pairs={{4,1},{5,0},{6,3},{7,2},{20,17},{21,16},{22,19},{23,18}} | collective-permute-start | bytes 442376 | tf_op jit(solution)/shard_map/ppermute | solution.py:382
  23.4 1.3 %collective-permute-start.10 = (f32[18,8,256]{2,1,0:T(8,128)S(1)}, f32[18,8,256]{2,1,0:T(8,128)S(1)}, u32[]{:S(2)}, u32[]{:S(2)}) collective-permute-start(f32[18,8,256]{2,1,0:T(8,128)S(1)} %get-tuple-element.49), channel_id=1, source_target_pairs={{5,2},{6,1},{21,18},{22,17}} | collective-permute-start | bytes 442376 | tf_op jit(solution)/shard_map/ppermute | solution.py:382
  24.8 34.0 %collective-permute-done.9.refs_7_ = f32[18,8,256]{2,1,0:T(8,128)S(1)} collective-permute-done((f32[18,8,256]{2,1,0:T(8,128)S(1)}, f32[18,8,256]{2,1,0:T(8,128)S(1)}, u32[]{:S(2)}, u32[]{:S(2)}) %collective-permute-start.9) | collective-permute-done | bytes 147488 | tf_op jit(solution)/shard_map/ppermute | solution.py:382
  58.8 2.3 %collective-permute-done.10.refs_8_ = f32[18,8,256]{2,1,0:T(8,128)S(1)} collective-permute-done((f32[18,8,256]{2,1,0:T(8,128)S(1)}, f32[18,8,256]{2,1,0:T(8,128)S(1)}, u32[]{:S(2)}, u32[]{:S(2)}) %collective-permute-start.10) | collective-permute-done | bytes 147488 | tf_op jit(solution)/shard_map/ppermute | solution.py:382
  61.1 1.8 %shard_map.82 = (f32[16,8,256]{2,1,0:T(8,128)S(1)}, f32[48,8,256]{2,1,0:T(8,128)S(1)}) custom-call(f32[102,8,256]{2,1,0:T(8,128)S(1)} %get-tuple-element.29.refs_0_, f32[24,8,256]{2,1,0:T(8,128)S(1)} %get-tuple-element.35.refs_1_, f32[24,8,256]{2,1,0:T(8,128)S(1)} %get-tuple-element.36.refs_2_, f32[48,8,256]{2,1,0:T(8,128)S(1)} %get-tuple-element.32.refs_3_, ...), custom_call_target="tpu_custom_call" | custom-call | flops 40000000 | bytes 4194304 | tf_op jit(solution)/shard_map/pallas_call | solution.py:390
  62.9 1.9 %collective-permute-start.15 = (f32[16,8,256]{2,1,0:T(8,128)S(1)}, f32[16,8,256]{2,1,0:T(8,128)S(1)}, u32[]{:S(2)}, u32[]{:S(2)}) collective-permute-start(f32[16,8,256]{2,1,0:T(8,128)S(1)} %get-tuple-element.53), channel_id=1, source_target_pairs={{0,4},{1,5},{2,6},{3,7},{4,0},{5,1},{6,2},{7,3},{16,20},{17,21},{1... | collective-permute-start | bytes 393224 | tf_op jit(solution)/shard_map/ppermute | solution.py:418
  64.8 1.3 %collective-permute-start.14 = (f32[16,8,256]{2,1,0:T(8,128)S(1)}, f32[16,8,256]{2,1,0:T(8,128)S(1)}, u32[]{:S(2)}, u32[]{:S(2)}) collective-permute-start(f32[16,8,256]{2,1,0:T(8,128)S(1)} %get-tuple-element.53), channel_id=1, source_target_pairs={{0,8},{1,9},{2,10},{3,11},{16,24},{17,25},{18,26},{19,27}} | collective-permute-start | bytes 393224 | tf_op jit(solution)/shard_map/ppermute | solution.py:382
  66.1 1.3 %collective-permute-start.13 = (f32[16,8,256]{2,1,0:T(8,128)S(1)}, f32[16,8,256]{2,1,0:T(8,128)S(1)}, u32[]{:S(2)}, u32[]{:S(2)}) collective-permute-start(f32[16,8,256]{2,1,0:T(8,128)S(1)} %get-tuple-element.53), channel_id=1, source_target_pairs={{0,12},{1,13},{2,14},{3,15},{16,28},{17,29},{18,30},{19,31}} | collective-permute-start | bytes 393224 | tf_op jit(solution)/shard_map/ppermute | solution.py:382
  67.4 0.8 %shard_map.83 = f32[384,256]{1,0:T(8,128)} custom-call(f32[48,8,256]{2,1,0:T(8,128)S(1)} %get-tuple-element.52.lines_ref), custom_call_target="tpu_custom_call" | custom-call | bytes 4194304 | tf_op jit(solution)/shard_map/pallas_call | solution.py:419
  68.3 1.5 %collective-permute-done.15 = f32[16,8,256]{2,1,0:T(8,128)S(1)} collective-permute-done((f32[16,8,256]{2,1,0:T(8,128)S(1)}, f32[16,8,256]{2,1,0:T(8,128)S(1)}, u32[]{:S(2)}, u32[]{:S(2)}) %collective-permute-start.15) | collective-permute-done | bytes 131104 | tf_op jit(solution)/shard_map/ppermute | solution.py:418
  69.7 1.2 %collective-permute-done.14 = f32[16,8,256]{2,1,0:T(8,128)S(1)} collective-permute-done((f32[16,8,256]{2,1,0:T(8,128)S(1)}, f32[16,8,256]{2,1,0:T(8,128)S(1)}, u32[]{:S(2)}, u32[]{:S(2)}) %collective-permute-start.14) | collective-permute-done | bytes 131104 | tf_op jit(solution)/shard_map/ppermute | solution.py:382
  70.9 2.3 %collective-permute-done.13 = f32[16,8,256]{2,1,0:T(8,128)S(1)} collective-permute-done((f32[16,8,256]{2,1,0:T(8,128)S(1)}, f32[16,8,256]{2,1,0:T(8,128)S(1)}, u32[]{:S(2)}, u32[]{:S(2)}) %collective-permute-start.13) | collective-permute-done | bytes 131104 | tf_op jit(solution)/shard_map/ppermute | solution.py:382
  73.2 0.7 shard_map.84
  (24 shorter events, 3.6 us)
Async XLA Ops:
  0.6 6.1 %copy-start = (f32[1,2,3,8,16,256]{5,4,3,2,1,0:T(8,128)S(1)}, f32[1,2,3,8,16,256]{5,4,3,2,1,0:T(8,128)}, u32[]{:S(2)}) copy-start(f32[1,2,3,8,16,256]{5,4,3,2,1,0:T(8,128)} %param.6) | copy-start | bytes 2359300
  2.0 4.7 %copy-start.1 = (f32[8,8]{1,0:T(8,128)S(1)}, f32[8,8]{1,0:T(8,128)}, u32[]{:S(2)}) copy-start(f32[8,8]{1,0:T(8,128)} %coupling_ref.1) | copy-start | bytes 772
  2.1 5.5 %collective-permute-start = (f32[24,8,256]{2,1,0:T(8,128)S(1)}, f32[24,8,256]{2,1,0:T(8,128)S(1)}, u32[]{:S(2)}, u32[]{:S(2)}) collective-permute-start(f32[24,8,256]{2,1,0:T(8,128)S(1)} %get-tuple-element.30), channel_id=1, source_target_pairs={{0,1},{1,0},{2,3},{3,2},{4,5},{5,4},{6,7},{7,6},{8,9},{9,8},{10,11... | collective-permute-start | bytes 589832 | tf_op jit(solution)/shard_map/ppermute | solution.py:366
  2.2 4.5 %copy-start.2 = (f32[8]{0:T(128)S(1)}, f32[8]{0:T(128)}, u32[]{:S(2)}) copy-start(f32[8]{0:T(128)} %damping_ref.1) | copy-start | bytes 100
  2.2 7.9 %collective-permute-start.1 = (f32[24,8,256]{2,1,0:T(8,128)S(1)}, f32[24,8,256]{2,1,0:T(8,128)S(1)}, u32[]{:S(2)}, u32[]{:S(2)}) collective-permute-start(f32[24,8,256]{2,1,0:T(8,128)S(1)} %get-tuple-element.31), channel_id=1, source_target_pairs={{1,2},{2,1},{5,6},{6,5},{9,10},{10,9},{13,14},{14,13},{17,18},{18,... | collective-permute-start | bytes 589832 | tf_op jit(solution)/shard_map/ppermute | solution.py:366
  11.7 2.1 %collective-permute-start.2 = (f32[48,8,256]{2,1,0:T(8,128)S(1)}, f32[48,8,256]{2,1,0:T(8,128)S(1)}, u32[]{:S(2)}, u32[]{:S(2)}) collective-permute-start(f32[48,8,256]{2,1,0:T(8,128)S(1)} %get-tuple-element.37), channel_id=1, source_target_pairs={{12,8},{13,9},{14,10},{15,11},{28,24},{29,25},{30,26},{31,27}} | collective-permute-start | bytes 1179656 | tf_op jit(solution)/shard_map/ppermute | solution.py:382
  12.4 1.4 %collective-permute-start.3 = (f32[18,8,256]{2,1,0:T(8,128)S(1)}, f32[18,8,256]{2,1,0:T(8,128)S(1)}, u32[]{:S(2)}, u32[]{:S(2)}) collective-permute-start(f32[18,8,256]{2,1,0:T(8,128)S(1)} %get-tuple-element.38), channel_id=1, source_target_pairs={{12,9},{13,8},{14,11},{15,10},{28,25},{29,24},{30,27},{31,26}} | collective-permute-start | bytes 442376 | tf_op jit(solution)/shard_map/ppermute | solution.py:382
  13.1 0.7 collective-permute-start.4
  15.6 2.1 %collective-permute-start.5 = (f32[48,8,256]{2,1,0:T(8,128)S(1)}, f32[48,8,256]{2,1,0:T(8,128)S(1)}, u32[]{:S(2)}, u32[]{:S(2)}) collective-permute-start(f32[48,8,256]{2,1,0:T(8,128)S(1)} %get-tuple-element.42), channel_id=1, source_target_pairs={{8,4},{9,5},{10,6},{11,7},{24,20},{25,21},{26,22},{27,23}} | collective-permute-start | bytes 1179656 | tf_op jit(solution)/shard_map/ppermute | solution.py:382
  16.3 1.4 %collective-permute-start.6 = (f32[18,8,256]{2,1,0:T(8,128)S(1)}, f32[18,8,256]{2,1,0:T(8,128)S(1)}, u32[]{:S(2)}, u32[]{:S(2)}) collective-permute-start(f32[18,8,256]{2,1,0:T(8,128)S(1)} %get-tuple-element.43), channel_id=1, source_target_pairs={{8,5},{9,4},{10,7},{11,6},{24,21},{25,20},{26,23},{27,22}} | collective-permute-start | bytes 442376 | tf_op jit(solution)/shard_map/ppermute | solution.py:382
  17.0 0.7 collective-permute-start.7
  19.5 41.6 %collective-permute-start.8 = (f32[48,8,256]{2,1,0:T(8,128)S(1)}, f32[48,8,256]{2,1,0:T(8,128)S(1)}, u32[]{:S(2)}, u32[]{:S(2)}) collective-permute-start(f32[48,8,256]{2,1,0:T(8,128)S(1)} %get-tuple-element.47), channel_id=1, source_target_pairs={{4,0},{5,1},{6,2},{7,3},{20,16},{21,17},{22,18},{23,19}} | collective-permute-start | bytes 1179656 | tf_op jit(solution)/shard_map/ppermute | solution.py:382
  20.8 4.0 %collective-permute-start.12 = (f32[16,8,256]{2,1,0:T(8,128)S(1)}, f32[16,8,256]{2,1,0:T(8,128)S(1)}, u32[]{:S(2)}, u32[]{:S(2)}) collective-permute-start(f32[16,8,256]{2,1,0:T(8,128)S(1)} %get-tuple-element.51), channel_id=1, source_target_pairs={{4,12},{5,13},{6,14},{7,15},{8,4},{9,5},{10,6},{11,7},{12,8},{13,9... | collective-permute-start | bytes 393224 | tf_op jit(solution)/shard_map/ppermute | solution.py:414
  21.5 3.3 %collective-permute-start.11 = (f32[16,8,256]{2,1,0:T(8,128)S(1)}, f32[16,8,256]{2,1,0:T(8,128)S(1)}, u32[]{:S(2)}, u32[]{:S(2)}) collective-permute-start(f32[16,8,256]{2,1,0:T(8,128)S(1)} %get-tuple-element.51), channel_id=1, source_target_pairs={{4,8},{5,9},{6,10},{7,11},{8,12},{9,13},{10,14},{11,15},{12,4},{13... | collective-permute-start | bytes 393224 | tf_op jit(solution)/shard_map/ppermute | solution.py:414
  22.1 36.6 %collective-permute-start.9 = (f32[18,8,256]{2,1,0:T(8,128)S(1)}, f32[18,8,256]{2,1,0:T(8,128)S(1)}, u32[]{:S(2)}, u32[]{:S(2)}) collective-permute-start(f32[18,8,256]{2,1,0:T(8,128)S(1)} %get-tuple-element.48), channel_id=1, source_target_pairs={{4,1},{5,0},{6,3},{7,2},{20,17},{21,16},{22,19},{23,18}} | collective-permute-start | bytes 442376 | tf_op jit(solution)/shard_map/ppermute | solution.py:382
  23.4 37.7 %collective-permute-start.10 = (f32[18,8,256]{2,1,0:T(8,128)S(1)}, f32[18,8,256]{2,1,0:T(8,128)S(1)}, u32[]{:S(2)}, u32[]{:S(2)}) collective-permute-start(f32[18,8,256]{2,1,0:T(8,128)S(1)} %get-tuple-element.49), channel_id=1, source_target_pairs={{5,2},{6,1},{21,18},{22,17}} | collective-permute-start | bytes 442376 | tf_op jit(solution)/shard_map/ppermute | solution.py:382
  62.9 6.8 %collective-permute-start.15 = (f32[16,8,256]{2,1,0:T(8,128)S(1)}, f32[16,8,256]{2,1,0:T(8,128)S(1)}, u32[]{:S(2)}, u32[]{:S(2)}) collective-permute-start(f32[16,8,256]{2,1,0:T(8,128)S(1)} %get-tuple-element.53), channel_id=1, source_target_pairs={{0,4},{1,5},{2,6},{3,7},{4,0},{5,1},{6,2},{7,3},{16,20},{17,21},{1... | collective-permute-start | bytes 393224 | tf_op jit(solution)/shard_map/ppermute | solution.py:418
  64.8 6.0 %collective-permute-start.14 = (f32[16,8,256]{2,1,0:T(8,128)S(1)}, f32[16,8,256]{2,1,0:T(8,128)S(1)}, u32[]{:S(2)}, u32[]{:S(2)}) collective-permute-start(f32[16,8,256]{2,1,0:T(8,128)S(1)} %get-tuple-element.53), channel_id=1, source_target_pairs={{0,8},{1,9},{2,10},{3,11},{16,24},{17,25},{18,26},{19,27}} | collective-permute-start | bytes 393224 | tf_op jit(solution)/shard_map/ppermute | solution.py:382
  66.1 7.0 %collective-permute-start.13 = (f32[16,8,256]{2,1,0:T(8,128)S(1)}, f32[16,8,256]{2,1,0:T(8,128)S(1)}, u32[]{:S(2)}, u32[]{:S(2)}) collective-permute-start(f32[16,8,256]{2,1,0:T(8,128)S(1)} %get-tuple-element.53), channel_id=1, source_target_pairs={{0,12},{1,13},{2,14},{3,15},{16,28},{17,29},{18,30},{19,31}} | collective-permute-start | bytes 393224 | tf_op jit(solution)/shard_map/ppermute | solution.py:382

commit v4 on v3

--- a/solution.py
+++ b/solution.py
@@ -150,11 +150,14 @@
     state, refs = refs[3 : 3 if first else 6], refs[3 if first else 6 :]
     if not first:
         lam_in, bias_in, refs = refs[0], refs[1], refs[2:]
+        added, refs = (refs[:-8], refs[-8:]) if last else ((), refs)
         mine = lax.axis_index("win") == target_win
     if last:
         (bias_ref, lam_ref), refs = refs[:2], refs[2:]
     else:
-        (bias_ref, lam_ref, main_ref, partner_out, other_out), refs = refs[:5], refs[5:]
+        (bias_ref, lam_ref, main_ref, other_out), refs = refs[:4], refs[4:]
+        if target_win == 1:
+            partner_out, refs = refs[0], refs[1:]
     x_ref, y_ref, w_ref, sum_ref, oc_out, keep_out = refs
     halo, ext, rows, layers = z.halo, z.ext, z.rows, z.layers
     first_row = lax.axis_index("lat") * rows - halo
@@ -280,7 +283,10 @@
                         write(sum_ref, place, part)
                     else:
                         if not first:
-                            part = each(lambda v, o: jnp.where(mine, v, o), part, read(bias_in, place))
+                            before = read(bias_in, place)
+                            for ref in added:
+                                before = add(before, read(ref, place))
+                            part = each(lambda v, o: jnp.where(mine, v, o), part, before)
                         write(bias_ref, place, part)
                     if order == z.steps - 1:
                         for c, value in enumerate((a, p, q)):
@@ -314,8 +320,9 @@
         for c in range(3):
             for m in range(halo):
                 head, foot = main_ref[c * rows + m], main_ref[c * rows + rows - halo + m]
-                partner_out[c * halo + m] = jnp.where(even, foot, head)
                 other_out[c * halo + m] = jnp.where(even, head, foot)
+                if target_win == 1:
+                    partner_out[c * halo + m] = jnp.where(even, foot, head)
 
 
 def turn_kernel(z, count, lines_ref, out_ref):
@@ -344,7 +351,7 @@
     _, steps, stages, layers, rows, cols = thickness.shape
     z = Sizes(steps, layers, rows, cols)
     n_win, n_lat = lax.axis_size("win"), lax.axis_size("lat")
-    win = lax.axis_index("win")
+    even = lax.axis_index("lat") % 2 == 0
     flat = thickness.reshape(steps * stages * layers * rows, cols)
     cube = (layers, cols)
     count = obs_cells.shape[2]
@@ -385,7 +392,7 @@
 
     def window(target_win, fields, state, results):
         first, last = target_win == n_win - 1, target_win == 0
-        outs = [one, state_rows] if last else [one, state_rows, state_rows, halo_rows, halo_rows]
+        outs = [one, state_rows] if last else [one, state_rows, state_rows] + [halo_rows] * (2 if target_win == 1 else 1)
         operands = fields + tuple(tables) + state + results
         return call(
             functools.partial(window_kernel, z, n_lat * rows, first, last, target_win),
@@ -395,24 +402,28 @@
             cost=40_000_000,
         )(*operands)
 
-    above, below, bias, lam, main, partner, other = window(n_win - 1, (h,) + near, (), ())
+    above, below, bias, lam, main, *edges = window(n_win - 1, (h,) + near, (), ())
     fields = (h, above, below)
     for source_win in range(n_win - 1, 0, -1):
-        state = (
-            relay(main, source_win, source_win - 1),
-            relay(partner, source_win, source_win - 1, pairs),
-            relay(other, source_win, source_win - 1, rests),
-        )
+        arrived = relay(main, source_win, source_win - 1)
+        beside = relay(edges[0], source_win, source_win - 1, rests)
+        if len(edges) > 1:
+            partners = relay(edges[1], source_win, source_win - 1, pairs)
+        else:
+            lines = arrived.reshape((3, rows) + cube)
+            edge = jnp.where(even, lines[:, rows - z.halo :], lines[:, : z.halo]).reshape(halo_rows)
+            partners = relay(edge, source_win - 1, source_win - 1, pairs)
+        state = (arrived, partners, beside)
         if source_win > 1:
-            bias, lam, main, partner, other = window(source_win - 1, fields, state, (lam, bias))
+            bias, lam, main, *edges = window(source_win - 1, fields, state, (lam, bias))
     others = n_win - 1
-    total = bias
+    added = ()
     for shift in range(1, others):
         moves = [
             ((1 + w) * n_lat + i, (1 + (w + shift) % others) * n_lat + i) for w in range(others) for i in range(n_lat)
         ]
-        total = total + lax.ppermute(bias, ("win", "lat"), moves)
-    mine, lam = window(0, fields, state, (lam, total))
+        added += (lax.ppermute(bias, ("win", "lat"), moves),)
+    mine, lam = window(0, fields, state, (lam, bias) + added)
     swap = [(a * n_lat + i, (1 - a) * n_lat + i) for a in range(2) for i in range(n_lat)]
     result = mine + sum(relay(mine, 0, target_win) for target_win in range(n_win - 1, 1, -1))
     result = result + lax.ppermute(mine, ("win", "lat"), swap)

time: 74.3 us -> 73.5 us (0.989)
    ppermute x1, waiting for transfers between devices: 1.46 us -> 0.35 us  [per_device(): result = result + lax.ppermute(mine, ('win', 'lat'), swap)]
where the time goes in v4:
time: 73.5 us; the launch traced here: 73.1 us
  waiting for transfers between devices  43.2 us (59%)
  starting transfers between devices  18.4 us (25%)
  Pallas kernels  10.5 us (14%)
  between operations  0.94 us (1%)
    ppermute x11, waiting for transfers between devices, relay(): return lax.ppermute(value, ('win', 'lat'), moves)  40.4 us
    ppermute x11, starting transfers between devices, relay(): return lax.ppermute(value, ('win', 'lat'), moves)  10.5 us
    pallas_call x4, Pallas kernels, window(): call(functools.partial(window_kernel, z, n_lat * rows, first, last, targe...  6.78 us
    ppermute x1, starting transfers between devices, per_device(): lax.ppermute(to_other, 'lat', rests)  4.5 us
    ppermute x1, waiting for transfers between devices, per_device(): lax.ppermute(to_other, 'lat', rests)  2.49 us
    ppermute x1, starting transfers between devices, per_device(): result = result + lax.ppermute(mine, ('win', 'lat'), swap)  1.92 us
  transfers between devices with their start and end apart: 16, of which 6 were waited for; matrix products, arithmetic and copies ran while one was open for 0% of the time, Pallas kernels for 2%

profile of v4, /device:TPU:1, one launch (start us, length us, event | category | flops | bytes accessed | tf_op | source)
XLA Modules:
  0.0 73.1 jit_solution(13458893718561871628)
XLA Ops:
  0.6 1.4 %shard_map.77 = (f32[24,8,256]{2,1,0:T(8,128)S(1)}, f32[24,8,256]{2,1,0:T(8,128)S(1)}, f32[6,8,256]{2,1,0:T(8,128)S(1)}) custom-call(f32[768,256]{1,0:T(8,128)} %bitcast.9, s32[2,256]{1,0:T(2,128)} %bitcast.17, f32[2,256]{1,0:T(2,128)} %bitcast.18, s32[16,256]{1,0:T(8,128)} %mask_in.1), custom_call_target="tpu_custom_call" | custom-call | bytes 4194304 | tf_op jit(solution)/shard_map/pallas_call | solution.py:359
  2.2 4.5 %collective-permute-start.1 = (f32[24,8,256]{2,1,0:T(8,128)S(1)}, f32[24,8,256]{2,1,0:T(8,128)S(1)}, u32[]{:S(2)}, u32[]{:S(2)}) collective-permute-start(f32[24,8,256]{2,1,0:T(8,128)S(1)} %get-tuple-element.29), channel_id=1, source_target_pairs={{1,2},{2,1},{5,6},{6,5},{9,10},{10,9},{13,14},{14,13},{17,18},{18,... | collective-permute-start | bytes 589832 | tf_op jit(solution)/shard_map/ppermute | solution.py:373
  6.7 0.8 %shard_map.78 = (f32[102,8,256]{2,1,0:T(8,128)S(1)}, f32[48,8,256]{2,1,0:T(8,128)S(1)}, f32[48,8,256]{2,1,0:T(8,128)S(1)}, f32[72,128]{1,0:T(8,128)S(1)}) custom-call(f32[8,8]{1,0:T(8,128)S(1)} %copy-done.1, f32[8]{0:T(128)S(1)} %copy-done.2, f32[768,256]{1,0:T(8,128)S(1)} %bitcast.10, f32[6,8,256]{2,1,0:T(8,128)S(1)} %get-tuple-element.26.own_ref), custom_call_target="tpu_custom_call" | custom-call | bytes 4194304 | tf_op jit(solution)/shard_map/pallas_call | solution.py:374
  7.5 2.5 %collective-permute-done.1.refs_2_ = f32[24,8,256]{2,1,0:T(8,128)S(1)} collective-permute-done((f32[24,8,256]{2,1,0:T(8,128)S(1)}, f32[24,8,256]{2,1,0:T(8,128)S(1)}, u32[]{:S(2)}, u32[]{:S(2)}) %collective-permute-start.1) | collective-permute-done | bytes 196640 | tf_op jit(solution)/shard_map/ppermute | solution.py:373
  10.0 1.6 %shard_map.79 = (f32[24,8,256]{2,1,0:T(8,128)S(1)}, f32[24,8,256]{2,1,0:T(8,128)S(1)}, f32[16,8,256]{2,1,0:T(8,128)S(1)}, f32[48,8,256]{2,1,0:T(8,128)S(1)}, f32...) custom-call(f32[102,8,256]{2,1,0:T(8,128)S(1)} %get-tuple-element.27.refs_0_, ...), custom_call_target="tpu_custom_call" | custom-call | flops 40000000 | bytes 4194304 | tf_op jit(solution)/shard_map/pallas_call | solution.py:397
  11.6 0.7 collective-permute-start.2
  12.4 0.7 collective-permute-start.4
  13.1 0.7 collective-permute-start.3
  13.8 1.7 %shard_map.80 = (f32[16,8,256]{2,1,0:T(8,128)S(1)}, f32[48,8,256]{2,1,0:T(8,128)S(1)}, f32[48,8,256]{2,1,0:T(8,128)S(1)}, f32[18,8,256]{2,1,0:T(8,128)S(1)}) custom-call(f32[102,8,256]{2,1,0:T(8,128)S(1)} %get-tuple-element.27.refs_0_, f32[24,8,256]{2,1,0:T(8,128)S(1)} %get-tuple-element.33.refs_1_, f32[24,8,256]{2,1,0:T(8,128)S(1)} %get-tuple-element.34.refs_2_, ...), custom_call_target="tpu_custom_call" | custom-call | flops 40000000 | bytes 4194304 | tf_op jit(solution)/shard_map/pallas_call | solution.py:397
  15.5 0.7 collective-permute-start.5
  17.6 1.7 %shard_map.81 = (f32[16,8,256]{2,1,0:T(8,128)S(1)}, f32[48,8,256]{2,1,0:T(8,128)S(1)}, f32[48,8,256]{2,1,0:T(8,128)S(1)}, f32[18,8,256]{2,1,0:T(8,128)S(1)}, f32[18,8,256]{2,1,0:T(8,128)S(1)}) custom-call(f32[102,8,256]{2,1,0:T(8,128)S(1)} %get-tuple-element.27.refs_0_, f32[24,8,256]{2,1,0:T(8,128)S(1)} %get-tuple-element.33.refs_1_, ...), custom_call_target="tpu_custom_call" | custom-call | flops 40000000 | bytes 4194304 | tf_op jit(solution)/shard_map/pallas_call | solution.py:397
  19.4 1.3 %collective-permute-start.8 = (f32[48,8,256]{2,1,0:T(8,128)S(1)}, f32[48,8,256]{2,1,0:T(8,128)S(1)}, u32[]{:S(2)}, u32[]{:S(2)}) collective-permute-start(f32[48,8,256]{2,1,0:T(8,128)S(1)} %get-tuple-element.43), channel_id=1, source_target_pairs={{4,0},{5,1},{6,2},{7,3},{20,16},{21,17},{22,18},{23,19}} | collective-permute-start | bytes 1179656 | tf_op jit(solution)/shard_map/ppermute | solution.py:389
  20.7 1.3 %collective-permute-start.9 = (f32[18,8,256]{2,1,0:T(8,128)S(1)}, f32[18,8,256]{2,1,0:T(8,128)S(1)}, u32[]{:S(2)}, u32[]{:S(2)}) collective-permute-start(f32[18,8,256]{2,1,0:T(8,128)S(1)} %get-tuple-element.44), channel_id=1, source_target_pairs={{4,1},{5,0},{6,3},{7,2},{20,17},{21,16},{22,19},{23,18}} | collective-permute-start | bytes 442376 | tf_op jit(solution)/shard_map/ppermute | solution.py:389
  22.0 1.3 %collective-permute-start.10 = (f32[18,8,256]{2,1,0:T(8,128)S(1)}, f32[18,8,256]{2,1,0:T(8,128)S(1)}, u32[]{:S(2)}, u32[]{:S(2)}) collective-permute-start(f32[18,8,256]{2,1,0:T(8,128)S(1)} %get-tuple-element.45), channel_id=1, source_target_pairs={{5,2},{6,1},{21,18},{22,17}} | collective-permute-start | bytes 442376 | tf_op jit(solution)/shard_map/ppermute | solution.py:389
  24.6 34.5 %collective-permute-done.9.refs_7_ = f32[18,8,256]{2,1,0:T(8,128)S(1)} collective-permute-done((f32[18,8,256]{2,1,0:T(8,128)S(1)}, f32[18,8,256]{2,1,0:T(8,128)S(1)}, u32[]{:S(2)}, u32[]{:S(2)}) %collective-permute-start.9) | collective-permute-done | bytes 147488 | tf_op jit(solution)/shard_map/ppermute | solution.py:389
  59.1 2.4 %collective-permute-done.10.refs_8_ = f32[18,8,256]{2,1,0:T(8,128)S(1)} collective-permute-done((f32[18,8,256]{2,1,0:T(8,128)S(1)}, f32[18,8,256]{2,1,0:T(8,128)S(1)}, u32[]{:S(2)}, u32[]{:S(2)}) %collective-permute-start.10) | collective-permute-done | bytes 147488 | tf_op jit(solution)/shard_map/ppermute | solution.py:389
  61.5 1.7 %shard_map.82 = (f32[16,8,256]{2,1,0:T(8,128)S(1)}, f32[48,8,256]{2,1,0:T(8,128)S(1)}) custom-call(f32[102,8,256]{2,1,0:T(8,128)S(1)} %get-tuple-element.27.refs_0_, f32[24,8,256]{2,1,0:T(8,128)S(1)} %get-tuple-element.33.refs_1_, f32[24,8,256]{2,1,0:T(8,128)S(1)} %get-tuple-element.34.refs_2_, f32[48,8,256]{2,1,0:T(8,128)S(1)} %get-tuple-element.30.refs_3_, ...), custom_call_target="tpu_custom_call" | custom-call | flops 40000000 | bytes 4194304 | tf_op jit(solution)/shard_map/pallas_call | solution.py:397
  63.2 1.9 %collective-permute-start.15 = (f32[16,8,256]{2,1,0:T(8,128)S(1)}, f32[16,8,256]{2,1,0:T(8,128)S(1)}, u32[]{:S(2)}, u32[]{:S(2)}) collective-permute-start(f32[16,8,256]{2,1,0:T(8,128)S(1)} %get-tuple-element.49), channel_id=1, source_target_pairs={{0,4},{1,5},{2,6},{3,7},{4,0},{5,1},{6,2},{7,3},{16,20},{17,21},{1... | collective-permute-start | bytes 393224 | tf_op jit(solution)/shard_map/ppermute | solution.py:429
  65.2 1.3 %collective-permute-start.14 = (f32[16,8,256]{2,1,0:T(8,128)S(1)}, f32[16,8,256]{2,1,0:T(8,128)S(1)}, u32[]{:S(2)}, u32[]{:S(2)}) collective-permute-start(f32[16,8,256]{2,1,0:T(8,128)S(1)} %get-tuple-element.49), channel_id=1, source_target_pairs={{0,8},{1,9},{2,10},{3,11},{16,24},{17,25},{18,26},{19,27}} | collective-permute-start | bytes 393224 | tf_op jit(solution)/shard_map/ppermute | solution.py:389
  66.5 1.3 %collective-permute-start.13 = (f32[16,8,256]{2,1,0:T(8,128)S(1)}, f32[16,8,256]{2,1,0:T(8,128)S(1)}, u32[]{:S(2)}, u32[]{:S(2)}) collective-permute-start(f32[16,8,256]{2,1,0:T(8,128)S(1)} %get-tuple-element.49), channel_id=1, source_target_pairs={{0,12},{1,13},{2,14},{3,15},{16,28},{17,29},{18,30},{19,31}} | collective-permute-start | bytes 393224 | tf_op jit(solution)/shard_map/ppermute | solution.py:389
  67.8 0.8 %shard_map.83 = f32[384,256]{1,0:T(8,128)} custom-call(f32[48,8,256]{2,1,0:T(8,128)S(1)} %get-tuple-element.48.lines_ref), custom_call_target="tpu_custom_call" | custom-call | bytes 4194304 | tf_op jit(solution)/shard_map/pallas_call | solution.py:430
  69.0 2.0 %collective-permute-done.14 = f32[16,8,256]{2,1,0:T(8,128)S(1)} collective-permute-done((f32[16,8,256]{2,1,0:T(8,128)S(1)}, f32[16,8,256]{2,1,0:T(8,128)S(1)}, u32[]{:S(2)}, u32[]{:S(2)}) %collective-permute-start.14) | collective-permute-done | bytes 131104 | tf_op jit(solution)/shard_map/ppermute | solution.py:389
  71.0 1.4 %collective-permute-done.13 = f32[16,8,256]{2,1,0:T(8,128)S(1)} collective-permute-done((f32[16,8,256]{2,1,0:T(8,128)S(1)}, f32[16,8,256]{2,1,0:T(8,128)S(1)}, u32[]{:S(2)}, u32[]{:S(2)}) %collective-permute-start.13) | collective-permute-done | bytes 131104 | tf_op jit(solution)/shard_map/ppermute | solution.py:389
  72.4 0.7 shard_map.84
  (25 shorter events, 3.3 us)
Async XLA Ops:
  0.6 6.1 %copy-start = (f32[1,2,3,8,16,256]{5,4,3,2,1,0:T(8,128)S(1)}, f32[1,2,3,8,16,256]{5,4,3,2,1,0:T(8,128)}, u32[]{:S(2)}) copy-start(f32[1,2,3,8,16,256]{5,4,3,2,1,0:T(8,128)} %param.6) | copy-start | bytes 2359300
  2.0 4.7 %copy-start.1 = (f32[8,8]{1,0:T(8,128)S(1)}, f32[8,8]{1,0:T(8,128)}, u32[]{:S(2)}) copy-start(f32[8,8]{1,0:T(8,128)} %coupling_ref.1) | copy-start | bytes 772
  2.1 5.5 %collective-permute-start = (f32[24,8,256]{2,1,0:T(8,128)S(1)}, f32[24,8,256]{2,1,0:T(8,128)S(1)}, u32[]{:S(2)}, u32[]{:S(2)}) collective-permute-start(f32[24,8,256]{2,1,0:T(8,128)S(1)} %get-tuple-element.28), channel_id=1, source_target_pairs={{0,1},{1,0},{2,3},{3,2},{4,5},{5,4},{6,7},{7,6},{8,9},{9,8},{10,11... | collective-permute-start | bytes 589832 | tf_op jit(solution)/shard_map/ppermute | solution.py:373
  2.2 4.5 %copy-start.2 = (f32[8]{0:T(128)S(1)}, f32[8]{0:T(128)}, u32[]{:S(2)}) copy-start(f32[8]{0:T(128)} %damping_ref.1) | copy-start | bytes 100
  2.2 7.9 %collective-permute-start.1 = (f32[24,8,256]{2,1,0:T(8,128)S(1)}, f32[24,8,256]{2,1,0:T(8,128)S(1)}, u32[]{:S(2)}, u32[]{:S(2)}) collective-permute-start(f32[24,8,256]{2,1,0:T(8,128)S(1)} %get-tuple-element.29), channel_id=1, source_target_pairs={{1,2},{2,1},{5,6},{6,5},{9,10},{10,9},{13,14},{14,13},{17,18},{18,... | collective-permute-start | bytes 589832 | tf_op jit(solution)/shard_map/ppermute | solution.py:373
  11.6 1.4 %collective-permute-start.2 = (f32[48,8,256]{2,1,0:T(8,128)S(1)}, f32[48,8,256]{2,1,0:T(8,128)S(1)}, u32[]{:S(2)}, u32[]{:S(2)}) collective-permute-start(f32[48,8,256]{2,1,0:T(8,128)S(1)} %get-tuple-element.35), channel_id=1, source_target_pairs={{12,8},{13,9},{14,10},{15,11},{28,24},{29,25},{30,26},{31,27}} | collective-permute-start | bytes 1179656 | tf_op jit(solution)/shard_map/ppermute | solution.py:389
  12.4 1.4 %collective-permute-start.4 = (f32[18,8,256]{2,1,0:T(8,128)S(1)}, f32[18,8,256]{2,1,0:T(8,128)S(1)}, u32[]{:S(2)}, u32[]{:S(2)}) collective-permute-start(f32[18,8,256]{2,1,0:T(8,128)S(1)} %get-tuple-element.36), channel_id=1, source_target_pairs={{13,10},{14,9},{29,26},{30,25}} | collective-permute-start | bytes 442376 | tf_op jit(solution)/shard_map/ppermute | solution.py:389
  13.1 0.7 collective-permute-start.3
  15.5 1.4 %collective-permute-start.5 = (f32[48,8,256]{2,1,0:T(8,128)S(1)}, f32[48,8,256]{2,1,0:T(8,128)S(1)}, u32[]{:S(2)}, u32[]{:S(2)}) collective-permute-start(f32[48,8,256]{2,1,0:T(8,128)S(1)} %get-tuple-element.39), channel_id=1, source_target_pairs={{8,4},{9,5},{10,6},{11,7},{24,20},{25,21},{26,22},{27,23}} | collective-permute-start | bytes 1179656 | tf_op jit(solution)/shard_map/ppermute | solution.py:389
  16.2 1.4 %collective-permute-start.7 = (f32[18,8,256]{2,1,0:T(8,128)S(1)}, f32[18,8,256]{2,1,0:T(8,128)S(1)}, u32[]{:S(2)}, u32[]{:S(2)}) collective-permute-start(f32[18,8,256]{2,1,0:T(8,128)S(1)} %get-tuple-element.40), channel_id=1, source_target_pairs={{9,6},{10,5},{25,22},{26,21}} | collective-permute-start | bytes 442376 | tf_op jit(solution)/shard_map/ppermute | solution.py:389
  16.9 0.7 collective-permute-start.6
  19.4 42.2 %collective-permute-start.8 = (f32[48,8,256]{2,1,0:T(8,128)S(1)}, f32[48,8,256]{2,1,0:T(8,128)S(1)}, u32[]{:S(2)}, u32[]{:S(2)}) collective-permute-start(f32[48,8,256]{2,1,0:T(8,128)S(1)} %get-tuple-element.43), channel_id=1, source_target_pairs={{4,0},{5,1},{6,2},{7,3},{20,16},{21,17},{22,18},{23,19}} | collective-permute-start | bytes 1179656 | tf_op jit(solution)/shard_map/ppermute | solution.py:389
  20.7 38.4 %collective-permute-start.9 = (f32[18,8,256]{2,1,0:T(8,128)S(1)}, f32[18,8,256]{2,1,0:T(8,128)S(1)}, u32[]{:S(2)}, u32[]{:S(2)}) collective-permute-start(f32[18,8,256]{2,1,0:T(8,128)S(1)} %get-tuple-element.44), channel_id=1, source_target_pairs={{4,1},{5,0},{6,3},{7,2},{20,17},{21,16},{22,19},{23,18}} | collective-permute-start | bytes 442376 | tf_op jit(solution)/shard_map/ppermute | solution.py:389
  22.0 39.6 %collective-permute-start.10 = (f32[18,8,256]{2,1,0:T(8,128)S(1)}, f32[18,8,256]{2,1,0:T(8,128)S(1)}, u32[]{:S(2)}, u32[]{:S(2)}) collective-permute-start(f32[18,8,256]{2,1,0:T(8,128)S(1)} %get-tuple-element.45), channel_id=1, source_target_pairs={{5,2},{6,1},{21,18},{22,17}} | collective-permute-start | bytes 442376 | tf_op jit(solution)/shard_map/ppermute | solution.py:389
  23.3 1.4 %collective-permute-start.12 = (f32[16,8,256]{2,1,0:T(8,128)S(1)}, f32[16,8,256]{2,1,0:T(8,128)S(1)}, u32[]{:S(2)}, u32[]{:S(2)}) collective-permute-start(f32[16,8,256]{2,1,0:T(8,128)S(1)} %get-tuple-element.47.refs_10_), channel_id=1, source_target_pairs={{4,12},{5,13},{6,14},{7,15},{8,4},{9,5},{10,6},{11,7},{12,8},{13,9... | collective-permute-start | bytes 393224 | tf_op jit(solution)/shard_map/ppermute | solution.py:425
  23.9 0.7 collective-permute-start.11
  63.2 5.7 %collective-permute-start.15 = (f32[16,8,256]{2,1,0:T(8,128)S(1)}, f32[16,8,256]{2,1,0:T(8,128)S(1)}, u32[]{:S(2)}, u32[]{:S(2)}) collective-permute-start(f32[16,8,256]{2,1,0:T(8,128)S(1)} %get-tuple-element.49), channel_id=1, source_target_pairs={{0,4},{1,5},{2,6},{3,7},{4,0},{5,1},{6,2},{7,3},{16,20},{17,21},{1... | collective-permute-start | bytes 393224 | tf_op jit(solution)/shard_map/ppermute | solution.py:429
  65.2 5.8 %collective-permute-start.14 = (f32[16,8,256]{2,1,0:T(8,128)S(1)}, f32[16,8,256]{2,1,0:T(8,128)S(1)}, u32[]{:S(2)}, u32[]{:S(2)}) collective-permute-start(f32[16,8,256]{2,1,0:T(8,128)S(1)} %get-tuple-element.49), channel_id=1, source_target_pairs={{0,8},{1,9},{2,10},{3,11},{16,24},{17,25},{18,26},{19,27}} | collective-permute-start | bytes 393224 | tf_op jit(solution)/shard_map/ppermute | solution.py:389
  66.5 5.9 %collective-permute-start.13 = (f32[16,8,256]{2,1,0:T(8,128)S(1)}, f32[16,8,256]{2,1,0:T(8,128)S(1)}, u32[]{:S(2)}, u32[]{:S(2)}) collective-permute-start(f32[16,8,256]{2,1,0:T(8,128)S(1)} %get-tuple-element.49), channel_id=1, source_target_pairs={{0,12},{1,13},{2,14},{3,15},{16,28},{17,29},{18,30},{19,31}} | collective-permute-start | bytes 393224 | tf_op jit(solution)/shard_map/ppermute | solution.py:389

commit v5 on v4

--- a/solution.py
+++ b/solution.py
@@ -156,7 +156,7 @@
         (bias_ref, lam_ref), refs = refs[:2], refs[2:]
     else:
         (bias_ref, lam_ref, main_ref, other_out), refs = refs[:4], refs[4:]
-        if target_win == 1:
+        if not first:
             partner_out, refs = refs[0], refs[1:]
     x_ref, y_ref, w_ref, sum_ref, oc_out, keep_out = refs
     halo, ext, rows, layers = z.halo, z.ext, z.rows, z.layers
@@ -321,7 +321,7 @@
             for m in range(halo):
                 head, foot = main_ref[c * rows + m], main_ref[c * rows + rows - halo + m]
                 other_out[c * halo + m] = jnp.where(even, head, foot)
-                if target_win == 1:
+                if not first:
                     partner_out[c * halo + m] = jnp.where(even, foot, head)
 
 
@@ -392,7 +392,7 @@
 
     def window(target_win, fields, state, results):
         first, last = target_win == n_win - 1, target_win == 0
-        outs = [one, state_rows] if last else [one, state_rows, state_rows] + [halo_rows] * (2 if target_win == 1 else 1)
+        outs = [one, state_rows] if last else [one, state_rows, state_rows] + [halo_rows] * (1 if first else 2)
         operands = fields + tuple(tables) + state + results
         return call(
             functools.partial(window_kernel, z, n_lat * rows, first, last, target_win),

time: 73.5 us -> 72.9 us (level)
  no operation moved by 1% of the time
where the time goes in v5:
time: 72.9 us; the launch traced here: 72.5 us
  waiting for transfers between devices  42.7 us (59%)
  starting transfers between devices  18.4 us (25%)
  Pallas kernels  10.4 us (14%)
  between operations  0.93 us (1%)
    ppermute x11, waiting for transfers between devices, relay(): return lax.ppermute(value, ('win', 'lat'), moves)  39.8 us
    ppermute x11, starting transfers between devices, relay(): return lax.ppermute(value, ('win', 'lat'), moves)  10.5 us
    pallas_call x4, Pallas kernels, window(): call(functools.partial(window_kernel, z, n_lat * rows, first, last, targe...  6.75 us
    ppermute x1, starting transfers between devices, per_device(): lax.ppermute(to_other, 'lat', rests)  4.5 us
    ppermute x1, waiting for transfers between devices, per_device(): lax.ppermute(to_other, 'lat', rests)  2.49 us
    ppermute x1, starting transfers between devices, per_device(): result = result + lax.ppermute(mine, ('win', 'lat'), swap)  1.92 us
  transfers between devices with their start and end apart: 16, of which 6 were waited for; matrix products, arithmetic and copies ran while one was open for 0% of the time, Pallas kernels for 2%

profile of v5, /device:TPU:1, one launch (start us, length us, event | category | flops | bytes accessed | tf_op | source)
XLA Modules:
  0.0 72.5 jit_solution(8906049799181563339)
XLA Ops:
  0.6 1.4 %shard_map.77 = (f32[24,8,256]{2,1,0:T(8,128)S(1)}, f32[24,8,256]{2,1,0:T(8,128)S(1)}, f32[6,8,256]{2,1,0:T(8,128)S(1)}) custom-call(f32[768,256]{1,0:T(8,128)} %bitcast.7, s32[2,256]{1,0:T(2,128)} %bitcast.13, f32[2,256]{1,0:T(2,128)} %bitcast.14, s32[16,256]{1,0:T(8,128)} %mask_in.1), custom_call_target="tpu_custom_call" | custom-call | bytes 4194304 | tf_op jit(solution)/shard_map/pallas_call | solution.py:359
  2.2 4.5 %collective-permute-start.1 = (f32[24,8,256]{2,1,0:T(8,128)S(1)}, f32[24,8,256]{2,1,0:T(8,128)S(1)}, u32[]{:S(2)}, u32[]{:S(2)}) collective-permute-start(f32[24,8,256]{2,1,0:T(8,128)S(1)} %get-tuple-element.30), channel_id=1, source_target_pairs={{1,2},{2,1},{5,6},{6,5},{9,10},{10,9},{13,14},{14,13},{17,18},{18,... | collective-permute-start | bytes 589832 | tf_op jit(solution)/shard_map/ppermute | solution.py:373
  6.7 0.8 %shard_map.78 = (f32[102,8,256]{2,1,0:T(8,128)S(1)}, f32[48,8,256]{2,1,0:T(8,128)S(1)}, f32[48,8,256]{2,1,0:T(8,128)S(1)}, f32[72,128]{1,0:T(8,128)S(1)}) custom-call(f32[8,8]{1,0:T(8,128)S(1)} %copy-done.1, f32[8]{0:T(128)S(1)} %copy-done.2, f32[768,256]{1,0:T(8,128)S(1)} %bitcast.8, f32[6,8,256]{2,1,0:T(8,128)S(1)} %get-tuple-element.27.own_ref), custom_call_target="tpu_custom_call" | custom-call | bytes 4194304 | tf_op jit(solution)/shard_map/pallas_call | solution.py:374
  7.5 2.5 %collective-permute-done.1.refs_2_ = f32[24,8,256]{2,1,0:T(8,128)S(1)} collective-permute-done((f32[24,8,256]{2,1,0:T(8,128)S(1)}, f32[24,8,256]{2,1,0:T(8,128)S(1)}, u32[]{:S(2)}, u32[]{:S(2)}) %collective-permute-start.1) | collective-permute-done | bytes 196640 | tf_op jit(solution)/shard_map/ppermute | solution.py:373
  10.0 1.6 %shard_map.79 = (f32[24,8,256]{2,1,0:T(8,128)S(1)}, f32[24,8,256]{2,1,0:T(8,128)S(1)}, f32[16,8,256]{2,1,0:T(8,128)S(1)}, f32[48,8,256]{2,1,0:T(8,128)S(1)}, f32...) custom-call(f32[102,8,256]{2,1,0:T(8,128)S(1)} %get-tuple-element.28.refs_0_, ...), custom_call_target="tpu_custom_call" | custom-call | flops 40000000 | bytes 4194304 | tf_op jit(solution)/shard_map/pallas_call | solution.py:397
  11.6 0.7 collective-permute-start.2
  12.4 0.7 collective-permute-start.4
  13.1 0.7 collective-permute-start.3
  13.8 1.7 %shard_map.80 = (f32[16,8,256]{2,1,0:T(8,128)S(1)}, f32[48,8,256]{2,1,0:T(8,128)S(1)}, f32[48,8,256]{2,1,0:T(8,128)S(1)}, f32[18,8,256]{2,1,0:T(8,128)S(1)}, f32[18,8,256]{2,1,0:T(8,128)S(1)}) custom-call(f32[102,8,256]{2,1,0:T(8,128)S(1)} %get-tuple-element.28.refs_0_, f32[24,8,256]{2,1,0:T(8,128)S(1)} %get-tuple-element.34.refs_1_, ...), custom_call_target="tpu_custom_call" | custom-call | flops 40000000 | bytes 4194304 | tf_op jit(solution)/shard_map/pallas_call | solution.py:397
  15.5 0.7 collective-permute-start.5
  17.6 1.7 %shard_map.81 = (f32[16,8,256]{2,1,0:T(8,128)S(1)}, f32[48,8,256]{2,1,0:T(8,128)S(1)}, f32[48,8,256]{2,1,0:T(8,128)S(1)}, f32[18,8,256]{2,1,0:T(8,128)S(1)}, f32[18,8,256]{2,1,0:T(8,128)S(1)}) custom-call(f32[102,8,256]{2,1,0:T(8,128)S(1)} %get-tuple-element.28.refs_0_, f32[24,8,256]{2,1,0:T(8,128)S(1)} %get-tuple-element.34.refs_1_, ...), custom_call_target="tpu_custom_call" | custom-call | flops 40000000 | bytes 4194304 | tf_op jit(solution)/shard_map/pallas_call | solution.py:397
  19.3 1.3 %collective-permute-start.8 = (f32[48,8,256]{2,1,0:T(8,128)S(1)}, f32[48,8,256]{2,1,0:T(8,128)S(1)}, u32[]{:S(2)}, u32[]{:S(2)}) collective-permute-start(f32[48,8,256]{2,1,0:T(8,128)S(1)} %get-tuple-element.45), channel_id=1, source_target_pairs={{4,0},{5,1},{6,2},{7,3},{20,16},{21,17},{22,18},{23,19}} | collective-permute-start | bytes 1179656 | tf_op jit(solution)/shard_map/ppermute | solution.py:389
  20.6 1.3 %collective-permute-start.9 = (f32[18,8,256]{2,1,0:T(8,128)S(1)}, f32[18,8,256]{2,1,0:T(8,128)S(1)}, u32[]{:S(2)}, u32[]{:S(2)}) collective-permute-start(f32[18,8,256]{2,1,0:T(8,128)S(1)} %get-tuple-element.46), channel_id=1, source_target_pairs={{4,1},{5,0},{6,3},{7,2},{20,17},{21,16},{22,19},{23,18}} | collective-permute-start | bytes 442376 | tf_op jit(solution)/shard_map/ppermute | solution.py:389
  21.9 1.3 %collective-permute-start.10 = (f32[18,8,256]{2,1,0:T(8,128)S(1)}, f32[18,8,256]{2,1,0:T(8,128)S(1)}, u32[]{:S(2)}, u32[]{:S(2)}) collective-permute-start(f32[18,8,256]{2,1,0:T(8,128)S(1)} %get-tuple-element.47), channel_id=1, source_target_pairs={{5,2},{6,1},{21,18},{22,17}} | collective-permute-start | bytes 442376 | tf_op jit(solution)/shard_map/ppermute | solution.py:389
  24.6 31.0 %collective-permute-done.9.refs_7_ = f32[18,8,256]{2,1,0:T(8,128)S(1)} collective-permute-done((f32[18,8,256]{2,1,0:T(8,128)S(1)}, f32[18,8,256]{2,1,0:T(8,128)S(1)}, u32[]{:S(2)}, u32[]{:S(2)}) %collective-permute-start.9) | collective-permute-done | bytes 147488 | tf_op jit(solution)/shard_map/ppermute | solution.py:389
  55.6 5.7 %collective-permute-done.10.refs_8_ = f32[18,8,256]{2,1,0:T(8,128)S(1)} collective-permute-done((f32[18,8,256]{2,1,0:T(8,128)S(1)}, f32[18,8,256]{2,1,0:T(8,128)S(1)}, u32[]{:S(2)}, u32[]{:S(2)}) %collective-permute-start.10) | collective-permute-done | bytes 147488 | tf_op jit(solution)/shard_map/ppermute | solution.py:389
  61.3 1.7 %shard_map.82 = (f32[16,8,256]{2,1,0:T(8,128)S(1)}, f32[48,8,256]{2,1,0:T(8,128)S(1)}) custom-call(f32[102,8,256]{2,1,0:T(8,128)S(1)} %get-tuple-element.28.refs_0_, f32[24,8,256]{2,1,0:T(8,128)S(1)} %get-tuple-element.34.refs_1_, f32[24,8,256]{2,1,0:T(8,128)S(1)} %get-tuple-element.35.refs_2_, f32[48,8,256]{2,1,0:T(8,128)S(1)} %get-tuple-element.31.refs_3_, ...), custom_call_target="tpu_custom_call" | custom-call | flops 40000000 | bytes 4194304 | tf_op jit(solution)/shard_map/pallas_call | solution.py:397
  63.1 1.9 %collective-permute-start.15 = (f32[16,8,256]{2,1,0:T(8,128)S(1)}, f32[16,8,256]{2,1,0:T(8,128)S(1)}, u32[]{:S(2)}, u32[]{:S(2)}) collective-permute-start(f32[16,8,256]{2,1,0:T(8,128)S(1)} %get-tuple-element.51), channel_id=1, source_target_pairs={{0,4},{1,5},{2,6},{3,7},{4,0},{5,1},{6,2},{7,3},{16,20},{17,21},{1... | collective-permute-start | bytes 393224 | tf_op jit(solution)/shard_map/ppermute | solution.py:429
  65.0 1.3 %collective-permute-start.14 = (f32[16,8,256]{2,1,0:T(8,128)S(1)}, f32[16,8,256]{2,1,0:T(8,128)S(1)}, u32[]{:S(2)}, u32[]{:S(2)}) collective-permute-start(f32[16,8,256]{2,1,0:T(8,128)S(1)} %get-tuple-element.51), channel_id=1, source_target_pairs={{0,8},{1,9},{2,10},{3,11},{16,24},{17,25},{18,26},{19,27}} | collective-permute-start | bytes 393224 | tf_op jit(solution)/shard_map/ppermute | solution.py:389
  66.3 1.3 %collective-permute-start.13 = (f32[16,8,256]{2,1,0:T(8,128)S(1)}, f32[16,8,256]{2,1,0:T(8,128)S(1)}, u32[]{:S(2)}, u32[]{:S(2)}) collective-permute-start(f32[16,8,256]{2,1,0:T(8,128)S(1)} %get-tuple-element.51), channel_id=1, source_target_pairs={{0,12},{1,13},{2,14},{3,15},{16,28},{17,29},{18,30},{19,31}} | collective-permute-start | bytes 393224 | tf_op jit(solution)/shard_map/ppermute | solution.py:389
  67.6 0.8 %shard_map.83 = f32[384,256]{1,0:T(8,128)} custom-call(f32[48,8,256]{2,1,0:T(8,128)S(1)} %get-tuple-element.50.lines_ref), custom_call_target="tpu_custom_call" | custom-call | bytes 4194304 | tf_op jit(solution)/shard_map/pallas_call | solution.py:430
  68.8 1.6 %collective-permute-done.14 = f32[16,8,256]{2,1,0:T(8,128)S(1)} collective-permute-done((f32[16,8,256]{2,1,0:T(8,128)S(1)}, f32[16,8,256]{2,1,0:T(8,128)S(1)}, u32[]{:S(2)}, u32[]{:S(2)}) %collective-permute-start.14) | collective-permute-done | bytes 131104 | tf_op jit(solution)/shard_map/ppermute | solution.py:389
  70.4 1.4 %collective-permute-done.13 = f32[16,8,256]{2,1,0:T(8,128)S(1)} collective-permute-done((f32[16,8,256]{2,1,0:T(8,128)S(1)}, f32[16,8,256]{2,1,0:T(8,128)S(1)}, u32[]{:S(2)}, u32[]{:S(2)}) %collective-permute-start.13) | collective-permute-done | bytes 131104 | tf_op jit(solution)/shard_map/ppermute | solution.py:389
  71.8 0.7 shard_map.84
  (24 shorter events, 3.2 us)
Async XLA Ops:
  0.6 6.1 %copy-start = (f32[1,2,3,8,16,256]{5,4,3,2,1,0:T(8,128)S(1)}, f32[1,2,3,8,16,256]{5,4,3,2,1,0:T(8,128)}, u32[]{:S(2)}) copy-start(f32[1,2,3,8,16,256]{5,4,3,2,1,0:T(8,128)} %param.6) | copy-start | bytes 2359300
  2.0 4.7 %copy-start.1 = (f32[8,8]{1,0:T(8,128)S(1)}, f32[8,8]{1,0:T(8,128)}, u32[]{:S(2)}) copy-start(f32[8,8]{1,0:T(8,128)} %coupling_ref.1) | copy-start | bytes 772
  2.1 5.5 %collective-permute-start = (f32[24,8,256]{2,1,0:T(8,128)S(1)}, f32[24,8,256]{2,1,0:T(8,128)S(1)}, u32[]{:S(2)}, u32[]{:S(2)}) collective-permute-start(f32[24,8,256]{2,1,0:T(8,128)S(1)} %get-tuple-element.29), channel_id=1, source_target_pairs={{0,1},{1,0},{2,3},{3,2},{4,5},{5,4},{6,7},{7,6},{8,9},{9,8},{10,11... | collective-permute-start | bytes 589832 | tf_op jit(solution)/shard_map/ppermute | solution.py:373
  2.2 4.5 %copy-start.2 = (f32[8]{0:T(128)S(1)}, f32[8]{0:T(128)}, u32[]{:S(2)}) copy-start(f32[8]{0:T(128)} %damping_ref.1) | copy-start | bytes 100
  2.2 7.9 %collective-permute-start.1 = (f32[24,8,256]{2,1,0:T(8,128)S(1)}, f32[24,8,256]{2,1,0:T(8,128)S(1)}, u32[]{:S(2)}, u32[]{:S(2)}) collective-permute-start(f32[24,8,256]{2,1,0:T(8,128)S(1)} %get-tuple-element.30), channel_id=1, source_target_pairs={{1,2},{2,1},{5,6},{6,5},{9,10},{10,9},{13,14},{14,13},{17,18},{18,... | collective-permute-start | bytes 589832 | tf_op jit(solution)/shard_map/ppermute | solution.py:373
  11.6 1.4 %collective-permute-start.2 = (f32[48,8,256]{2,1,0:T(8,128)S(1)}, f32[48,8,256]{2,1,0:T(8,128)S(1)}, u32[]{:S(2)}, u32[]{:S(2)}) collective-permute-start(f32[48,8,256]{2,1,0:T(8,128)S(1)} %get-tuple-element.36), channel_id=1, source_target_pairs={{12,8},{13,9},{14,10},{15,11},{28,24},{29,25},{30,26},{31,27}} | collective-permute-start | bytes 1179656 | tf_op jit(solution)/shard_map/ppermute | solution.py:389
  12.4 1.4 %collective-permute-start.4 = (f32[18,8,256]{2,1,0:T(8,128)S(1)}, f32[18,8,256]{2,1,0:T(8,128)S(1)}, u32[]{:S(2)}, u32[]{:S(2)}) collective-permute-start(f32[18,8,256]{2,1,0:T(8,128)S(1)} %get-tuple-element.37), channel_id=1, source_target_pairs={{13,10},{14,9},{29,26},{30,25}} | collective-permute-start | bytes 442376 | tf_op jit(solution)/shard_map/ppermute | solution.py:389
  13.1 0.7 collective-permute-start.3
  15.5 2.1 %collective-permute-start.5 = (f32[48,8,256]{2,1,0:T(8,128)S(1)}, f32[48,8,256]{2,1,0:T(8,128)S(1)}, u32[]{:S(2)}, u32[]{:S(2)}) collective-permute-start(f32[48,8,256]{2,1,0:T(8,128)S(1)} %get-tuple-element.40), channel_id=1, source_target_pairs={{8,4},{9,5},{10,6},{11,7},{24,20},{25,21},{26,22},{27,23}} | collective-permute-start | bytes 1179656 | tf_op jit(solution)/shard_map/ppermute | solution.py:389
  16.2 1.4 %collective-permute-start.6 = (f32[18,8,256]{2,1,0:T(8,128)S(1)}, f32[18,8,256]{2,1,0:T(8,128)S(1)}, u32[]{:S(2)}, u32[]{:S(2)}) collective-permute-start(f32[18,8,256]{2,1,0:T(8,128)S(1)} %get-tuple-element.41), channel_id=1, source_target_pairs={{8,5},{9,4},{10,7},{11,6},{24,21},{25,20},{26,23},{27,22}} | collective-permute-start | bytes 442376 | tf_op jit(solution)/shard_map/ppermute | solution.py:389
  16.9 0.7 collective-permute-start.7
  19.3 42.0 %collective-permute-start.8 = (f32[48,8,256]{2,1,0:T(8,128)S(1)}, f32[48,8,256]{2,1,0:T(8,128)S(1)}, u32[]{:S(2)}, u32[]{:S(2)}) collective-permute-start(f32[48,8,256]{2,1,0:T(8,128)S(1)} %get-tuple-element.45), channel_id=1, source_target_pairs={{4,0},{5,1},{6,2},{7,3},{20,16},{21,17},{22,18},{23,19}} | collective-permute-start | bytes 1179656 | tf_op jit(solution)/shard_map/ppermute | solution.py:389
  20.6 35.0 %collective-permute-start.9 = (f32[18,8,256]{2,1,0:T(8,128)S(1)}, f32[18,8,256]{2,1,0:T(8,128)S(1)}, u32[]{:S(2)}, u32[]{:S(2)}) collective-permute-start(f32[18,8,256]{2,1,0:T(8,128)S(1)} %get-tuple-element.46), channel_id=1, source_target_pairs={{4,1},{5,0},{6,3},{7,2},{20,17},{21,16},{22,19},{23,18}} | collective-permute-start | bytes 442376 | tf_op jit(solution)/shard_map/ppermute | solution.py:389
  21.9 39.4 %collective-permute-start.10 = (f32[18,8,256]{2,1,0:T(8,128)S(1)}, f32[18,8,256]{2,1,0:T(8,128)S(1)}, u32[]{:S(2)}, u32[]{:S(2)}) collective-permute-start(f32[18,8,256]{2,1,0:T(8,128)S(1)} %get-tuple-element.47), channel_id=1, source_target_pairs={{5,2},{6,1},{21,18},{22,17}} | collective-permute-start | bytes 442376 | tf_op jit(solution)/shard_map/ppermute | solution.py:389
  23.2 1.4 %collective-permute-start.12 = (f32[16,8,256]{2,1,0:T(8,128)S(1)}, f32[16,8,256]{2,1,0:T(8,128)S(1)}, u32[]{:S(2)}, u32[]{:S(2)}) collective-permute-start(f32[16,8,256]{2,1,0:T(8,128)S(1)} %get-tuple-element.49.refs_10_), channel_id=1, source_target_pairs={{4,12},{5,13},{6,14},{7,15},{8,4},{9,5},{10,6},{11,7},{12,8},{13,9... | collective-permute-start | bytes 393224 | tf_op jit(solution)/shard_map/ppermute | solution.py:425
  23.9 0.7 collective-permute-start.11
  63.1 5.7 %collective-permute-start.15 = (f32[16,8,256]{2,1,0:T(8,128)S(1)}, f32[16,8,256]{2,1,0:T(8,128)S(1)}, u32[]{:S(2)}, u32[]{:S(2)}) collective-permute-start(f32[16,8,256]{2,1,0:T(8,128)S(1)} %get-tuple-element.51), channel_id=1, source_target_pairs={{0,4},{1,5},{2,6},{3,7},{4,0},{5,1},{6,2},{7,3},{16,20},{17,21},{1... | collective-permute-start | bytes 393224 | tf_op jit(solution)/shard_map/ppermute | solution.py:429
  65.0 5.4 %collective-permute-start.14 = (f32[16,8,256]{2,1,0:T(8,128)S(1)}, f32[16,8,256]{2,1,0:T(8,128)S(1)}, u32[]{:S(2)}, u32[]{:S(2)}) collective-permute-start(f32[16,8,256]{2,1,0:T(8,128)S(1)} %get-tuple-element.51), channel_id=1, source_target_pairs={{0,8},{1,9},{2,10},{3,11},{16,24},{17,25},{18,26},{19,27}} | collective-permute-start | bytes 393224 | tf_op jit(solution)/shard_map/ppermute | solution.py:389
  66.3 5.5 %collective-permute-start.13 = (f32[16,8,256]{2,1,0:T(8,128)S(1)}, f32[16,8,256]{2,1,0:T(8,128)S(1)}, u32[]{:S(2)}, u32[]{:S(2)}) collective-permute-start(f32[16,8,256]{2,1,0:T(8,128)S(1)} %get-tuple-element.51), channel_id=1, source_target_pairs={{0,12},{1,13},{2,14},{3,15},{16,28},{17,29},{18,30},{19,31}} | collective-permute-start | bytes 393224 | tf_op jit(solution)/shard_map/ppermute | solution.py:389
